TPU v7x, 32 devices: a whole 2x2x4 slice. The times are simulated.
32 devices in a mesh: shard: 8 (over z, core), rep: 4 (over y, x).
Axes of the slice: x: 2, y: 2, z: 4, core: 2. Of those that a mesh axis runs over, the one named last changes fastest.
Arguments:
- tokens: bfloat16 [2, 8192, 1024], P(None, ('shard', 'rep')), may hold values from -6 to 6
- cotangent: bfloat16 [2, 8192, 1024], P(None, ('shard', 'rep')), may hold values from -6 to 6
- seq_lengths: int32 [2, 4, 8, 4], P(None, 'rep'), may hold values from 1 to 128, 256 in all within a row
- dealing: int32 [2, 4, 32], P(None, 'rep'), may hold values from 0 to 31, each once within a row
- attention_gain: bfloat16 [1024], P('shard'), may hold values from 0.25 to 1.75
- attention_shift: bfloat16 [1024], P('shard'), may hold values from -1 to 1
- input_weight: bfloat16 [1024, 3072], P('shard'), may hold values from -0.25 to 0.25
- query_bias: bfloat16 [1024], P('shard'), may hold values from -1 to 1
- value_bias: bfloat16 [1024], P('shard'), may hold values from -1 to 1
- output_weight: bfloat16 [1024, 1024], P('shard'), may hold values from -0.5 to 0.5
- output_bias: bfloat16 [1024], P('shard'), may hold values from -1 to 1
- feed_gain: bfloat16 [1024], P('shard'), may hold values from 0.25 to 1.75
- feed_shift: bfloat16 [1024], P('shard'), may hold values from -1 to 1
- up_weight: bfloat16 [1024, 4096], P('shard'), may hold values from -0.1875 to 0.1875
- up_bias: bfloat16 [4096], P('shard'), may hold values from -1 to 1
- down_weight: bfloat16 [4096, 1024], P('shard'), may hold values from -0.09375 to 0.09375
- down_bias: bfloat16 [1024], P('shard'), may hold values from -1 to 1
Outputs:
- block_out: bfloat16 [2, 8192, 1024], P(None, ('shard', 'rep'))
- input_grad: bfloat16 [2, 8192, 1024], P(None, ('shard', 'rep'))
- attention_gain_grad: float32 [1024], P('shard')
- attention_shift_grad: float32 [1024], P('shard')
- input_weight_grad: float32 [1024, 3072], P('shard')
- query_bias_grad: float32 [1024], P('shard')
- value_bias_grad: float32 [1024], P('shard')
- output_weight_grad: float32 [1024, 1024], P('shard')
- output_bias_grad: float32 [1024], P('shard')
- feed_gain_grad: float32 [1024], P('shard')
- feed_shift_grad: float32 [1024], P('shard')
- up_weight_grad: float32 [1024, 4096], P('shard')
- up_bias_grad: float32 [4096], P('shard')
- down_weight_grad: float32 [4096, 1024], P('shard')
- down_bias_grad: float32 [1024], P('shard')
Inputs may be any that keep to these rules, and one draw needn't show every extreme that they name: `seq_lengths`: for every micro-batch and replica, the 4 lengths given for each index of shard add up to 256. `dealing`: for every micro-batch and replica, each dealt number appears once; number n goes to index n // 4 of shard.
All inputs are finite; a program needn't handle non-finite values.
Results may differ from a plain program's by a relative error of at most 0.013.
The roundings to bfloat16 on the way count: a program that leaves them out, or rounds other values in their place, can miss the bound.
Values may be sent and summed in bfloat16 or wider, within the bound.
A program may use at most 256 MiB of HBM per device.

v0:
```python
from functools import partial

import jax
import jax.numpy as jnp
from jax import lax
from jax.sharding import PartitionSpec as P

HD = 64


EPSILON = 1e-05
MASKED = -1e30


def deal_maps(seq_lengths, dealing, rows_dev):
    groups, per_device = seq_lengths.shape
    total_seqs = groups * per_device
    numbers = jnp.arange(total_seqs, dtype=jnp.int32)
    flat_lengths = seq_lengths.reshape(total_seqs)
    matched = (dealing[:, None] == numbers[None, :]).astype(jnp.int32)
    packed_length = jnp.sum(matched * flat_lengths[None, :], axis=1, dtype=jnp.int32)
    packed_start = jnp.cumsum(packed_length, dtype=jnp.int32) - packed_length
    start_of = jnp.sum(matched * packed_start[:, None], axis=0, dtype=jnp.int32).reshape(
        groups, per_device
    )
    bin_start = jnp.cumsum(seq_lengths, axis=1, dtype=jnp.int32) - seq_lengths
    places = jnp.arange(rows_dev, dtype=jnp.int32)
    inside = (places[None, :, None] >= bin_start[:, None, :]).astype(jnp.int32)
    segment = jnp.sum(inside, axis=2, dtype=jnp.int32) - 1
    picked = (segment[:, :, None] == jnp.arange(per_device, dtype=jnp.int32)[None, None, :]).astype(
        jnp.int32
    )
    position = places[None, :] - jnp.sum(picked * bin_start[:, None, :], axis=2, dtype=jnp.int32)
    source = jnp.sum(picked * start_of[:, None, :], axis=2, dtype=jnp.int32) + position
    total_rows = groups * rows_dev
    all_rows = jnp.arange(total_rows, dtype=jnp.int32)
    owner_seq = (
        jnp.sum(
            (all_rows[:, None] >= packed_start[None, :]).astype(jnp.int32), axis=1, dtype=jnp.int32
        )
        - 1
    )
    owner_hit = (owner_seq[:, None] == numbers[None, :]).astype(jnp.int32)
    offset = all_rows - jnp.sum(owner_hit * packed_start[None, :], axis=1, dtype=jnp.int32)
    target = jnp.sum(owner_hit * dealing[None, :], axis=1, dtype=jnp.int32)
    target_hit = (target[:, None] == numbers[None, :]).astype(jnp.int32)
    flat_start = bin_start.reshape(total_seqs)
    backward_row = (
        target // per_device * rows_dev
        + jnp.sum(target_hit * flat_start[None, :], axis=1, dtype=jnp.int32)
        + offset
    )
    return (
        source.reshape(total_rows),
        segment.reshape(total_rows),
        position.reshape(total_rows),
        backward_row,
    )


def layer_norm(values, norm_gain, norm_shift):
    center = values - jnp.mean(values, axis=-1, keepdims=True)
    spread = jnp.mean(center * center, axis=-1, keepdims=True)
    return center * lax.rsqrt(spread + EPSILON) * norm_gain + norm_shift


def gelu_tanh(values):
    return jax.nn.gelu(values, approximate=True)


def rows_dot(left, right):
    return lax.dot_general(
        left, right, (((0,), (0,)), ((), ())), preferred_element_type=jnp.float32
    )


def back_dot(left, right):
    return lax.dot_general(
        left, right, (((1,), (1,)), ((), ())), preferred_element_type=jnp.float32
    )


def column_sum(values):
    return jnp.sum(values.astype(jnp.float32), axis=0)


def attention_scores(queries, keys_all, allowed):
    raw_scores = jnp.einsum("qhd,khd->hqk", queries, keys_all, preferred_element_type=jnp.float32)
    return jnp.where(allowed[None], raw_scores * float(HD) ** (-0.5), MASKED)


def take_rows(wanted, carried, pieces):
    row_count = pieces[0].shape[1]
    present = (wanted >= 0) & (wanted < row_count)
    clipped = jnp.clip(wanted, 0, row_count - 1)[:, :, None]
    return tuple(
        (
            jnp.where(
                present[:, :, None], jnp.take_along_axis(shard_rows, clipped, axis=1), previous
            )
            for shard_rows, previous in zip(pieces, carried)
        )
    )


def forward_rows(token_rows, segment, position, weights):
    (
        attention_gain,
        attention_shift,
        input_weight,
        query_bias,
        value_bias,
        output_weight,
        output_bias,
        feed_gain,
        feed_shift,
        up_weight,
        up_bias,
        down_weight,
        down_bias,
    ) = weights
    width = token_rows.shape[1]
    heads = width // HD
    inputs = token_rows.astype(jnp.float32)
    normed, first_back = jax.vjp(
        layer_norm, inputs, attention_gain.astype(jnp.float32), attention_shift.astype(jnp.float32)
    )
    normed_low = normed.astype(jnp.bfloat16)
    mixed = jnp.dot(normed_low, input_weight, preferred_element_type=jnp.float32)
    queries = (
        (mixed[:, :width] + query_bias.astype(jnp.float32))
        .astype(jnp.bfloat16)
        .reshape(-1, heads, HD)
    )
    keys_all = mixed[:, width : 2 * width].astype(jnp.bfloat16).reshape(-1, heads, HD)
    values_all = (
        (mixed[:, 2 * width :] + value_bias.astype(jnp.float32))
        .astype(jnp.bfloat16)
        .reshape(-1, heads, HD)
    )
    allowed = (segment[:, None] == segment[None, :]) & (position[None, :] <= position[:, None])
    scores = attention_scores(queries, keys_all, allowed)
    log_total = jax.nn.logsumexp(scores, axis=-1, keepdims=True)
    soft_low = jnp.exp(scores - log_total).astype(jnp.bfloat16)
    attended = jnp.einsum(
        "hqk,khd->qhd", soft_low, values_all, preferred_element_type=jnp.float32
    ).reshape(-1, width)
    branch = attended.astype(jnp.bfloat16)
    middle = (
        inputs
        + jnp.dot(branch, output_weight, preferred_element_type=jnp.float32)
        + output_bias.astype(jnp.float32)
    )
    normed_two, second_back = jax.vjp(
        layer_norm, middle, feed_gain.astype(jnp.float32), feed_shift.astype(jnp.float32)
    )
    normed_two_low = normed_two.astype(jnp.bfloat16)
    hidden = jnp.dot(
        normed_two_low, up_weight, preferred_element_type=jnp.float32
    ) + up_bias.astype(jnp.float32)
    activated, gelu_back = jax.vjp(gelu_tanh, hidden)
    activated_low = activated.astype(jnp.bfloat16)
    result = (
        middle
        + jnp.dot(activated_low, down_weight, preferred_element_type=jnp.float32)
        + down_bias.astype(jnp.float32)
    )
    saved_state = (
        normed_low,
        queries,
        keys_all,
        values_all,
        allowed,
        log_total,
        branch,
        normed_two_low,
        activated_low,
        first_back,
        second_back,
        gelu_back,
    )
    return (result.astype(jnp.bfloat16), saved_state)


def backward_rows(cotangent_rows, saved_state, matrices):
    input_weight, output_weight, up_weight, down_weight = matrices
    (
        normed_low,
        queries,
        keys_all,
        values_all,
        allowed,
        log_total,
        branch,
        normed_two_low,
        activated_low,
        first_back,
        second_back,
        gelu_back,
    ) = saved_state
    width = branch.shape[1]
    heads = width // HD
    score_scale = float(HD) ** (-0.5)
    upstream = cotangent_rows.astype(jnp.float32)
    down_low = upstream.astype(jnp.bfloat16)
    down_weight_grad = rows_dot(activated_low, down_low)
    down_bias_grad = column_sum(down_low)
    (hidden_grad,) = gelu_back(back_dot(down_low, down_weight))
    hidden_low = hidden_grad.astype(jnp.bfloat16)
    up_weight_grad = rows_dot(normed_two_low, hidden_low)
    up_bias_grad = column_sum(hidden_low)
    feed_part, feed_gain_grad, feed_shift_grad = second_back(back_dot(hidden_low, up_weight))
    middle_grad = upstream + feed_part
    output_low = middle_grad.astype(jnp.bfloat16)
    output_weight_grad = rows_dot(branch, output_low)
    output_bias_grad = column_sum(output_low)
    attended_low = back_dot(output_low, output_weight).astype(jnp.bfloat16).reshape(-1, heads, HD)
    scores = attention_scores(queries, keys_all, allowed)
    soft = jnp.exp(scores - log_total)
    soft_grad = jnp.einsum(
        "qhd,khd->hqk", attended_low, values_all, preferred_element_type=jnp.float32
    )
    score_low = (soft * (soft_grad - jnp.sum(soft * soft_grad, axis=-1, keepdims=True))).astype(
        jnp.bfloat16
    )
    query_grad = (
        (
            jnp.einsum("hqk,khd->qhd", score_low, keys_all, preferred_element_type=jnp.float32)
            * score_scale
        )
        .astype(jnp.bfloat16)
        .reshape(-1, width)
    )
    key_grad = (
        (
            jnp.einsum("hqk,qhd->khd", score_low, queries, preferred_element_type=jnp.float32)
            * score_scale
        )
        .astype(jnp.bfloat16)
        .reshape(-1, width)
    )
    value_grad = (
        jnp.einsum(
            "hqk,qhd->khd",
            soft.astype(jnp.bfloat16),
            attended_low,
            preferred_element_type=jnp.float32,
        )
        .astype(jnp.bfloat16)
        .reshape(-1, width)
    )
    mixed_grad = jnp.concatenate([query_grad, key_grad, value_grad], axis=1)
    input_weight_grad = rows_dot(normed_low, mixed_grad)
    inputs_part, attention_gain_grad, attention_shift_grad = first_back(
        back_dot(mixed_grad, input_weight)
    )
    input_grad = (middle_grad + inputs_part).astype(jnp.bfloat16)
    return (
        input_grad,
        (
            attention_gain_grad,
            attention_shift_grad,
            input_weight_grad,
            column_sum(query_grad),
            column_sum(value_grad),
            output_weight_grad,
            output_bias_grad,
            feed_gain_grad,
            feed_shift_grad,
            up_weight_grad,
            up_bias_grad,
            down_weight_grad,
            down_bias_grad,
        ),
    )


def shards(
    tokens,
    cotangent,
    seq_lengths,
    dealing,
    attention_gain,
    attention_shift,
    input_weight,
    query_bias,
    value_bias,
    output_weight,
    output_bias,
    feed_gain,
    feed_shift,
    up_weight,
    up_bias,
    down_weight,
    down_bias,
):
    micro_count, tok_rows, width = tokens.shape
    own_start = lax.axis_index("shard") * tok_rows
    full_maps = jax.vmap(partial(deal_maps, rows_dev=tok_rows))(seq_lengths[:, 0], dealing[:, 0])
    source, segment, position, backward_row = [
        lax.dynamic_slice_in_dim(member, own_start, tok_rows, 1) for member in full_maps
    ]
    empty_rows = jnp.zeros_like(tokens)
    dealt_tokens, dealt_cotangent = take_rows(
        source,
        (empty_rows, empty_rows),
        (
            lax.all_gather(tokens, "shard", axis=1, tiled=True),
            lax.all_gather(cotangent, "shard", axis=1, tiled=True),
        ),
    )
    weights = (
        attention_gain,
        attention_shift,
        input_weight,
        query_bias,
        value_bias,
        output_weight,
        output_bias,
        feed_gain,
        feed_shift,
        up_weight,
        up_bias,
        down_weight,
        down_bias,
    )
    totals = None
    results = []
    input_grads = []
    for micro_step in range(micro_count):
        forward_weights = (
            lax.all_gather(weights[0], "shard", axis=0, tiled=True),
            lax.all_gather(weights[1], "shard", axis=0, tiled=True),
            lax.all_gather(weights[2], "shard", axis=0, tiled=True),
            lax.all_gather(weights[3], "shard", axis=0, tiled=True),
            lax.all_gather(weights[4], "shard", axis=0, tiled=True),
            lax.all_gather(weights[5], "shard", axis=0, tiled=True),
            lax.all_gather(weights[6], "shard", axis=0, tiled=True),
            lax.all_gather(weights[7], "shard", axis=0, tiled=True),
            lax.all_gather(weights[8], "shard", axis=0, tiled=True),
            lax.all_gather(weights[9], "shard", axis=0, tiled=True),
            lax.all_gather(weights[10], "shard", axis=0, tiled=True),
            lax.all_gather(weights[11], "shard", axis=0, tiled=True),
            lax.all_gather(weights[12], "shard", axis=0, tiled=True),
        )
        result, saved_state = forward_rows(
            dealt_tokens[micro_step], segment[micro_step], position[micro_step], forward_weights
        )
        matrices = (
            lax.all_gather(input_weight, "shard", axis=0, tiled=True),
            lax.all_gather(output_weight, "shard", axis=0, tiled=True),
            lax.all_gather(up_weight, "shard", axis=0, tiled=True),
            lax.all_gather(down_weight, "shard", axis=0, tiled=True),
        )
        input_grad, local_grads = backward_rows(dealt_cotangent[micro_step], saved_state, matrices)
        results.append(result)
        input_grads.append(input_grad)
        if micro_step == 0:
            totals = local_grads
        else:
            totals = tuple((earlier + latest for earlier, latest in zip(totals, local_grads)))
    totals = lax.psum_scatter(totals, "shard", scatter_dimension=0, tiled=True)
    totals = lax.psum(totals, "rep")
    restored_out, restored_grad = take_rows(
        backward_row,
        (empty_rows, empty_rows),
        (
            lax.all_gather(jnp.stack(results), "shard", axis=1, tiled=True),
            lax.all_gather(jnp.stack(input_grads), "shard", axis=1, tiled=True),
        ),
    )
    return (restored_out, restored_grad) + tuple(totals)


def solution(mesh):
    return jax.shard_map(
        shards,
        mesh=mesh,
        in_specs=(
            P(None, ("shard", "rep"), None),
            P(None, ("shard", "rep"), None),
            P(None, "rep", None, None),
            P(None, "rep", None),
            P("shard"),
            P("shard"),
            P("shard", None),
            P("shard"),
            P("shard"),
            P("shard", None),
            P("shard"),
            P("shard"),
            P("shard"),
            P("shard", None),
            P("shard"),
            P("shard", None),
            P("shard"),
        ),
        out_specs=(
            P(None, ("shard", "rep"), None),
            P(None, ("shard", "rep"), None),
            P("shard"),
            P("shard"),
            P("shard", None),
            P("shard"),
            P("shard"),
            P("shard", None),
            P("shard"),
            P("shard"),
            P("shard"),
            P("shard", None),
            P("shard"),
            P("shard", None),
            P("shard"),
        ),
        check_vma=False,
    )
```

profile of v0, /device:TPU:0, one launch (start us, length us, event | category | flops | bytes accessed | tf_op | source)
XLA Modules:
  0.0 1307.7 jit_solution(15719994966998990020)
XLA Ops:
  11.6 13.5 %all-gather = bf16[8,1,128]{2,1,0:T(2,128)(2,1)S(1)} all-gather(bf16[1,1,128]{2,1,0:T(2,128)(2,1)S(1)} %bitcast.346), channel_id=1, replica_groups=mesh['shard'=8,'rep'=4] {'shard'}, dimensions={0}, use_global_device_ids=true | all-gather | bytes 2304 | tf_op jit(solution)/shard_map/all_gather | solution.py:332
  25.1 9.0 all-gather.1
  34.1 12.6 all-gather.3
  46.8 9.1 all-gather.2
  55.9 12.1 all-gather.4
  67.9 9.1 all-gather.5
  77.0 10.3 all-gather.6
  88.1 14.0 %all-gather.7 = bf16[8,1,512]{2,1,0:T(2,128)(2,1)S(1)} all-gather(bf16[1,1,512]{2,1,0:T(2,128)(2,1)S(1)} %reshape.473), channel_id=1, replica_groups=mesh['shard'=8,'rep'=4] {'shard'}, dimensions={0}, use_global_device_ids=true | all-gather | bytes 9216 | tf_op jit(solution)/shard_map/all_gather | solution.py:342
  104.7 8.1 gather_fusion.2
  112.7 64.0 %all-gather.18.cloned.1.call-done = bf16[2,2048,1024]{2,1,0:T(8,128)(2,1)} async-done(((bf16[2,256,1024]{2,1,0:T(8,128)(2,1)}), bf16[2,2048,1024]{2,1,0:T(8,128)(2,1)}) %all-gather.18.cloned.1.call-update) | async-done | bytes 8388624 | tf_op jit(solution)/shard_map/all_gather | solution.py:308
  176.8 11.4 gather_fusion
  191.4 50.2 %all-gather.20.cloned.1.call-done = bf16[1024,3072]{1,0:T(8,128)(2,1)} async-done(((bf16[128,3072]{1,0:T(8,128)(2,1)}), bf16[1024,3072]{1,0:T(8,128)(2,1)}) %all-gather.20.cloned.1.call-update) | async-done | bytes 6291472 | tf_op jit(solution)/shard_map/all_gather | solution.py:334
  279.5 74.3 %all-gather.24.cloned.1.call-done = bf16[1024,4096]{1,0:T(8,128)(2,1)} async-done(((bf16[128,4096]{1,0:T(8,128)(2,1)}), bf16[1024,4096]{1,0:T(8,128)(2,1)}) %all-gather.24.cloned.1.call-update) | async-done | bytes 8388624 | tf_op jit(solution)/shard_map/all_gather | solution.py:341
  353.8 8.3 convolution_add_fusion.4
  366.7 69.3 %all-gather.26.cloned.1.call-done = bf16[4096,1024]{1,0:T(8,128)(2,1)} async-done(((bf16[512,1024]{1,0:T(8,128)(2,1)}), bf16[4096,1024]{1,0:T(8,128)(2,1)}) %all-gather.26.cloned.1.call-update) | async-done | bytes 8388624 | tf_op jit(solution)/shard_map/all_gather | solution.py:343
  435.9 8.5 convert_reduce_fusion.1
  457.1 7.2 multiply_reduce_fusion.3
  507.4 11.0 fusion.65
  518.4 11.7 convolution_add_fusion
  534.7 10.1 convolution_add_fusion.1
  545.5 9.3 all-gather.8
  554.8 7.8 fusion.39
  584.1 65.0 %reduce-scatter.5.cloned.1.call-done = f32[128,3072]{1,0:T(8,128)} async-done(((f32[1024,3072]{1,0:T(8,128)}), f32[128,3072]{1,0:T(8,128)}) %reduce-scatter.5.cloned.1.call-update) | async-done | bytes 1572880 | tf_op jit(solution)/shard_map/reduce_scatter | solution.py:362
  649.2 169.0 %reduce-scatter.11.cloned.1.call-done = f32[512,1024]{1,0:T(8,128)} async-done(((f32[4096,1024]{1,0:T(8,128)}), f32[512,1024]{1,0:T(8,128)}) %reduce-scatter.11.cloned.1.call-update) | async-done | bytes 2097168 | tf_op jit(solution)/shard_map/reduce_scatter | solution.py:362
  818.2 168.9 %reduce-scatter.9.cloned.1.call-done = f32[128,4096]{1,0:T(8,128)} async-done(((f32[1024,4096]{1,0:T(8,128)}), f32[128,4096]{1,0:T(8,128)}) %reduce-scatter.9.cloned.1.call-update) | async-done | bytes 2097168 | tf_op jit(solution)/shard_map/reduce_scatter | solution.py:362
  989.4 28.7 %all-reduce.9 = (f32[1024]{0:T(1024)S(1)}, f32[1024]{0:T(1024)S(1)}, f32[1024]{0:T(1024)S(1)}, f32[1024]{0:T(1024)S(1)}, f32[1024]{0:T(1024)S(1)}, /*index=5*/f3...) all-reduce(f32[1024]{0:T(1024)S(1)} %add.367, ...), channel_id=2, replica_groups=mesh['shard'=8,'rep'=4] {'shard'}, use_global_device_ids=true, to_apply=%region_35.37.clone | all-reduce | flops 12288 | bytes 98304
  1018.8 10.7 all-reduce.10
  1029.5 41.1 %all-gather.28.cloned.1.call-done = bf16[2,2048,1024]{2,1,0:T(8,128)(2,1)} async-done(((bf16[2,256,1024]{2,1,0:T(8,128)(2,1)}), bf16[2,2048,1024]{2,1,0:T(8,128)(2,1)}) %all-gather.28.cloned.1.call-update) | async-done | bytes 8388624 | tf_op jit(solution)/shard_map/all_gather | solution.py:368
  1070.6 8.1 gather_fusion.1
  1078.7 74.4 %all-gather.32.cloned.1.call-done = bf16[2,2048,1024]{2,1,0:T(8,128)(2,1)} async-done(((bf16[2,256,1024]{2,1,0:T(8,128)(2,1)}), bf16[2,2048,1024]{2,1,0:T(8,128)(2,1)}) %all-gather.32.cloned.1.call-update) | async-done | bytes 8388624 | tf_op jit(solution)/shard_map/all_gather | solution.py:369
  1153.1 8.1 gather_fusion.3
  1162.8 130.7 %all-reduce.14.cloned.1.call-done = (f32[128,3072]{1,0:T(8,128)}, f32[128,1024]{1,0:T(8,128)}, f32[128,4096]{1,0:T(8,128)}, f32[512,1024]{1,0:T(8,128)}) async-done(((f32[128,3072]{1,0:T(8,128)}, f32[128,1024]{1,0:T(8,128)}, f32[128,4096]{1,0:T(8,128)}, f32[512,1024]{1,0:T(8,128)}), (f32[128,3072]{1,0:T(8,128)}, f32[128,1024]{1,0:T(8,128)}, f32[128,4096]{1,0:T(8,128)}, ...) | async-done | bytes 6291472 | tf_op jit(solution)/shard_map/psum | solution.py:363
  (364 shorter events, 145.0 us)
Async XLA Ops:
  7.3 97.4 %all-gather.30.cloned.1.call-start = ((), (), s32[]{:S(2)}) async-start(), calls=%async_computation.10 | async-start | bytes 9437184 | tf_op jit(solution)/shard_map/all_gather | solution.py:309
  8.0 168.8 %all-gather.18.cloned.1.call-start = ((), (), s32[]{:S(2)}) async-start(), calls=%async_computation.4 | async-start | bytes 9437184 | tf_op jit(solution)/shard_map/all_gather | solution.py:308
  8.8 232.9 %all-gather.20.cloned.1.call-start = ((), (), s32[]{:S(2)}) async-start(), calls=%async_computation.5 | async-start | bytes 7077888 | tf_op jit(solution)/shard_map/all_gather | solution.py:334
  9.5 261.4 %all-gather.22.cloned.1.call-start = ((), (), s32[]{:S(2)}) async-start(), calls=%async_computation.6 | async-start | bytes 2359296 | tf_op jit(solution)/shard_map/all_gather | solution.py:337
  10.1 343.8 %all-gather.24.cloned.1.call-start = ((), (), s32[]{:S(2)}) async-start(), calls=%async_computation.7 | async-start | bytes 9437184 | tf_op jit(solution)/shard_map/all_gather | solution.py:341
  10.7 425.3 %all-gather.26.cloned.1.call-start = ((), (), s32[]{:S(2)}) async-start(), calls=%async_computation.8 | async-start | bytes 9437184 | tf_op jit(solution)/shard_map/all_gather | solution.py:343
  11.2 572.9 %reduce-scatter.7.cloned.1.call-start = ((), (), s32[]{:S(2)}) async-start(), calls=%async_computation.13 | async-start | bytes 4718592 | tf_op jit(solution)/shard_map/reduce_scatter | solution.py:362
  191.4 309.3 %copy-start.51 = (f32[256]{0:T(256)}, f32[256]{0:T(256)S(1)}, u32[]{:S(2)}) copy-start(f32[256]{0:T(256)S(1)} %fusion.78) | copy-start | bytes 3076
  273.4 191.0 %copy-start.48 = (f32[256]{0:T(256)}, f32[256]{0:T(256)S(1)}, u32[]{:S(2)}) copy-start(f32[256]{0:T(256)S(1)} %broadcast_multiply_fusion.2) | copy-start | bytes 3076
  470.6 178.5 %reduce-scatter.5.cloned.1.call-start = ((), (), s32[]{:S(2)}) async-start(), calls=%async_computation.12 | async-start | bytes 14155776 | tf_op jit(solution)/shard_map/reduce_scatter | solution.py:362
  507.3 310.9 %reduce-scatter.11.cloned.1.call-start = ((), (), s32[]{:S(2)}) async-start(), calls=%async_computation.15 | async-start | bytes 18874368 | tf_op jit(solution)/shard_map/reduce_scatter | solution.py:362
  530.2 456.9 %reduce-scatter.9.cloned.1.call-start = ((), (), s32[]{:S(2)}) async-start(), calls=%async_computation.14 | async-start | bytes 18874368 | tf_op jit(solution)/shard_map/reduce_scatter | solution.py:362
  544.9 525.7 %all-gather.28.cloned.1.call-start = ((), (), s32[]{:S(2)}) async-start(), calls=%async_computation.9 | async-start | bytes 9437184 | tf_op jit(solution)/shard_map/all_gather | solution.py:368
  570.1 583.0 %all-gather.32.cloned.1.call-start = ((), (), s32[]{:S(2)}) async-start(), calls=%async_computation.11 | async-start | bytes 9437184 | tf_op jit(solution)/shard_map/all_gather | solution.py:369
  583.9 403.2 %copy-start.92 = (u32[32]{0:T(128)S(1)}, u32[32]{0:T(128)}, u32[]{:S(2)}) copy-start(u32[32]{0:T(128)} %constant.178) | copy-start | bytes 388
  583.9 405.1 %copy-start.75 = (s32[1,2,2,128]{3,2,1,0:T(2,128)S(1)}, s32[1,2,2,128]{3,2,1,0:T(2,128)}, u32[]{:S(2)}) copy-start(s32[1,2,2,128]{3,2,1,0:T(2,128)} %get-tuple-element.133) | copy-start | bytes 6148
  583.9 405.1 %copy-start.56 = (s32[2,256]{1,0:T(2,128)S(1)}, s32[2,256]{1,0:T(2,128)}, u32[]{:S(2)}) copy-start(s32[2,256]{1,0:T(2,128)} %copy-done.55) | copy-start | bytes 6148
  583.9 405.2 %copy-start.73 = (f32[16,64]{1,0:T(8,128)S(1)}, f32[16,64]{1,0:T(8,128)}, u32[]{:S(2)}) copy-start(f32[16,64]{1,0:T(8,128)} %get-tuple-element.127) | copy-start | bytes 12292
  583.9 405.2 %copy-start.74 = (f32[16,64]{1,0:T(8,128)S(1)}, f32[16,64]{1,0:T(8,128)}, u32[]{:S(2)}) copy-start(f32[16,64]{1,0:T(8,128)} %get-tuple-element.125) | copy-start | bytes 12292
  583.9 405.2 %copy-start.49 = (f32[16,64]{1,0:T(8,128)S(1)}, f32[16,64]{1,0:T(8,128)}, u32[]{:S(2)}) copy-start(f32[16,64]{1,0:T(8,128)} %get-tuple-element.121) | copy-start | bytes 12292
  583.9 405.2 %copy-start.50 = (f32[16,64]{1,0:T(8,128)S(1)}, f32[16,64]{1,0:T(8,128)}, u32[]{:S(2)}) copy-start(f32[16,64]{1,0:T(8,128)} %get-tuple-element.123) | copy-start | bytes 12292
  583.9 405.3 %copy-start.57 = (f32[4096]{0:T(1024)S(1)}, f32[4096]{0:T(1024)}, u32[]{:S(2)}) copy-start(f32[4096]{0:T(1024)} %get-tuple-element.129) | copy-start | bytes 49156
  583.9 405.3 %copy-start.58 = (f32[4096]{0:T(1024)S(1)}, f32[4096]{0:T(1024)}, u32[]{:S(2)}) copy-start(f32[4096]{0:T(1024)} %get-tuple-element.131) | copy-start | bytes 49156
  583.9 405.3 %copy-start.78 = (f32[1024]{0:T(1024)S(1)}, f32[1024]{0:T(1024)}, u32[]{:S(2)}) copy-start(f32[1024]{0:T(1024)} %get-tuple-element.22) | copy-start | bytes 12292
  584.0 405.3 %copy-start.79 = (f32[1024]{0:T(1024)S(1)}, f32[1024]{0:T(1024)}, u32[]{:S(2)}) copy-start(f32[1024]{0:T(1024)} %get-tuple-element.102) | copy-start | bytes 12292
  584.0 405.3 %copy-start.76 = (f32[1024]{0:T(1024)S(1)}, f32[1024]{0:T(1024)}, u32[]{:S(2)}) copy-start(f32[1024]{0:T(1024)} %get-tuple-element.32) | copy-start | bytes 12292
  584.0 405.3 %copy-start.77 = (f32[1024]{0:T(1024)S(1)}, f32[1024]{0:T(1024)}, u32[]{:S(2)}) copy-start(f32[1024]{0:T(1024)} %get-tuple-element.100) | copy-start | bytes 12292
  584.0 405.3 %copy-start.61 = (f32[1024]{0:T(1024)S(1)}, f32[1024]{0:T(1024)}, u32[]{:S(2)}) copy-start(f32[1024]{0:T(1024)} %get-tuple-element.29) | copy-start | bytes 12292
  584.0 405.3 %copy-start.62 = (f32[1024]{0:T(1024)S(1)}, f32[1024]{0:T(1024)}, u32[]{:S(2)}) copy-start(f32[1024]{0:T(1024)} %get-tuple-element.30) | copy-start | bytes 12292
  584.0 405.3 %copy-start.59 = (f32[1024]{0:T(1024)S(1)}, f32[1024]{0:T(1024)}, u32[]{:S(2)}) copy-start(f32[1024]{0:T(1024)} %get-tuple-element.82) | copy-start | bytes 12292
  584.0 405.3 %copy-start.60 = (f32[1024]{0:T(1024)S(1)}, f32[1024]{0:T(1024)}, u32[]{:S(2)}) copy-start(f32[1024]{0:T(1024)} %get-tuple-element.84) | copy-start | bytes 12292
  584.1 709.5 %all-reduce.14.cloned.1.call-start = ((), (), s32[]{:S(2)}) async-start(), calls=%async_computation.16 | async-start | bytes 12582912 | tf_op jit(solution)/shard_map/psum | solution.py:363
  (74 other events, 1389.2 us)
Sparse Core Ops, SparseCore 0:
  9.7 84.8 all-gather.29
  96.2 80.5 all-gather.17
  178.4 63.1 all-gather.19
  243.1 27.7 all-gather.21
  272.4 81.4 all-gather.23
  355.3 80.5 all-gather.25
  470.8 48.3 reduce-scatter.6
  521.5 127.6 reduce-scatter.4
  651.5 166.6 reduce-scatter.10
  820.4 166.6 reduce-scatter.8
  989.3 81.2 all-gather.27
  1072.6 80.4 all-gather.31
  1156.8 136.6 all-reduce.13
where the time goes:
time: 1310 us
  waiting for transfers between devices  913 us (70%)
  matrix products  152 us (12%)
  blocking collectives  138 us (11%)
  local copies, waits for them, and re-layouts  64.4 us (5%)
  other arithmetic  22.4 us (2%)
  between operations  17.1 us (1%)
    reduce_scatter x4, waiting for transfers between devices, shards(): totals = lax.psum_scatter(totals, 'shard', scatter_dimension=0, tiled=True)  403 us
    psum x1, waiting for transfers between devices, shards(): totals = lax.psum(totals, 'rep')  131 us
    all_gather x1, waiting for transfers between devices, shards(): lax.all_gather(jnp.stack(input_grads), 'shard', axis=1, tiled=True)  74.4 us
    all_gather x1, waiting for transfers between devices, shards(): lax.all_gather(weights[9], 'shard', axis=0, tiled=True)  74.3 us
    all_gather x1, waiting for transfers between devices, shards(): lax.all_gather(weights[11], 'shard', axis=0, tiled=True)  69.3 us
    all_gather x1, waiting for transfers between devices, shards(): lax.all_gather(tokens, 'shard', axis=1, tiled=True)  64 us
    all_gather x1, waiting for transfers between devices, shards(): lax.all_gather(weights[2], 'shard', axis=0, tiled=True)  50.2 us
    dot_general x8, matrix products, rows_dot(): lax.dot_general(left, right, (((0,), (0,)), ((), ())), preferred_element_...  49.8 us
  transfers between devices with their start and end apart: 13, of which 11 were waited for; matrix products, arithmetic and copies ran while one was open for 14% of the time, Pallas kernels for 0%

commit v1 on v0

v1 whole, which is shorter than its diff:
```python
from functools import partial

import jax
import jax.numpy as jnp
from jax import lax
from jax.experimental import pallas as pl
from jax.experimental.pallas import tpu as pltpu
from jax.sharding import PartitionSpec as P

HD = 64
BLOCK = 128
EPSILON = 1e-05
MASKED = -1e30
AXES = ("shard", "rep")
F32 = jnp.float32
LOW = jnp.bfloat16


def dot(left, right):
    return jnp.dot(left, right, preferred_element_type=F32)


def rows_dot(left, right):
    return lax.dot_general(left, right, (((0,), (0,)), ((), ())), preferred_element_type=F32)


def back_dot(left, right):
    return lax.dot_general(left, right, (((1,), (1,)), ((), ())), preferred_element_type=F32)


def pick(stacked, index, axis=0):
    return lax.dynamic_index_in_dim(stacked, index, axis, keepdims=False)


def normalize(values):
    center = values - jnp.mean(values, axis=-1, keepdims=True)
    inverse = lax.rsqrt(jnp.mean(center * center, axis=-1, keepdims=True) + EPSILON)
    return center * inverse, inverse


def normalize_back(upper, gain, unit, inverse):
    scaled = upper * gain
    mean_scaled = jnp.mean(scaled, axis=-1, keepdims=True)
    mean_product = jnp.mean(scaled * unit, axis=-1, keepdims=True)
    return inverse * (scaled - mean_scaled - unit * mean_product)


def gelu_tanh(values):
    return jax.nn.gelu(values, approximate=True)


def sequence_starts(seq_lengths, dealing, first, rows):
    total = dealing.shape[0]
    numbers = jnp.arange(total, dtype=jnp.int32)
    matched = (dealing[:, None] == numbers[None, :]).astype(jnp.int32)
    packed_length = jnp.sum(matched * seq_lengths.reshape(total)[None, :], axis=1)
    before = (numbers[None, :] < numbers[:, None]).astype(jnp.int32)
    packed_start = jnp.sum(before * packed_length[None, :], axis=1)
    own = first + jnp.arange(rows, dtype=jnp.int32)
    return jnp.max(
        jnp.where(packed_start[None, :] <= own[:, None], packed_start[None, :], 0), axis=1
    )


def window(ref, row, previous, column):
    return jnp.concatenate(
        [
            ref[pl.ds(previous, BLOCK), column : column + BLOCK],
            ref[pl.ds(row, BLOCK), column : column + BLOCK],
        ],
        axis=0,
    )


def block_rows(step, blocks, body_rows):
    micro, block = step // blocks, step % blocks
    row = pl.multiple_of(step * BLOCK, BLOCK)
    previous = jnp.where(block == 0, body_rows + micro * BLOCK, row - BLOCK)
    return row, pl.multiple_of(previous, BLOCK)


def soft_weights(query_half, keys, allowed):
    scores = back_dot(query_half, keys) * float(HD) ** (-0.5)
    scores = jnp.where(allowed, scores, MASKED)
    top = jnp.max(scores, axis=1, keepdims=True)
    powers = jnp.exp(scores - top)
    return powers / jnp.sum(powers, axis=1, keepdims=True)


def allowed_keys(start_ref, row):
    places = lax.broadcasted_iota(jnp.int32, (BLOCK, 2 * BLOCK), 1)
    lines = lax.broadcasted_iota(jnp.int32, (BLOCK, 2 * BLOCK), 0)
    return (places >= start_ref[pl.ds(row, BLOCK), :]) & (places <= lines + BLOCK)


def attention_kernel(blocks, width, mixed_ref, start_ref, branch_ref):
    body_rows = branch_ref.shape[0]
    left = lax.broadcasted_iota(jnp.int32, (BLOCK, BLOCK), 1) < HD

    def step_body(step, _):
        row, previous = block_rows(step, blocks, body_rows)
        allowed = allowed_keys(start_ref, row)
        for column in range(0, width, BLOCK):
            queries = mixed_ref[pl.ds(row, BLOCK), column : column + BLOCK]
            keys = window(mixed_ref, row, previous, width + column)
            values = window(mixed_ref, row, previous, 2 * width + column)
            parts = []
            for half in (left, ~left):
                soft = soft_weights(jnp.where(half, queries, 0), keys, allowed)
                parts.append(dot(soft.astype(LOW), values))
            branch_ref[pl.ds(row, BLOCK), column : column + BLOCK] = jnp.where(
                left, parts[0], parts[1]
            ).astype(LOW)
        return 0

    lax.fori_loop(0, body_rows // BLOCK, step_body, 0)


def attention_back_kernel(blocks, width, mixed_ref, start_ref, upper_ref, grad_ref, sums_ref):
    body_rows = upper_ref.shape[0]
    left = lax.broadcasted_iota(jnp.int32, (BLOCK, BLOCK), 1) < HD
    left_tall = lax.broadcasted_iota(jnp.int32, (2 * BLOCK, BLOCK), 1) < HD
    scale = float(HD) ** (-0.5)
    sums_ref[...] = jnp.zeros_like(sums_ref)

    def step_body(step, _):
        row, previous = block_rows(step, blocks, body_rows)
        allowed = allowed_keys(start_ref, row)
        for column in range(0, width, BLOCK):
            queries = mixed_ref[pl.ds(row, BLOCK), column : column + BLOCK]
            keys = window(mixed_ref, row, previous, width + column)
            values = window(mixed_ref, row, previous, 2 * width + column)
            upper = upper_ref[pl.ds(row, BLOCK), column : column + BLOCK]
            parts = []
            for half in (left, ~left):
                soft = soft_weights(jnp.where(half, queries, 0), keys, allowed)
                soft_grad = back_dot(jnp.where(half, upper, 0), values)
                total = jnp.sum(soft * soft_grad, axis=1, keepdims=True)
                score_low = (soft * (soft_grad - total)).astype(LOW)
                parts.append(
                    (
                        dot(score_low, keys) * scale,
                        rows_dot(score_low, queries) * scale,
                        rows_dot(soft.astype(LOW), upper),
                    )
                )
            grad_ref[pl.ds(row, BLOCK), column : column + BLOCK] = jnp.where(
                left, parts[0][0], parts[1][0]
            ).astype(LOW)
            for slot in (1, 2):
                joined = jnp.where(left_tall, parts[0][slot], parts[1][slot])
                place = (slot - 1) * width + column
                sums_ref[pl.ds(previous, BLOCK), place : place + BLOCK] += joined[:BLOCK]
                sums_ref[pl.ds(row, BLOCK), place : place + BLOCK] += joined[BLOCK:]
        return 0

    lax.fori_loop(0, body_rows // BLOCK, step_body, 0)
    grad_ref[:, width:] = sums_ref[...].astype(LOW)
    grad_ref[body_rows:, :width] = jnp.zeros((grad_ref.shape[0] - body_rows, width), LOW)


def attention(mixed, starts, blocks):
    width = mixed.shape[1] // 3
    rows = starts.shape[0]
    vmem = pl.BlockSpec(memory_space=pltpu.VMEM)
    return pl.pallas_call(
        partial(attention_kernel, blocks, width),
        out_shape=jax.ShapeDtypeStruct((rows, width), LOW),
        in_specs=[vmem, vmem],
        out_specs=vmem,
        cost_estimate=pl.CostEstimate(
            flops=rows * width * BLOCK * 16, bytes_accessed=8 << 20, transcendentals=0
        ),
        compiler_params=pltpu.CompilerParams(vmem_limit_bytes=40 << 20),
    )(mixed, starts)


def attention_back(mixed, starts, upper, blocks):
    width = mixed.shape[1] // 3
    rows = starts.shape[0]
    vmem = pl.BlockSpec(memory_space=pltpu.VMEM)
    return pl.pallas_call(
        partial(attention_back_kernel, blocks, width),
        out_shape=jax.ShapeDtypeStruct(mixed.shape, LOW),
        in_specs=[vmem, vmem, vmem],
        out_specs=vmem,
        scratch_shapes=[pltpu.VMEM((mixed.shape[0], 2 * width), F32)],
        cost_estimate=pl.CostEstimate(
            flops=rows * width * BLOCK * 40, bytes_accessed=16 << 20, transcendentals=0
        ),
        compiler_params=pltpu.CompilerParams(vmem_limit_bytes=40 << 20),
    )(mixed, starts, upper)


class Links:
    def __init__(self, chips, reps):
        self.chips, self.reps = chips, reps
        shard = lax.axis_index("shard")
        self.chip, self.core, self.rep = shard // 2, shard % 2, lax.axis_index("rep")

    def flat(self, chip, core, rep):
        return (chip * 2 + core) * self.reps + rep

    def swap(self, values, chip=0, core=0, rep=0):
        pairs = [
            (self.flat(a, b, d), self.flat(a ^ chip, b ^ core, d ^ rep))
            for a in range(self.chips)
            for b in range(2)
            for d in range(self.reps)
        ]
        return lax.ppermute(values, AXES, pairs)

    def shift(self, values, by):
        pairs = [
            (self.flat(a, b, d), self.flat(a + by, b, d))
            for a in range(self.chips)
            if 0 <= a + by < self.chips
            for b in range(2)
            for d in range(self.reps)
        ]
        return lax.ppermute(values, AXES, pairs)

    def by_core(self, own, other, axis):
        first = jnp.where(self.core == 0, own, other)
        second = jnp.where(self.core == 0, other, own)
        return jnp.concatenate([first, second], axis=axis)

    def halves(self, matrix, parts):
        rows, columns = matrix.shape
        blocks = self.chips * parts
        view = matrix.reshape(rows, blocks, 2, columns // (2 * blocks))
        keep = pick(view, self.core, 2).reshape(rows, columns // 2)
        give = pick(view, 1 - self.core, 2).reshape(rows, columns // 2)
        return self.by_core(keep, self.swap(give, core=1), 0)

    def gather(self, chip_rows):
        rows, columns = chip_rows.shape
        quarter = rows // self.reps
        quarters = chip_rows.reshape(self.reps, quarter, columns)
        piece = pick(quarters, self.rep)
        pieces = jnp.stack([self.swap(piece, chip=j) for j in range(1, self.chips)])
        found = [pieces] + [None] * (self.reps - 1)
        if self.reps == 4:
            half = quarter // 2
            found[1] = self.swap(pieces, rep=1)
            found[2] = self.swap(pieces, rep=2)
            upper = self.swap(found[1][:, :half], rep=2)
            lower = self.swap(found[2][:, half:], rep=1)
            found[3] = jnp.concatenate([upper, lower], axis=1)
        else:
            for j in range(1, self.reps):
                found[j] = self.swap(pieces, rep=j)
        stacked = jnp.stack(
            [
                jnp.concatenate([pick(quarters, self.rep ^ j)[None], found[j]], axis=0)
                for j in range(self.reps)
            ]
        )
        ordered = []
        for chip in range(self.chips):
            for rep in range(self.reps):
                at = (self.rep ^ rep, self.chip ^ chip, 0, 0)
                ordered.append(
                    lax.dynamic_slice(stacked, at, (1, 1, quarter, columns)).reshape(
                        quarter, columns
                    )
                )
        return jnp.concatenate(ordered, axis=0)

    def reduce(self, grads):
        chips, reps = self.chips, self.reps
        rows, columns = grads.shape
        quarter = rows // (chips * reps)
        view = grads.astype(LOW).reshape(chips, reps, quarter, columns)
        mine = pick(view, self.rep, 1).astype(F32)
        if reps == 4:
            half = quarter // 2
            across = pick(view, self.rep ^ 3, 1)
            upper = self.swap(across[:, :half], rep=1)
            lower = self.swap(across[:, half:], rep=2)
            to_x = pick(view, self.rep ^ 1, 1)
            to_y = pick(view, self.rep ^ 2, 1)
            to_x = jnp.concatenate(
                [to_x[:, :half], (to_x[:, half:].astype(F32) + lower.astype(F32)).astype(LOW)],
                axis=1,
            )
            to_y = jnp.concatenate(
                [(to_y[:, :half].astype(F32) + upper.astype(F32)).astype(LOW), to_y[:, half:]],
                axis=1,
            )
            mine = (
                mine + self.swap(to_x, rep=1).astype(F32) + self.swap(to_y, rep=2).astype(F32)
            )
        else:
            for j in range(1, reps):
                mine = mine + self.swap(pick(view, self.rep ^ j, 1), rep=j).astype(F32)
        total = pick(mine, self.chip)
        sends = mine.astype(LOW)
        for j in range(1, chips):
            total = total + self.swap(pick(sends, self.chip ^ j), chip=j).astype(F32)
        return self.spread(total.astype(LOW))

    def spread(self, own):
        if self.reps == 4:
            half = own.shape[0] // 2
            from_x = self.swap(own, rep=1)
            from_y = self.swap(own, rep=2)
            upper = self.swap(from_x[:half], rep=2)
            lower = self.swap(from_y[half:], rep=1)
            found = [own, from_x, from_y, jnp.concatenate([upper, lower], axis=0)]
        else:
            found = [own] + [self.swap(own, rep=j) for j in range(1, self.reps)]
        stacked = jnp.stack(found)
        return jnp.concatenate([pick(stacked, self.rep ^ j) for j in range(self.reps)], axis=0)

    def unhalves(self, chip_rows, parts):
        rows, columns = chip_rows.shape
        view = chip_rows.reshape(2, rows // 2, columns)
        blocks = self.chips * parts
        keep = pick(view, self.core).reshape(rows // 2, blocks, 1, columns // blocks)
        came = self.swap(pick(view, 1 - self.core), core=1)
        came = came.reshape(rows // 2, blocks, 1, columns // blocks)
        return self.by_core(keep, came, 2).reshape(rows // 2, 2 * columns)

    def gather_vectors(self, packed):
        pair = self.by_core(packed[None], self.swap(packed, core=1)[None], 0)
        found = jnp.stack([pair] + [self.swap(pair, chip=j) for j in range(1, self.chips)])
        ordered = [pick(found, self.chip ^ j) for j in range(self.chips)]
        return jnp.concatenate(ordered, axis=0)

    def reduce_vectors(self, partial_sums):
        chips, reps = self.chips, self.reps
        view = partial_sums.reshape(chips, 2, -1)
        total = None
        for a in range(chips):
            for b in range(2):
                row = pick(pick(view, self.chip ^ a), self.core ^ b)
                row = row if a == b == 0 else self.swap(row, chip=a, core=b)
                total = row if total is None else total + row
        terms = [total] + [self.swap(total, rep=j) for j in range(1, reps)]
        while len(terms) > 1:
            terms = [terms[i] + terms[i + 1] for i in range(0, len(terms), 2)]
        return terms[0]


def shards(
    chips,
    reps,
    tokens,
    cotangent,
    seq_lengths,
    dealing,
    attention_gain,
    attention_shift,
    input_weight,
    query_bias,
    value_bias,
    output_weight,
    output_bias,
    feed_gain,
    feed_shift,
    up_weight,
    up_bias,
    down_weight,
    down_bias,
):
    links = Links(chips, reps)
    core, chip = links.core, links.chip
    micro, tok_rows, width = tokens.shape
    shard_count = 2 * chips
    own_rows = micro * tok_rows
    blocks = 2 * tok_rows // BLOCK

    def own_of(values):
        return pick(values.reshape(micro, 2, tok_rows, -1), core, 1).reshape(own_rows, -1)

    def other_of(values):
        return pick(values.reshape(micro, 2, tok_rows, -1), 1 - core, 1).reshape(own_rows, -1)

    def pair_rows(own):
        came = links.swap(own, core=1)
        shape = (micro, 1, tok_rows, own.shape[-1])
        return links.by_core(own.reshape(shape), came.reshape(shape), 1).reshape(2 * own_rows, -1)

    def pair_sum(partial_values):
        return own_of(partial_values) + links.swap(other_of(partial_values), core=1)

    vectors = (
        attention_gain,
        attention_shift,
        query_bias,
        value_bias,
        output_bias,
        feed_gain,
        feed_shift,
        down_bias,
        up_bias,
    )
    lengths = [member.shape[0] for member in vectors]
    table = links.gather_vectors(jnp.concatenate(vectors)).astype(F32)
    wholes, at = [], 0
    for length in lengths:
        wholes.append(table[:, at : at + length])
        at += length

    def whole(index):
        return wholes[index].reshape(1, -1)

    def core_part(index):
        return pick(wholes[index].reshape(chips, 2, -1), core, 1).reshape(1, -1)

    input_part = links.gather(links.halves(input_weight, 3))
    output_part = links.gather(output_weight)
    up_part = links.gather(links.halves(up_weight, 1))
    down_part = links.gather(down_weight)

    inputs = tokens.reshape(own_rows, width).astype(F32)
    unit_one, inverse_one = normalize(inputs)
    normed = (unit_one * whole(0) + whole(1)).astype(LOW)
    chip_normed = pair_rows(normed)
    tail = chip_normed.reshape(micro, 2 * tok_rows, width)[:, 2 * tok_rows - BLOCK :]
    halo = links.shift(tail.reshape(micro * BLOCK, width), 1)
    all_normed = jnp.concatenate([chip_normed, halo], axis=0)
    down_low = pair_rows(cotangent.reshape(own_rows, width))
    first = chip * 2 * tok_rows
    starts = jnp.stack(
        [
            sequence_starts(seq_lengths[m, 0], dealing[m, 0], first, 2 * tok_rows)
            for m in range(micro)
        ]
    )
    block_first = first + jnp.arange(2 * tok_rows, dtype=jnp.int32) // BLOCK * BLOCK - BLOCK
    starts = (starts - block_first[None, :]).reshape(2 * own_rows, 1)

    half = width // 2
    bias = jnp.concatenate([core_part(2), jnp.zeros((1, half), F32), core_part(3)], axis=1)
    mixed = (dot(all_normed, input_part) + bias).astype(LOW)
    branch = attention(mixed, starts, blocks)
    middle = inputs + pair_sum(dot(branch, output_part)) + whole(4)
    unit_two, inverse_two = normalize(middle)
    normed_two = pair_rows((unit_two * whole(5) + whole(6)).astype(LOW))
    hidden = dot(normed_two, up_part) + core_part(8)
    activated, gelu_back = jax.vjp(gelu_tanh, hidden)
    activated = activated.astype(LOW)
    down_grad = links.reduce(rows_dot(activated, down_low)).astype(F32)
    result = middle + pair_sum(dot(activated, down_part)) + whole(7)

    upstream = cotangent.reshape(own_rows, width).astype(F32)
    (hidden_grad,) = gelu_back(back_dot(down_low, down_part))
    hidden_low = hidden_grad.astype(LOW)
    up_grad = links.unhalves(links.reduce(rows_dot(normed_two, hidden_low)), 1).astype(F32)
    upper_two = pair_sum(back_dot(hidden_low, up_part))
    middle_grad = upstream + normalize_back(upper_two, whole(5), unit_two, inverse_two)
    output_own = middle_grad.astype(LOW)
    output_low = pair_rows(output_own)
    output_grad = links.reduce(rows_dot(branch, output_low)).astype(F32)
    attended = back_dot(output_low, output_part).astype(LOW)
    mixed_grad = attention_back(mixed, starts, attended, blocks)
    input_weight_grad = links.unhalves(links.reduce(rows_dot(all_normed, mixed_grad)), 3).astype(F32)
    back_halo = links.shift(mixed_grad[2 * own_rows :, half:], -1)
    body = mixed_grad[: 2 * own_rows].reshape(micro, 2 * tok_rows, 3 * half)
    tail_grad = body[:, 2 * tok_rows - BLOCK :, half:].astype(F32) + back_halo.reshape(
        micro, BLOCK, width
    ).astype(F32)
    body = body.at[:, 2 * tok_rows - BLOCK :, half:].set(tail_grad.astype(LOW))
    upper_one = pair_sum(back_dot(body.reshape(2 * own_rows, 3 * half), input_part))
    input_grad = middle_grad + normalize_back(upper_one, whole(0), unit_one, inverse_one)

    def by_shard(values):
        return values.reshape(shard_count, -1)

    def by_core_shard(values):
        spread = values.reshape(chips, 1, -1)
        mask = jnp.arange(2, dtype=jnp.int32)[None, :, None] == core
        return jnp.where(mask, spread, 0.0).reshape(shard_count, -1)

    def column_sum(values):
        return jnp.sum(values.astype(F32), axis=0)

    packed = jnp.concatenate(
        [
            by_shard(column_sum(upper_one * unit_one)),
            by_shard(column_sum(upper_one)),
            by_core_shard(column_sum(mixed_grad[:, :half])),
            by_core_shard(column_sum(mixed_grad[:, width:])),
            by_shard(column_sum(output_own)),
            by_shard(column_sum(upper_two * unit_two)),
            by_shard(column_sum(upper_two)),
            by_shard(column_sum(upstream)),
            by_core_shard(column_sum(hidden_low)),
        ],
        axis=1,
    )
    sums = links.reduce_vectors(packed)
    vector_grads, at = [], 0
    for length in lengths:
        vector_grads.append(sums[at : at + length])
        at += length
    return (
        result.astype(LOW).reshape(tokens.shape),
        input_grad.astype(LOW).reshape(tokens.shape),
        vector_grads[0],
        vector_grads[1],
        input_weight_grad,
        vector_grads[2],
        vector_grads[3],
        output_grad,
        vector_grads[4],
        vector_grads[5],
        vector_grads[6],
        up_grad,
        vector_grads[8],
        down_grad,
        vector_grads[7],
    )


def solution(mesh):
    rows_spec = P(None, ("shard", "rep"), None)
    vector, matrix = P("shard"), P("shard", None)
    weight_specs = (
        vector,
        vector,
        matrix,
        vector,
        vector,
        matrix,
        vector,
        vector,
        vector,
        matrix,
        vector,
        matrix,
        vector,
    )
    return jax.shard_map(
        partial(shards, mesh.shape["shard"] // 2, mesh.shape["rep"]),
        mesh=mesh,
        in_specs=(rows_spec, rows_spec, P(None, "rep", None, None), P(None, "rep", None))
        + weight_specs,
        out_specs=(rows_spec, rows_spec) + weight_specs,
        check_vma=False,
    )
```

time: 1310 us -> 556 us (0.42)
  waiting for transfers between devices: 913 us -> 221 us
  blocking collectives: 138 us -> 0 us
  starting transfers between devices: 0.92 us -> 103 us
  matrix products: 152 us -> 61.8 us
  Pallas kernels: 0 us -> 41.8 us
  other arithmetic: 22.4 us -> 57.2 us
  between operations: 17.1 us -> 3.52 us
    reduce_scatter x4 -> x0, waiting for transfers between devices: 403 us -> none  [shards(): totals = lax.psum_scatter(totals, 'shard', scatter_dimension=0, tiled=True)]
    all_gather x8 -> x0, waiting for transfers between devices: 376 us -> none  [the longest x1 74.4 us: shards(): lax.all_gather(jnp.stack(input_grads), 'shard', axis=1, tiled=True)]
    ppermute x0 -> x100, waiting for transfers between devices: none -> 221 us  [the longest x98 211 us: swap(): return lax.ppermute(values, AXES, pairs)]
    psum x1 -> x0, waiting for transfers between devices: 131 us -> none  [shards(): totals = lax.psum(totals, 'rep')]
    ppermute x0 -> x100, starting transfers between devices: none -> 103 us  [the longest x98 100 us: swap(): return lax.ppermute(values, AXES, pairs)]
    all_gather x9 -> x0, blocking collectives: 98.9 us -> none  [the longest x1 14 us: shards(): lax.all_gather(weights[10], 'shard', axis=0, tiled=True)]
    pallas_call x0 -> x2, Pallas kernels: none -> 41.8 us  [the longest x1 33 us: attention_back(): pl.pallas_call(partial(attention_back_kernel, blocks, width), out_shape=j...]
    dot_general x20 -> x4, matrix products: 56.9 us -> 16.2 us  [dot(): return jnp.dot(left, right, preferred_element_type=F32)]
  transfers between devices with their start and end apart: 13 -> 100, of which waited for: 11 -> 46; matrix products, arithmetic and copies ran while one was open for 14% -> 21% of each run, Pallas kernels for 0% -> 2%
where the time goes in v1:
time: 556 us; the launch traced here: 547 us
  waiting for transfers between devices  221 us (40%)
  starting transfers between devices  103 us (19%)
  matrix products  61.8 us (11%)
  local copies, waits for them, and re-layouts  57.7 us (10%)
  other arithmetic  57.2 us (10%)
  Pallas kernels  41.8 us (8%)
    ppermute x98, waiting for transfers between devices, swap(): return lax.ppermute(values, AXES, pairs)  211 us
    ppermute x98, starting transfers between devices, swap(): return lax.ppermute(values, AXES, pairs)  100 us
    pallas_call x1, Pallas kernels, attention_back(): pl.pallas_call(partial(attention_back_kernel, blocks, width), out_shape=j...  33 us
    dot_general x4, matrix products, back_dot(): lax.dot_general(left, right, (((1,), (1,)), ((), ())), preferred_element_...  24.6 us
    unnamed x202, local copies, waits for them, and re-layouts  21 us
    dot_general x4, matrix products, rows_dot(): lax.dot_general(left, right, (((0,), (0,)), ((), ())), preferred_element_...  20.9 us
    dynamic_slice x16, local copies, waits for them, and re-layouts, pick(): return lax.dynamic_index_in_dim(stacked, index, axis, keepdims=False)  20.4 us
    dot_general x4, matrix products, dot(): return jnp.dot(left, right, preferred_element_type=F32)  16.2 us
  transfers between devices with their start and end apart: 100, of which 46 were waited for; matrix products, arithmetic and copies ran while one was open for 21% of the time, Pallas kernels for 2%

profile of v1, /device:TPU:0, one launch (start us, length us, event | category | flops | bytes accessed | tf_op | source)
XLA Modules:
  0.0 546.7 jit_solution(15020706483039573285)
XLA Ops:
  2.4 5.1 collective-permute-start.16
  53.7 4.2 collective-permute-done.18
  58.4 3.8 collective-permute-done.32
  90.1 14.9 %collective-permute-done.8 = bf16[64,1536]{1,0:T(8,128)(2,1)S(1)} collective-permute-done((bf16[64,1536]{1,0:T(8,128)(2,1)}, bf16[64,1536]{1,0:T(8,128)(2,1)S(1)}, u32[]{:S(2)}, u32[]{:S(2)}) %collective-permute-start.8) | collective-permute-done | bytes 196640 | tf_op jit(solution)/shard_map/ppermute | solution.py:211
  109.7 7.7 %collective-permute-done.25 = bf16[64,2048]{1,0:T(8,128)(2,1)S(1)} collective-permute-done((bf16[64,2048]{1,0:T(8,128)(2,1)S(1)}, bf16[64,2048]{1,0:T(8,128)(2,1)S(1)}, u32[]{:S(2)}, u32[]{:S(2)}) %collective-permute-start.25) | collective-permute-done | bytes 262176 | tf_op jit(solution)/shard_map/ppermute | solution.py:211
  123.7 14.1 %collective-permute-done.34 = bf16[3,128,1024]{2,1,0:T(8,128)(2,1)S(1)} collective-permute-done((bf16[3,128,1024]{2,1,0:T(8,128)(2,1)S(1)}, bf16[3,128,1024]{2,1,0:T(8,128)(2,1)S(1)}, u32[]{:S(2)}, u32[]{:S(2)}) %collective-permute-start.34) | collective-permute-done | bytes 786464 | tf_op jit(solution)/shard_map/ppermute | solution.py:211
  143.8 6.6 %collective-permute-done.10 = bf16[3,64,1536]{2,1,0:T(8,128)(2,1)S(1)} collective-permute-done((bf16[3,64,1536]{2,1,0:T(8,128)(2,1)S(1)}, bf16[3,64,1536]{2,1,0:T(8,128)(2,1)S(1)}, u32[]{:S(2)}, u32[]{:S(2)}) %collective-permute-start.10) | collective-permute-done | bytes 589856 | tf_op jit(solution)/shard_map/ppermute | solution.py:211
  152.1 21.1 %collective-permute-done.37 = bf16[3,64,1024]{2,1,0:T(8,128)(2,1)S(1)} collective-permute-done((bf16[3,64,1024]{2,1,0:T(8,128)(2,1)S(1)}, bf16[3,64,1024]{2,1,0:T(8,128)(2,1)S(1)}, u32[]{:S(2)}, u32[]{:S(2)}) %collective-permute-start.37) | collective-permute-done | bytes 393248 | tf_op jit(solution)/shard_map/ppermute | solution.py:211
  184.6 5.0 fusion.7.mixed_ref
  189.7 8.8 %shard_map.280 = bf16[1024,512]{1,0:T(8,128)(2,1)S(1)} custom-call(bf16[1280,1536]{1,0:T(8,128)(2,1)S(1)} %fusion.7.mixed_ref, s32[1024,1]{1,0:T(8,128)S(1)} %bitcast.530), custom_call_target="tpu_custom_call" | custom-call | flops 1073741824 | bytes 8388608 | tf_op jit(solution)/shard_map/pallas_call | solution.py:166
  209.2 4.5 fusion.98
  213.8 5.4 fusion.79
  219.2 13.6 %convert_reduce_fusion = (f32[2048]{0:T(1024)S(1)}, bf16[1024,2048]{1,0:T(8,128)(2,1)}) fusion(f32[1024,2048]{1,0:T(8,128)} %copy-done.59, f32[2048]{0:T(1024)S(1)} %bitcast.636, bf16[1024,1024]{1,0:T(8,128)(2,1)S(1)} %bitcast.564, bf16[2048,1024]{1,0:T(8,128)(2,1)S(1)} %bitcast_dynamic-update-slice_fusion), kind=kOutput, calls=%fused_computation.10 | convolution fusion | flops 4343199744 | bytes 18890752 | tf_op jit(solution)/shard_map/dot_general | solution.py:28
  232.8 10.0 %convolution_convert_fusion = bf16[2048,1024]{1,0:T(8,128)(2,1)S(1)} fusion(bf16[1024,1024]{1,0:T(8,128)(2,1)S(1)} %bitcast.565, f32[1024,2048]{1,0:T(8,128)} %copy-done.59, f32[2048]{0:T(1024)S(1)} %bitcast.637), kind=kOutput, calls=%fused_computation.15 | convolution fusion | flops 4318035968 | bytes 14688256 | tf_op jit(solution)/shard_map/dot_general | solution.py:24
  242.8 5.1 convolution_convert_fusion.1
  250.1 6.3 %fusion.99 = f32[1024,1024]{1,0:T(8,128)S(1)} fusion(bf16[1024,2048]{1,0:T(8,128)(2,1)} %get-tuple-element.101, bf16[1024,2048]{1,0:T(8,128)(2,1)S(1)} %bitcast_dynamic-update-slice_fusion.16), kind=kOutput, calls=%fused_computation.414 | convolution fusion | flops 4294967296 | bytes 12582912 | tf_op jit(solution)/shard_map/dot_general | solution.py:28
  264.4 6.9 %collective-permute-done.77 = bf16[4,32,2048]{2,1,0:T(8,128)(2,1)S(1)} collective-permute-done((bf16[4,32,2048]{2,1,0:T(8,128)(2,1)S(1)}, bf16[4,32,2048]{2,1,0:T(8,128)(2,1)S(1)}, u32[]{:S(2)}, u32[]{:S(2)}) %collective-permute-start.77) | collective-permute-done | bytes 524320 | tf_op jit(solution)/shard_map/ppermute | solution.py:211
  275.7 6.8 %collective-permute-done.89 = bf16[4,64,1024]{2,1,0:T(8,128)(2,1)S(1)} collective-permute-done((bf16[4,64,1024]{2,1,0:T(8,128)(2,1)S(1)}, bf16[4,64,1024]{2,1,0:T(8,128)(2,1)S(1)}, u32[]{:S(2)}, u32[]{:S(2)}) %collective-permute-start.89) | collective-permute-done | bytes 524320 | tf_op jit(solution)/shard_map/ppermute | solution.py:211
  287.9 17.1 %collective-permute-done.80 = bf16[4,64,2048]{2,1,0:T(8,128)(2,1)S(1)} collective-permute-done((bf16[4,64,2048]{2,1,0:T(8,128)(2,1)S(1)}, bf16[4,64,2048]{2,1,0:T(8,128)(2,1)S(1)}, u32[]{:S(2)}, u32[]{:S(2)}) %collective-permute-start.80) | collective-permute-done | bytes 1048608 | tf_op jit(solution)/shard_map/ppermute | solution.py:211
  307.1 19.3 %collective-permute-done.92 = bf16[4,128,1024]{2,1,0:T(8,128)(2,1)S(1)} collective-permute-done((bf16[4,128,1024]{2,1,0:T(8,128)(2,1)S(1)}, bf16[4,128,1024]{2,1,0:T(8,128)(2,1)S(1)}, u32[]{:S(2)}, u32[]{:S(2)}) %collective-permute-start.92) | collective-permute-done | bytes 1048608 | tf_op jit(solution)/shard_map/ppermute | solution.py:211
  333.0 7.7 %collective-permute-done.82 = bf16[64,2048]{1,0:T(8,128)(2,1)S(1)} collective-permute-done((bf16[64,2048]{1,0:T(8,128)(2,1)S(1)}, bf16[64,2048]{1,0:T(8,128)(2,1)S(1)}, u32[]{:S(2)}, u32[]{:S(2)}) %collective-permute-start.82) | collective-permute-done | bytes 262176 | tf_op jit(solution)/shard_map/ppermute | solution.py:211
  340.6 4.0 collective-permute-done.81
  346.7 14.6 %collective-permute-done.94 = bf16[128,1024]{1,0:T(8,128)(2,1)S(1)} collective-permute-done((bf16[128,1024]{1,0:T(8,128)(2,1)S(1)}, bf16[128,1024]{1,0:T(8,128)(2,1)S(1)}, u32[]{:S(2)}, u32[]{:S(2)}) %collective-permute-start.94) | collective-permute-done | bytes 262176 | tf_op jit(solution)/shard_map/ppermute | solution.py:211
  366.6 4.0 collective-permute-done.84
  373.1 3.9 multiply_reduce_fusion
  377.0 4.0 convert_reduce_fusion.5
  407.3 33.0 %shard_map.281 = bf16[1280,1536]{1,0:T(8,128)(2,1)S(1)} custom-call(bf16[1280,1536]{1,0:T(8,128)(2,1)S(1)} %copy-done.2, s32[1024,1]{1,0:T(8,128)S(1)} %bitcast.531, bf16[1024,512]{1,0:T(8,128)(2,1)S(1)} %convolution_convert_fusion.4.upper_ref), custom_call_target="tpu_custom_call" | custom-call | flops 2684354560 | bytes 16777216 | tf_op jit(solution)/shard_map/pallas_call | solution.py:182
  440.4 4.5 convolution_convert_fusion.2
  452.7 9.6 %collective-permute-done.66 = bf16[4,16,1024]{2,1,0:T(8,128)(2,1)S(1)} collective-permute-done((bf16[4,16,1024]{2,1,0:T(8,128)(2,1)S(1)}, bf16[4,16,1024]{2,1,0:T(8,128)(2,1)S(1)}, u32[]{:S(2)}, u32[]{:S(2)}) %collective-permute-start.66) | collective-permute-done | bytes 131104 | tf_op jit(solution)/shard_map/ppermute | solution.py:211
  467.8 3.7 collective-permute-done.67
  487.1 10.5 %collective-permute-done.42 = bf16[256,1024]{1,0:T(8,128)(2,1)S(1)} collective-permute-done((bf16[256,1024]{1,0:T(8,128)(2,1)S(1)}, bf16[256,1024]{1,0:T(8,128)(2,1)S(1)}, u32[]{:S(2)}, u32[]{:S(2)}) %collective-permute-start.42) | collective-permute-done | bytes 524320 | tf_op jit(solution)/shard_map/ppermute | solution.py:221
  531.6 3.7 collective-permute-start.47
  (590 shorter events, 253.4 us)
Async XLA Ops:
  2.4 45.7 %collective-permute-start.16 = (bf16[32,1024]{1,0:T(8,128)(2,1)}, bf16[32,1024]{1,0:T(8,128)(2,1)S(1)}, u32[]{:S(2)}, u32[]{:S(2)}) collective-permute-start(bf16[32,1024]{1,0:T(8,128)(2,1)} %bitcast.55), channel_id=1, source_target_pairs={{0,24},{1,25},{2,26},{3,27},{4,28},{5,29},{6,30},{7,31},{8,16},{9,... | collective-permute-start | bytes 196616 | tf_op jit(solution)/shard_map/ppermute | solution.py:211
  7.5 42.1 %collective-permute-start.15 = (bf16[32,1024]{1,0:T(8,128)(2,1)}, bf16[32,1024]{1,0:T(8,128)(2,1)S(1)}, u32[]{:S(2)}, u32[]{:S(2)}) collective-permute-start(bf16[32,1024]{1,0:T(8,128)(2,1)} %bitcast.55), channel_id=1, source_target_pairs={{0,16},{1,17},{2,18},{3,19},{4,20},{5,21},{6,22},{7,23},{8,24},{9,... | collective-permute-start | bytes 196616 | tf_op jit(solution)/shard_map/ppermute | solution.py:211
  36.9 21.0 %collective-permute-start.33 = (bf16[128,1024]{1,0:T(8,128)(2,1)}, bf16[128,1024]{1,0:T(8,128)(2,1)S(1)}, u32[]{:S(2)}, u32[]{:S(2)}) collective-permute-start(bf16[128,1024]{1,0:T(8,128)(2,1)} %bitcast.573), channel_id=1, source_target_pairs={{0,24},{1,25},{2,26},{3,27},{4,28},{5,29},{6,30},{7,31},{8,16},{9,... | collective-permute-start | bytes 786440 | tf_op jit(solution)/shard_map/ppermute | solution.py:211
  38.8 23.4 %collective-permute-start.32 = (bf16[128,1024]{1,0:T(8,128)(2,1)}, bf16[128,1024]{1,0:T(8,128)(2,1)S(1)}, u32[]{:S(2)}, u32[]{:S(2)}) collective-permute-start(bf16[128,1024]{1,0:T(8,128)(2,1)} %bitcast.574), channel_id=1, source_target_pairs={{0,16},{1,17},{2,18},{3,19},{4,20},{5,21},{6,22},{7,23},{8,24},{9,... | collective-permute-start | bytes 786440 | tf_op jit(solution)/shard_map/ppermute | solution.py:211
  49.6 24.7 %collective-permute-start.6 = (bf16[128,1536]{0,1:T(8,128)(2,1)}, bf16[128,1536]{0,1:T(8,128)(2,1)S(1)}, u32[]{:S(2)}, u32[]{:S(2)}) collective-permute-start(bf16[128,1536]{0,1:T(8,128)(2,1)} %bitcast.607), channel_id=1, source_target_pairs={{0,4},{1,5},{2,6},{3,7},{4,0},{5,1},{6,2},{7,3},{8,12},{9,13},{10,... | collective-permute-start | bytes 1179656 | tf_op jit(solution)/shard_map/ppermute | solution.py:211
  57.8 21.8 %collective-permute-start.23 = (bf16[128,2048]{0,1:T(8,128)(2,1)}, bf16[128,2048]{0,1:T(8,128)(2,1)}, u32[]{:S(2)}, u32[]{:S(2)}) collective-permute-start(bf16[128,2048]{0,1:T(8,128)(2,1)} %bitcast.90), channel_id=1, source_target_pairs={{0,4},{1,5},{2,6},{3,7},{4,0},{5,1},{6,2},{7,3},{8,12},{9,13},{10,... | collective-permute-start | bytes 1572872 | tf_op jit(solution)/shard_map/ppermute | solution.py:211
  57.9 62.6 %collective-permute-start.39 = (bf16[512,1024]{1,0:T(8,128)(2,1)S(1)}, bf16[512,1024]{1,0:T(8,128)(2,1)}, u32[]{:S(2)}, u32[]{:S(2)}) collective-permute-start(bf16[512,1024]{1,0:T(8,128)(2,1)S(1)} %bitcast.532), channel_id=1, source_target_pairs={{0,4},{1,5},{2,6},{3,7},{4,0},{5,1},{6,2},{7,3},{8,12},{9,13},{10,... | collective-permute-start | bytes 3145736 | tf_op jit(solution)/shard_map/ppermute | solution.py:211
  70.7 68.9 %collective-permute-start.4 = (bf16[512,1024]{1,0:T(8,128)(2,1)}, bf16[512,1024]{1,0:T(8,128)(2,1)}, u32[]{:S(2)}, u32[]{:S(2)}) collective-permute-start(bf16[512,1024]{1,0:T(8,128)(2,1)} %fusion.29), channel_id=1, source_target_pairs={{0,4},{1,5},{2,6},{3,7},{4,0},{5,1},{6,2},{7,3},{8,12},{9,13},{10,... | collective-permute-start | bytes 3145736 | tf_op jit(solution)/shard_map/ppermute | solution.py:211
  79.6 25.3 %collective-permute-start.8 = (bf16[64,1536]{1,0:T(8,128)(2,1)}, bf16[64,1536]{1,0:T(8,128)(2,1)S(1)}, u32[]{:S(2)}, u32[]{:S(2)}) collective-permute-start(bf16[64,1536]{1,0:T(8,128)(2,1)} %bitcast.22), channel_id=1, source_target_pairs={{0,16},{1,17},{2,18},{3,19},{4,20},{5,21},{6,22},{7,23},{8,24},{9,... | collective-permute-start | bytes 589832 | tf_op jit(solution)/shard_map/ppermute | solution.py:211
  79.6 25.3 %collective-permute-start.7 = (bf16[64,1536]{1,0:T(8,128)(2,1)}, bf16[64,1536]{1,0:T(8,128)(2,1)S(1)}, u32[]{:S(2)}, u32[]{:S(2)}) collective-permute-start(bf16[64,1536]{1,0:T(8,128)(2,1)} %bitcast.22), channel_id=1, source_target_pairs={{0,8},{1,9},{2,10},{3,11},{4,12},{5,13},{6,14},{7,15},{8,0},{9,1},... | collective-permute-start | bytes 589832 | tf_op jit(solution)/shard_map/ppermute | solution.py:211
  117.4 20.4 %collective-permute-start.34 = (bf16[3,128,1024]{2,1,0:T(8,128)(2,1)S(1)}, bf16[3,128,1024]{2,1,0:T(8,128)(2,1)S(1)}, u32[]{:S(2)}, u32[]{:S(2)}) collective-permute-start(bf16[3,128,1024]{2,1,0:T(8,128)(2,1)S(1)} %copy-done.21), channel_id=1, source_target_pairs={{0,1},{1,0},{2,3},{3,2},{4,5},{5,4},{6,7},{7,6},{8,9},{9,8},{10,11... | collective-permute-start | bytes 2359304 | tf_op jit(solution)/shard_map/ppermute | solution.py:211
  118.9 23.5 %collective-permute-start.11 = (bf16[3,64,1536]{2,1,0:T(8,128)(2,1)S(1)}, bf16[3,64,1536]{2,1,0:T(8,128)(2,1)S(1)}, u32[]{:S(2)}, u32[]{:S(2)}) collective-permute-start(bf16[3,64,1536]{2,1,0:T(8,128)(2,1)S(1)} %pad_maximum_fusion.26), channel_id=1, source_target_pairs={{0,2},{1,3},{2,0},{3,1},{4,6},{5,7},{6,4},{7,5},{8,10},{9,11},{10,... | collective-permute-start | bytes 1769480 | tf_op jit(solution)/shard_map/ppermute | solution.py:211
  120.5 30.0 %collective-permute-start.10 = (bf16[3,64,1536]{2,1,0:T(8,128)(2,1)S(1)}, bf16[3,64,1536]{2,1,0:T(8,128)(2,1)S(1)}, u32[]{:S(2)}, u32[]{:S(2)}) collective-permute-start(bf16[3,64,1536]{2,1,0:T(8,128)(2,1)S(1)} %pad_maximum_fusion.26), channel_id=1, source_target_pairs={{0,1},{1,0},{2,3},{3,2},{4,5},{5,4},{6,7},{7,6},{8,9},{9,8},{10,11... | collective-permute-start | bytes 1769480 | tf_op jit(solution)/shard_map/ppermute | solution.py:211
  122.9 59.7 %collective-permute-start.28 = (bf16[3,64,2048]{2,1,0:T(8,128)(2,1)S(1)}, bf16[3,64,2048]{2,1,0:T(8,128)(2,1)S(1)}, u32[]{:S(2)}, u32[]{:S(2)}) collective-permute-start(bf16[3,64,2048]{2,1,0:T(8,128)(2,1)S(1)} %pad_maximum_fusion.20), channel_id=1, source_target_pairs={{0,2},{1,3},{2,0},{3,1},{4,6},{5,7},{6,4},{7,5},{8,10},{9,11},{10,... | collective-permute-start | bytes 2359304 | tf_op jit(solution)/shard_map/ppermute | solution.py:211
  137.8 45.4 %collective-permute-start.27 = (bf16[3,64,2048]{2,1,0:T(8,128)(2,1)S(1)}, bf16[3,64,2048]{2,1,0:T(8,128)(2,1)S(1)}, u32[]{:S(2)}, u32[]{:S(2)}) collective-permute-start(bf16[3,64,2048]{2,1,0:T(8,128)(2,1)S(1)} %pad_maximum_fusion.20), channel_id=1, source_target_pairs={{0,1},{1,0},{2,3},{3,2},{4,5},{5,4},{6,7},{7,6},{8,9},{9,8},{10,11... | collective-permute-start | bytes 2359304 | tf_op jit(solution)/shard_map/ppermute | solution.py:211
  139.6 33.7 %collective-permute-start.37 = (bf16[3,64,1024]{2,1,0:T(8,128)(2,1)S(1)}, bf16[3,64,1024]{2,1,0:T(8,128)(2,1)S(1)}, u32[]{:S(2)}, u32[]{:S(2)}) collective-permute-start(bf16[3,64,1024]{2,1,0:T(8,128)(2,1)S(1)} %slice.308), channel_id=1, source_target_pairs={{0,1},{1,0},{2,3},{3,2},{4,5},{5,4},{6,7},{7,6},{8,9},{9,8},{10,11... | collective-permute-start | bytes 1179656 | tf_op jit(solution)/shard_map/ppermute | solution.py:211
  142.4 32.3 %collective-permute-start.36 = (bf16[3,64,1024]{2,1,0:T(8,128)(2,1)S(1)}, bf16[3,64,1024]{2,1,0:T(8,128)(2,1)S(1)}, u32[]{:S(2)}, u32[]{:S(2)}) collective-permute-start(bf16[3,64,1024]{2,1,0:T(8,128)(2,1)S(1)} %slice.307), channel_id=1, source_target_pairs={{0,2},{1,3},{2,0},{3,1},{4,6},{5,7},{6,4},{7,5},{8,10},{9,11},{10,... | collective-permute-start | bytes 1179656 | tf_op jit(solution)/shard_map/ppermute | solution.py:211
  150.4 34.1 %collective-permute-start.5 = (bf16[256,1024]{1,0:T(8,128)(2,1)S(1)}, bf16[256,1024]{1,0:T(8,128)(2,1)S(1)}, u32[]{:S(2)}, u32[]{:S(2)}) collective-permute-start(bf16[256,1024]{1,0:T(8,128)(2,1)S(1)} %bitcast.604), channel_id=1, source_target_pairs={{0,8},{1,9},{2,10},{3,11},{4,12},{5,13},{6,14},{7,15},{8,16},{9,17... | collective-permute-start | bytes 1572872 | tf_op jit(solution)/shard_map/ppermute | solution.py:221
  258.5 24.0 %collective-permute-start.89 = (bf16[4,64,1024]{2,1,0:T(8,128)(2,1)S(1)}, bf16[4,64,1024]{2,1,0:T(8,128)(2,1)S(1)}, u32[]{:S(2)}, u32[]{:S(2)}) collective-permute-start(bf16[4,64,1024]{2,1,0:T(8,128)(2,1)S(1)} %get-tuple-element.142), channel_id=1, source_target_pairs={{0,2},{1,3},{2,0},{3,1},{4,6},{5,7},{6,4},{7,5},{8,10},{9,11},{10,... | collective-permute-start | bytes 1572872 | tf_op jit(solution)/shard_map/ppermute | solution.py:211
  263.4 41.6 %collective-permute-start.80 = (bf16[4,64,2048]{2,1,0:T(8,128)(2,1)S(1)}, bf16[4,64,2048]{2,1,0:T(8,128)(2,1)S(1)}, u32[]{:S(2)}, u32[]{:S(2)}) collective-permute-start(bf16[4,64,2048]{2,1,0:T(8,128)(2,1)S(1)} %pad_maximum_fusion.13), channel_id=1, source_target_pairs={{0,2},{1,3},{2,0},{3,1},{4,6},{5,7},{6,4},{7,5},{8,10},{9,11},{10,... | collective-permute-start | bytes 3145736 | tf_op jit(solution)/shard_map/ppermute | solution.py:211
  271.5 33.5 %collective-permute-start.78 = (bf16[4,64,2048]{2,1,0:T(8,128)(2,1)S(1)}, bf16[4,64,2048]{2,1,0:T(8,128)(2,1)S(1)}, u32[]{:S(2)}, u32[]{:S(2)}) collective-permute-start(bf16[4,64,2048]{2,1,0:T(8,128)(2,1)S(1)} %pad_maximum_fusion.12), channel_id=1, source_target_pairs={{0,1},{1,0},{2,3},{3,2},{4,5},{5,4},{6,7},{7,6},{8,9},{9,8},{10,11... | collective-permute-start | bytes 3145736 | tf_op jit(solution)/shard_map/ppermute | solution.py:211
  274.7 51.7 %collective-permute-start.92 = (bf16[4,128,1024]{2,1,0:T(8,128)(2,1)S(1)}, bf16[4,128,1024]{2,1,0:T(8,128)(2,1)S(1)}, u32[]{:S(2)}, u32[]{:S(2)}) collective-permute-start(bf16[4,128,1024]{2,1,0:T(8,128)(2,1)S(1)} %pad_maximum_fusion.17), channel_id=1, source_target_pairs={{0,2},{1,3},{2,0},{3,1},{4,6},{5,7},{6,4},{7,5},{8,10},{9,11},{10,... | collective-permute-start | bytes 3145736 | tf_op jit(solution)/shard_map/ppermute | solution.py:211
  282.8 43.6 %collective-permute-start.90 = (bf16[4,128,1024]{2,1,0:T(8,128)(2,1)S(1)}, bf16[4,128,1024]{2,1,0:T(8,128)(2,1)S(1)}, u32[]{:S(2)}, u32[]{:S(2)}) collective-permute-start(bf16[4,128,1024]{2,1,0:T(8,128)(2,1)S(1)} %pad_maximum_fusion.16), channel_id=1, source_target_pairs={{0,1},{1,0},{2,3},{3,2},{4,5},{5,4},{6,7},{7,6},{8,9},{9,8},{10,11... | collective-permute-start | bytes 3145736 | tf_op jit(solution)/shard_map/ppermute | solution.py:211
  285.6 86.4 %collective-permute-start.40 = (f32[512,1024]{1,0:T(8,128)}, f32[512,1024]{1,0:T(8,128)}, u32[]{:S(2)}, u32[]{:S(2)}) collective-permute-start(f32[512,1024]{1,0:T(8,128)} %bitcast.154), channel_id=1, source_target_pairs={{0,4},{1,5},{2,6},{3,7},{4,0},{5,1},{6,2},{7,3},{8,12},{9,13},{10,... | collective-permute-start | bytes 6291464 | tf_op jit(solution)/shard_map/ppermute | solution.py:211
  305.0 72.0 %collective-permute-start.38 = (f32[512,1024]{1,0:T(8,128)}, f32[512,1024]{1,0:T(8,128)}, u32[]{:S(2)}, u32[]{:S(2)}) collective-permute-start(f32[512,1024]{1,0:T(8,128)} %bitcast.144), channel_id=1, source_target_pairs={{0,4},{1,5},{2,6},{3,7},{4,0},{5,1},{6,2},{7,3},{8,12},{9,13},{10,... | collective-permute-start | bytes 6291464 | tf_op jit(solution)/shard_map/ppermute | solution.py:211
  305.7 24.7 %collective-permute-start.83 = (bf16[64,2048]{1,0:T(8,128)(2,1)S(1)}, bf16[64,2048]{1,0:T(8,128)(2,1)S(1)}, u32[]{:S(2)}, u32[]{:S(2)}) collective-permute-start(bf16[64,2048]{1,0:T(8,128)(2,1)S(1)} %get-tuple-element.153), channel_id=1, source_target_pairs={{0,24},{1,25},{2,26},{3,27},{4,28},{5,29},{6,30},{7,31},{8,16},{9,... | collective-permute-start | bytes 786440 | tf_op jit(solution)/shard_map/ppermute | solution.py:211
  340.6 20.7 %collective-permute-start.94 = (bf16[128,1024]{1,0:T(8,128)(2,1)S(1)}, bf16[128,1024]{1,0:T(8,128)(2,1)S(1)}, u32[]{:S(2)}, u32[]{:S(2)}) collective-permute-start(bf16[128,1024]{1,0:T(8,128)(2,1)S(1)} %get-tuple-element.141), channel_id=1, source_target_pairs={{0,16},{1,17},{2,18},{3,19},{4,20},{5,21},{6,22},{7,23},{8,24},{9,... | collective-permute-start | bytes 786440 | tf_op jit(solution)/shard_map/ppermute | solution.py:211
  345.3 20.0 %collective-permute-start.85 = (bf16[64,2048]{1,0:T(8,128)(2,1)S(1)}, bf16[64,2048]{1,0:T(8,128)(2,1)S(1)}, u32[]{:S(2)}, u32[]{:S(2)}) collective-permute-start(bf16[64,2048]{1,0:T(8,128)(2,1)S(1)} %fusion.45), channel_id=1, source_target_pairs={{0,2},{1,3},{2,0},{3,1},{4,6},{5,7},{6,4},{7,5},{8,10},{9,11},{10,... | collective-permute-start | bytes 786440 | tf_op jit(solution)/shard_map/ppermute | solution.py:211
  381.1 19.9 %collective-permute-start.41 = (bf16[512,1024]{1,0:T(8,128)(2,1)}, bf16[512,1024]{1,0:T(8,128)(2,1)}, u32[]{:S(2)}, u32[]{:S(2)}) collective-permute-start(bf16[512,1024]{1,0:T(8,128)(2,1)} %get-tuple-element.103), channel_id=1, source_target_pairs={{0,4},{1,5},{2,6},{3,7},{4,0},{5,1},{6,2},{7,3},{8,12},{9,13},{10,... | collective-permute-start | bytes 3145736 | tf_op jit(solution)/shard_map/ppermute | solution.py:211
  462.9 20.3 %collective-permute-start.57 = (bf16[4,64,1536]{2,1,0:T(8,128)(2,1)S(1)}, bf16[4,64,1536]{2,1,0:T(8,128)(2,1)S(1)}, u32[]{:S(2)}, u32[]{:S(2)}) collective-permute-start(bf16[4,64,1536]{2,1,0:T(8,128)(2,1)S(1)} %pad_maximum_fusion.23), channel_id=1, source_target_pairs={{0,2},{1,3},{2,0},{3,1},{4,6},{5,7},{6,4},{7,5},{8,10},{9,11},{10,... | collective-permute-start | bytes 2359304 | tf_op jit(solution)/shard_map/ppermute | solution.py:211
  480.6 36.0 %collective-permute-start.74 = (bf16[32,1024]{1,0:T(8,128)(2,1)S(1)}, bf16[32,1024]{1,0:T(8,128)(2,1)S(1)}, u32[]{:S(2)}, u32[]{:S(2)}) collective-permute-start(bf16[32,1024]{1,0:T(8,128)(2,1)S(1)} %fusion.51), channel_id=1, source_target_pairs={{0,2},{1,3},{2,0},{3,1},{4,6},{5,7},{6,4},{7,5},{8,10},{9,11},{10,... | collective-permute-start | bytes 196616 | tf_op jit(solution)/shard_map/ppermute | solution.py:211
  481.8 36.0 %collective-permute-start.73 = (bf16[32,1024]{1,0:T(8,128)(2,1)S(1)}, bf16[32,1024]{1,0:T(8,128)(2,1)S(1)}, u32[]{:S(2)}, u32[]{:S(2)}) collective-permute-start(bf16[32,1024]{1,0:T(8,128)(2,1)S(1)} %fusion.51), channel_id=1, source_target_pairs={{0,1},{1,0},{2,3},{3,2},{4,5},{5,4},{6,7},{7,6},{8,9},{9,8},{10,11... | collective-permute-start | bytes 196616 | tf_op jit(solution)/shard_map/ppermute | solution.py:211
  (129 other events, 1509.7 us)

commit v2 on v1

--- a/solution.py
+++ b/solution.py
@@ -342,6 +342,427 @@
             terms = [terms[i] + terms[i + 1] for i in range(0, len(terms), 2)]
         return terms[0]
 
+class Copies:
+    def __init__(self, send, recv, links):
+        self.send, self.recv, self.links = send, recv, links
+        self.places, self.started = {}, []
+
+    def make(self, name, source, target, device):
+        place = self.places.setdefault(name, len(self.places))
+        return pltpu.make_async_remote_copy(
+            src_ref=source,
+            dst_ref=target,
+            send_sem=self.send.at[place],
+            recv_sem=self.recv.at[place],
+            device_id=device,
+            device_id_type=pl.DeviceIdType.MESH,
+        )
+
+    def start(self, name, source, target, device, when=None):
+        copy = self.make(name, source, target, device)
+        run_when(when, copy.start)
+        self.started.append((when, copy))
+
+    def arrived(self, name, target, when=None):
+        copy = self.make(name, target, target, self.links.other(x=1))
+        run_when(when, copy.wait_recv)
+
+    def finish(self):
+        for when, copy in self.started:
+            run_when(when, copy.wait_send)
+
+
+def run_when(when, body):
+    if when is None:
+        body()
+    else:
+        pl.when(when)(body)
+
+
+class Place:
+    def __init__(self, chips):
+        shard = lax.axis_index("shard")
+        self.chips, self.shard = chips, shard
+        self.chip, self.core, self.rep = shard // 2, lax.rem(shard, 2), lax.axis_index("rep")
+
+    def flipped(self, bits):
+        x, y = lax.rem(self.rep, 2), self.rep // 2
+        x = 1 - x if bits & 1 else x
+        y = 1 - y if bits & 2 else y
+        return y * 2 + x
+
+    def other(self, x=0, y=0, core=0, chip=None):
+        chip = self.chip if chip is None else chip
+        side = 1 - self.core if core else self.core
+        return {"shard": chip * 2 + side, "rep": self.flipped(x + 2 * y)}
+
+    def shard_at(self, step):
+        return lax.rem(self.shard + step, 2 * self.chips)
+
+    def greet(self, barrier_devices):
+        barrier = pltpu.get_barrier_semaphore()
+        for device in barrier_devices:
+            pl.semaphore_signal(barrier, 1, device_id=device, device_id_type=pl.DeviceIdType.MESH)
+        pl.semaphore_wait(barrier, len(barrier_devices))
+
+    def neighbours(self):
+        shards = [
+            {"shard": self.shard_at(step), "rep": self.rep} for step in range(1, 2 * self.chips)
+        ]
+        return shards + [self.other(x=1), self.other(y=1)]
+
+
+def gather_kernel(
+    chips, splits, vec_in, in_in, out_in, up_in, down_in, *refs
+):
+    table, wholes, (send, recv, local) = refs[0], refs[1:5], refs[5:]
+    shards_in = (in_in, out_in, up_in, down_in)
+    at = Place(chips)
+    copies = Copies(send, recv, at)
+    at.greet(at.neighbours())
+    own_copies = []
+
+    def keep(source, target):
+        copy = pltpu.make_async_copy(source, target, local.at[len(own_copies)])
+        copy.start()
+        own_copies.append(copy)
+
+    keep(vec_in, table.at[at.shard])
+    for step in range(1, 2 * chips):
+        copies.start(
+            ("vec", step), vec_in, table.at[at.shard], {"shard": at.shard_at(step), "rep": at.rep}
+        )
+    kept = []
+    for index, (source, whole, blocks) in enumerate(zip(shards_in, wholes, splits)):
+        rows = source.shape[0]
+        first = len(own_copies)
+        if blocks is None:
+            keep(source, whole.at[pl.ds(pl.multiple_of(at.chip * rows, rows), rows)])
+        else:
+            width = source.shape[1] // (2 * blocks)
+            place = pl.ds(pl.multiple_of(at.shard * rows, rows), rows)
+            for block in range(blocks):
+                columns = pl.ds(block * width, width)
+
+                def side(core):
+                    return pl.ds(pl.multiple_of((2 * block + core) * width, width), width)
+
+                copies.start(
+                    ("pair", index, block),
+                    source.at[:, side(1 - at.core)],
+                    whole.at[place, columns],
+                    at.other(core=1),
+                )
+                keep(source.at[:, side(at.core)], whole.at[place, columns])
+        kept.append(own_copies[first:])
+
+    def piece(index, chip, part=None):
+        whole = wholes[index]
+        rows = whole.shape[0] // chips
+        quarter = rows // 4
+        if splits[index] is None and index == 1:
+            return whole.at[pl.ds(pl.multiple_of(chip * rows, rows), rows)]
+        start, size = chip * rows + at.rep * quarter, quarter
+        if part is not None:
+            bits, piece_half = part
+            start = chip * rows + at.flipped(bits) * quarter
+            if piece_half is not None:
+                size = quarter // 2
+                start = start + piece_half * size
+        return whole.at[pl.ds(pl.multiple_of(start, size), size)]
+
+    ways = (("up", 1), ("down", -1))
+
+    def neighbour(step):
+        return at.other(chip=jnp.clip(at.chip + step, 0, chips - 1))
+
+    def can_send(step):
+        return at.chip < chips - 1 if step > 0 else at.chip > 0
+
+    def has(step, distance):
+        return at.chip >= distance if step > 0 else at.chip + distance < chips
+
+    def open_z(index):
+        for copy in kept[index]:
+            copy.wait()
+        if splits[index] is not None:
+            rows = shards_in[index].shape[0]
+            width = shards_in[index].shape[1] // (2 * splits[index])
+            place = pl.ds(pl.multiple_of((at.chip * 2 + 1 - at.core) * rows, rows), rows)
+            for block in range(splits[index]):
+                copies.arrived(
+                    ("pair", index, block), wholes[index].at[place, pl.ds(block * width, width)]
+                )
+        for name, step in ways:
+            mine = piece(index, at.chip)
+            copies.start((name, index, 1), mine, mine, neighbour(step), can_send(step))
+
+    def pass_on(index):
+        for distance in range(1, chips):
+            for name, step in ways:
+                when = has(step, distance)
+                chip = jnp.clip(at.chip - step * distance, 0, chips - 1)
+                found = piece(index, chip)
+                copies.arrived((name, index, distance), found, when)
+                if distance < chips - 1:
+                    copies.start(
+                        (name, index, distance + 1),
+                        found,
+                        found,
+                        neighbour(step),
+                        when & can_send(step),
+                    )
+                if index != 1:
+                    copies.start(("x", name, index, distance), found, found, at.other(x=1), when)
+                    copies.start(("y", name, index, distance), found, found, at.other(y=1), when)
+
+    def across(index):
+        if index == 1:
+            return
+        for distance in range(1, chips):
+            for name, step in ways:
+                when = has(step, distance)
+                chip = jnp.clip(at.chip - step * distance, 0, chips - 1)
+                key = (name, index, distance)
+                copies.arrived(("x",) + key, piece(index, chip, (1, None)), when)
+                upper = piece(index, chip, (1, 0))
+                copies.start(("xy",) + key, upper, upper, at.other(y=1), when)
+                copies.arrived(("y",) + key, piece(index, chip, (2, None)), when)
+                lower = piece(index, chip, (2, 1))
+                copies.start(("yx",) + key, lower, lower, at.other(x=1), when)
+
+    def close(index):
+        if index == 1:
+            return
+        for distance in range(1, chips):
+            for name, step in ways:
+                when = has(step, distance)
+                chip = jnp.clip(at.chip - step * distance, 0, chips - 1)
+                key = (name, index, distance)
+                copies.arrived(("xy",) + key, piece(index, chip, (3, 0)), when)
+                copies.arrived(("yx",) + key, piece(index, chip, (3, 1)), when)
+
+    count = len(wholes)
+    open_z(0)
+    for index in range(count):
+        if index + 1 < count:
+            open_z(index + 1)
+        pass_on(index)
+        across(index)
+    for index in range(count):
+        close(index)
+    own_copies[0].wait()
+    for step in range(1, 2 * chips):
+        copies.arrived(("vec", step), table.at[at.shard_at(2 * chips - step)])
+    copies.finish()
+
+
+def gather_weights(packed, matrices, splits, chips):
+    any_space = pl.BlockSpec(memory_space=pl.ANY)
+    vmem = pl.BlockSpec(memory_space=pltpu.VMEM)
+    shapes = [jax.ShapeDtypeStruct((2 * chips,) + packed.shape, LOW)]
+    for matrix, blocks in zip(matrices, splits):
+        rows, columns = matrix.shape
+        shape = (chips * rows, columns) if blocks is None else (2 * chips * rows, columns // 2)
+        shapes.append(jax.ShapeDtypeStruct(shape, LOW))
+    return pl.pallas_call(
+        partial(gather_kernel, chips, splits),
+        out_shape=tuple(shapes),
+        in_specs=[any_space] * 5,
+        out_specs=tuple([vmem] * 5),
+        scratch_shapes=[
+            pltpu.SemaphoreType.DMA((160,)),
+            pltpu.SemaphoreType.DMA((160,)),
+            pltpu.SemaphoreType.DMA((32,)),
+        ],
+        compiler_params=pltpu.CompilerParams(
+            collective_id=0, has_side_effects=True, vmem_limit_bytes=40 << 20
+        ),
+    )(packed, *matrices)
+
+
+def reduce_kernel(chips, chunks, blocks_of, *refs):
+    grads, sums_in = refs[:4], refs[4]
+    outs, sums_out = refs[5:9], refs[9]
+    scratch = refs[10:]
+    count = len(chunks)
+    across, from_x, from_y, mine, from_z, totals = [
+        scratch[k * count : (k + 1) * count] for k in range(6)
+    ]
+    sums_came, rep_came, rep_sent, send, recv = scratch[6 * count :]
+    at = Place(chips)
+    copies = Copies(send, recv, at)
+    peers = [at.other(chip=lax.rem(at.chip + step, chips)) for step in range(1, chips)]
+    at.greet(at.neighbours())
+    x_side, y_side = at.other(x=1), at.other(y=1)
+    rep_x, rep_y, rep_xy = at.flipped(1), at.flipped(2), at.flipped(3)
+
+    def view(n):
+        index, first, width = chunks[n]
+        return grads[index], pl.ds(first, width), grads[index].shape[2] // 2
+
+    def send_across(n):
+        grad, columns, half = view(n)
+        upper, lower = pl.ds(0, half), pl.ds(half, half)
+        copies.start(("ax", n), grad.at[:, rep_xy, upper, columns], across[n].at[0], x_side)
+        copies.start(("ay", n), grad.at[:, rep_xy, lower, columns], across[n].at[1], y_side)
+        copies.start(("bx", n), grad.at[:, rep_x, upper, columns], from_x[n].at[:, upper], x_side)
+        copies.start(("by", n), grad.at[:, rep_y, lower, columns], from_y[n].at[:, lower], y_side)
+
+    def add_across(n):
+        grad, columns, half = view(n)
+        upper, lower = pl.ds(0, half), pl.ds(half, half)
+        copies.arrived(("ay", n), across[n].at[1])
+        across[n][1] = (
+            across[n][1].astype(F32) + grad[:, rep_x, half : 2 * half, columns].astype(F32)
+        ).astype(LOW)
+        copies.start(("cx", n), across[n].at[1], from_x[n].at[:, lower], x_side)
+        copies.arrived(("ax", n), across[n].at[0])
+        across[n][0] = (
+            across[n][0].astype(F32) + grad[:, rep_y, 0:half, columns].astype(F32)
+        ).astype(LOW)
+        copies.start(("cy", n), across[n].at[0], from_y[n].at[:, upper], y_side)
+
+    def add_reps(n):
+        grad, columns, half = view(n)
+        upper, lower = pl.ds(0, half), pl.ds(half, half)
+        copies.arrived(("bx", n), from_x[n].at[:, upper])
+        copies.arrived(("by", n), from_y[n].at[:, lower])
+        copies.arrived(("cx", n), from_x[n].at[:, lower])
+        copies.arrived(("cy", n), from_y[n].at[:, upper])
+        mine[n][...] = (
+            grad[:, at.rep, :, columns].astype(F32)
+            + from_x[n][...].astype(F32)
+            + from_y[n][...].astype(F32)
+        ).astype(LOW)
+        for step in range(1, chips):
+            chip = lax.rem(at.chip + step, chips)
+            copies.start(("z", n, step), mine[n].at[chip], from_z[n].at[step - 1], peers[step - 1])
+
+    def add_chips(n):
+        grad, columns, half = view(n)
+        for step in range(1, chips):
+            copies.arrived(("z", n, step), from_z[n].at[step - 1])
+        total = (
+            grad[at.chip, at.rep, :, columns].astype(F32)
+            + from_x[n][at.chip].astype(F32)
+            + from_y[n][at.chip].astype(F32)
+        )
+        for step in range(chips - 1):
+            total = total + from_z[n][step].astype(F32)
+        totals[n][at.rep] = total.astype(LOW)
+        own = totals[n].at[at.rep]
+        copies.start(("ex", n), own, own, x_side)
+        copies.start(("ey", n), own, own, y_side)
+
+    def spread(n):
+        grad, columns, half = view(n)
+        copies.arrived(("ex", n), totals[n].at[rep_x])
+        part = totals[n].at[rep_x, pl.ds(0, half)]
+        copies.start(("exy", n), part, part, y_side)
+        copies.arrived(("ey", n), totals[n].at[rep_y])
+        part = totals[n].at[rep_y, pl.ds(half, half)]
+        copies.start(("eyx", n), part, part, x_side)
+
+    def sides(n):
+        index, first, width = chunks[n]
+        block = blocks_of[index]
+        for start in range(0, width, block):
+            yield start, ((first + start) // block) * 2, block
+
+    def deliver(n):
+        index, first, width = chunks[n]
+        half = grads[index].shape[2] // 2
+        copies.arrived(("exy", n), totals[n].at[rep_xy, pl.ds(0, half)])
+        copies.arrived(("eyx", n), totals[n].at[rep_xy, pl.ds(half, half)])
+        if blocks_of[index] is None:
+            outs[index][:, :, first : first + width] = totals[n][...]
+            return
+        for start, place, block in sides(n):
+            columns = pl.ds(pl.multiple_of((place + at.core) * block, block), block)
+            copies.start(
+                ("pair", n, start),
+                totals[n].at[pl.ds(2 * (1 - at.core), 2), :, pl.ds(start, block)],
+                outs[index].at[:, :, columns],
+                at.other(core=1),
+            )
+            outs[index][:, :, columns] = totals[n][pl.ds(2 * at.core, 2), :, start : start + block]
+
+    def receive(n):
+        index = chunks[n][0]
+        if blocks_of[index] is None:
+            return
+        for start, place, block in sides(n):
+            columns = pl.ds(pl.multiple_of((place + 1 - at.core) * block, block), block)
+            copies.arrived(("pair", n, start), outs[index].at[:, :, columns])
+
+    for step in range(1, 2 * chips):
+        target = at.shard_at(step)
+        copies.start(
+            ("sum", step), sums_in.at[target], sums_came.at[step - 1], {"shard": target, "rep": at.rep}
+        )
+    stages = (send_across, add_across, add_reps, add_chips, spread, deliver, receive)
+    for time in range(count + 2 * len(stages)):
+        for k, stage in enumerate(stages):
+            n = time - (k if k < 2 else 2 * k - 2)
+            if 0 <= n < count:
+                stage(n)
+        if time == 1:
+            total = sums_in[at.shard]
+            for step in range(1, 2 * chips):
+                copies.arrived(("sum", step), sums_came.at[step - 1])
+                total = total + sums_came[step - 1]
+            rep_sent[0] = total
+            copies.start(("sumx",), rep_sent.at[0], rep_came.at[0], x_side)
+        if time == 2:
+            copies.arrived(("sumx",), rep_came.at[0])
+            rep_sent[1] = rep_sent[0] + rep_came[0]
+            copies.start(("sumy",), rep_sent.at[1], rep_came.at[1], y_side)
+        if time == 3:
+            copies.arrived(("sumy",), rep_came.at[1])
+            sums_out[...] = rep_sent[1] + rep_came[1]
+    copies.finish()
+
+
+def reduce_grads(grads, sums, blocks_of, chips, chunk_width):
+    chunks = []
+    views = [grad.reshape(chips, 4, grad.shape[0] // (4 * chips), grad.shape[1]) for grad in grads]
+    for index in (3, 2, 1, 0):
+        for first in range(0, views[index].shape[3], chunk_width):
+            chunks.append((index, first, min(chunk_width, views[index].shape[3] - first)))
+    vmem = pl.BlockSpec(memory_space=pltpu.VMEM)
+    out_shapes = []
+    for member, block in zip(views, blocks_of):
+        quarter, columns = member.shape[2:]
+        shape = (4, quarter, columns) if block is None else (2, quarter, 2 * columns)
+        out_shapes.append(jax.ShapeDtypeStruct(shape, LOW))
+    out_shapes.append(jax.ShapeDtypeStruct(sums.shape[1:], F32))
+    shapes = [(views[index].shape[2], width) for index, _, width in chunks]
+    scratch = [pltpu.VMEM((2, chips, q // 2, w), LOW) for q, w in shapes]
+    for _ in range(3):
+        scratch += [pltpu.VMEM((chips, q, w), LOW) for q, w in shapes]
+    scratch += [pltpu.VMEM((chips - 1, q, w), LOW) for q, w in shapes]
+    scratch += [pltpu.VMEM((4, q, w), LOW) for q, w in shapes]
+    scratch += [
+        pltpu.VMEM((2 * chips - 1,) + sums.shape[1:], F32),
+        pltpu.VMEM((2,) + sums.shape[1:], F32),
+        pltpu.VMEM((2,) + sums.shape[1:], F32),
+        pltpu.SemaphoreType.DMA((240,)),
+        pltpu.SemaphoreType.DMA((240,)),
+    ]
+    reduced = pl.pallas_call(
+        partial(reduce_kernel, chips, chunks, blocks_of),
+        out_shape=tuple(out_shapes),
+        in_specs=[vmem] * 5,
+        out_specs=tuple([vmem] * 5),
+        scratch_shapes=scratch,
+        compiler_params=pltpu.CompilerParams(
+            collective_id=1, has_side_effects=True, vmem_limit_bytes=60 << 20
+        ),
+    )(*views, sums)
+    flat = [member.reshape(-1, member.shape[2]).astype(F32) for member in reduced[:4]]
+    return flat, reduced[4]
+
 
 def shards(
     chips,
@@ -397,7 +818,29 @@
         up_bias,
     )
     lengths = [member.shape[0] for member in vectors]
-    table = links.gather_vectors(jnp.concatenate(vectors)).astype(F32)
+    packed_length = sum(lengths)
+    fast = reps == 4
+    lines = -(-packed_length // (16 * BLOCK)) * 16
+
+    def pad_lines(values):
+        values = jnp.pad(values, ((0, 0), (0, lines * BLOCK - packed_length)))
+        return values.reshape(-1, lines, BLOCK)
+
+    packed_in = jnp.concatenate(vectors)
+    if fast:
+        table, input_part, output_part, up_part, down_part = gather_weights(
+            pad_lines(packed_in[None])[0],
+            (input_weight, output_weight, up_weight, down_weight),
+            (3 * chips, None, chips, None),
+            chips,
+        )
+        table = table.reshape(shard_count, -1)[:, :packed_length].astype(F32)
+    else:
+        table = links.gather_vectors(packed_in).astype(F32)
+        input_part = links.gather(links.halves(input_weight, 3))
+        output_part = links.gather(output_weight)
+        up_part = links.gather(links.halves(up_weight, 1))
+        down_part = links.gather(down_weight)
     wholes, at = [], 0
     for length in lengths:
         wholes.append(table[:, at : at + length])
@@ -408,11 +851,6 @@
 
     def core_part(index):
         return pick(wholes[index].reshape(chips, 2, -1), core, 1).reshape(1, -1)
-
-    input_part = links.gather(links.halves(input_weight, 3))
-    output_part = links.gather(output_weight)
-    up_part = links.gather(links.halves(up_weight, 1))
-    down_part = links.gather(down_weight)
 
     inputs = tokens.reshape(own_rows, width).astype(F32)
     unit_one, inverse_one = normalize(inputs)
@@ -442,21 +880,21 @@
     hidden = dot(normed_two, up_part) + core_part(8)
     activated, gelu_back = jax.vjp(gelu_tanh, hidden)
     activated = activated.astype(LOW)
-    down_grad = links.reduce(rows_dot(activated, down_low)).astype(F32)
+    down_partial = rows_dot(activated, down_low).astype(LOW)
     result = middle + pair_sum(dot(activated, down_part)) + whole(7)
 
     upstream = cotangent.reshape(own_rows, width).astype(F32)
     (hidden_grad,) = gelu_back(back_dot(down_low, down_part))
     hidden_low = hidden_grad.astype(LOW)
-    up_grad = links.unhalves(links.reduce(rows_dot(normed_two, hidden_low)), 1).astype(F32)
+    up_partial = rows_dot(normed_two, hidden_low).astype(LOW)
     upper_two = pair_sum(back_dot(hidden_low, up_part))
     middle_grad = upstream + normalize_back(upper_two, whole(5), unit_two, inverse_two)
     output_own = middle_grad.astype(LOW)
     output_low = pair_rows(output_own)
-    output_grad = links.reduce(rows_dot(branch, output_low)).astype(F32)
+    output_partial = rows_dot(branch, output_low).astype(LOW)
     attended = back_dot(output_low, output_part).astype(LOW)
     mixed_grad = attention_back(mixed, starts, attended, blocks)
-    input_weight_grad = links.unhalves(links.reduce(rows_dot(all_normed, mixed_grad)), 3).astype(F32)
+    input_partial = rows_dot(all_normed, mixed_grad).astype(LOW)
     back_halo = links.shift(mixed_grad[2 * own_rows :, half:], -1)
     body = mixed_grad[: 2 * own_rows].reshape(micro, 2 * tok_rows, 3 * half)
     tail_grad = body[:, 2 * tok_rows - BLOCK :, half:].astype(F32) + back_halo.reshape(
@@ -491,7 +929,22 @@
         ],
         axis=1,
     )
-    sums = links.reduce_vectors(packed)
+    if fast:
+        grads, sums = reduce_grads(
+            (input_partial, output_partial, up_partial, down_partial),
+            pad_lines(packed),
+            (width // shard_count, None, up_part.shape[1] // chips, None),
+            chips,
+            512,
+        )
+        input_weight_grad, output_grad, up_grad, down_grad = grads
+        sums = sums.reshape(-1)[:packed_length]
+    else:
+        sums = links.reduce_vectors(packed)
+        input_weight_grad = links.unhalves(links.reduce(input_partial), 3).astype(F32)
+        output_grad = links.reduce(output_partial).astype(F32)
+        up_grad = links.unhalves(links.reduce(up_partial), 1).astype(F32)
+        down_grad = links.reduce(down_partial).astype(F32)
     vector_grads, at = [], 0
     for length in lengths:
         vector_grads.append(sums[at : at + length])

time: 556 us -> 468 us (0.84)
  Pallas kernels: 41.8 us -> 300 us
  waiting for transfers between devices: 221 us -> 29.5 us
  starting transfers between devices: 103 us -> 4.62 us
  other arithmetic: 57.2 us -> 29.4 us
  local copies, waits for them, and re-layouts: 57.7 us -> 32.5 us
    pallas_call x0 -> x2, Pallas kernels: none -> 257 us  [the longest x1 148 us: reduce_grads(): pl.pallas_call(partial(reduce_kernel, chips, chunks, blocks_of), out_shap...]
    ppermute x98 -> x8, waiting for transfers between devices: 211 us -> 10.4 us  [swap(): return lax.ppermute(values, AXES, pairs)]
    ppermute x98 -> x8, starting transfers between devices: 100 us -> 2.01 us  [swap(): return lax.ppermute(values, AXES, pairs)]
    dynamic_slice x16 -> x5, local copies, waits for them, and re-layouts: 20.4 us -> 2.21 us  [pick(): return lax.dynamic_index_in_dim(stacked, index, axis, keepdims=False)]
    another operation x34 -> x0, other arithmetic: 11.3 us -> none  [the longest x20 5.89 us: gather(): jnp.stack([jnp.concatenate([pick(quarters, self.rep ^ j)[None], found[j]]...]
    ppermute x2, waiting for transfers between devices: 10.5 us -> 19.1 us  [shift(): return lax.ppermute(values, AXES, pairs)]
    unnamed x202 -> x95, local copies, waits for them, and re-layouts: 21 us -> 26 us
  transfers between devices with their start and end apart: 100 -> 10, of which waited for: 46 -> 7; matrix products, arithmetic and copies ran while one was open for 21% -> 8% of each run, Pallas kernels for 2% -> 0%
where the time goes in v2:
time: 468 us; the launch traced here: 461 us
  Pallas kernels  300 us (64%)
  matrix products  63.6 us (14%)
  local copies, waits for them, and re-layouts  32.5 us (7%)
  waiting for transfers between devices  29.5 us (6%)
  other arithmetic  29.4 us (6%)
    pallas_call x1, Pallas kernels, reduce_grads(): pl.pallas_call(partial(reduce_kernel, chips, chunks, blocks_of), out_shap...  148 us
    pallas_call x1, Pallas kernels, gather_weights(): pl.pallas_call(partial(gather_kernel, chips, splits), out_shape=tuple(sha...  110 us
    pallas_call x1, Pallas kernels, attention_back(): pl.pallas_call(partial(attention_back_kernel, blocks, width), out_shape=j...  33 us
    unnamed x95, local copies, waits for them, and re-layouts  26 us
    dot_general x4, matrix products, rows_dot(): lax.dot_general(left, right, (((0,), (0,)), ((), ())), preferred_element_...  22.1 us
    dot_general x4, matrix products, back_dot(): lax.dot_general(left, right, (((1,), (1,)), ((), ())), preferred_element_...  21.3 us
    dot_general x4, matrix products, dot(): return jnp.dot(left, right, preferred_element_type=F32)  20.2 us
    ppermute x2, waiting for transfers between devices, shift(): return lax.ppermute(values, AXES, pairs)  19.1 us
  transfers between devices with their start and end apart: 10, of which 7 were waited for; matrix products, arithmetic and copies ran while one was open for 8% of the time, Pallas kernels for 0%

profile of v2, /device:TPU:0, one launch (start us, length us, event | category | flops | bytes accessed | tf_op | source)
XLA Modules:
  0.0 461.0 jit_solution(3756867957880075361)
XLA Ops:
  12.6 109.8 %shard_map.280 = (bf16[8,16,128]{2,1,0:T(8,128)(2,1)S(1)}, bf16[1024,1536]{1,0:T(8,128)(2,1)S(1)}, bf16[512,1024]{1,0:T(8,128)(2,1)S(1)}, bf16[1024,2048]{1,0:T(8,128)(2,1)S(1)}, bf16[2048,1024]{1,0:T(8,128)(2,1)}) custom-call(bf16[16,128]{1,0:T(8,128)(2,1)S(1)} %bitcast.218, bf16[128,3072]{1,0:T(8,128)(2,1)S(1)} %copy-done.6, ...), custom_call_target="tpu_custom_call" | custom-call | tf_op jit(solution)/shard_map/pallas_call | solution.py:568
  122.4 1.7 copy-done.10
  124.8 1.6 fusion.27
  127.2 2.2 collective-permute-done
  129.4 1.9 select_bitcast_fusion.3
  133.4 11.2 %collective-permute-done.1 = bf16[256,1024]{1,0:T(8,128)(2,1)S(1)} collective-permute-done((bf16[256,1024]{1,0:T(8,128)(2,1)S(1)}, bf16[256,1024]{1,0:T(8,128)(2,1)S(1)}, u32[]{:S(2)}, u32[]{:S(2)}) %collective-permute-start.1) | collective-permute-done | bytes 524320 | tf_op jit(solution)/shard_map/ppermute | solution.py:221
  144.6 6.8 %fusion.7.mixed_ref = bf16[1280,1536]{1,0:T(8,128)(2,1)S(1)} fusion(bf16[1024,1536]{1,0:T(8,128)(2,1)} %copy-done.10, f32[1536]{0:T(1024)S(1)} %fusion.37, bf16[256,1024]{1,0:T(8,128)(2,1)S(1)} %collective-permute-done.1, bf16[1024,1024]{1,0:T(8,128)(2,1)} %bitcast.232), kind=kOutput, calls=%fused_computation.12 | convolution fusion | flops 4035706880 | bytes 9705472 | tf_op jit(solution)/shard_map/dot_general | solution.py:20
  151.4 9.3 %shard_map.281 = bf16[1024,512]{1,0:T(8,128)(2,1)S(1)} custom-call(bf16[1280,1536]{1,0:T(8,128)(2,1)S(1)} %fusion.7.mixed_ref, s32[1024,1]{1,0:T(8,128)S(1)} %bitcast.215), custom_call_target="tpu_custom_call" | custom-call | flops 1073741824 | bytes 8388608 | tf_op jit(solution)/shard_map/pallas_call | solution.py:166
  163.2 3.6 collective-permute-done.2
  169.2 1.7 select_bitcast_fusion.1
  173.4 1.9 broadcast_select_fusion.3
  175.6 2.7 copy-done.9
  178.3 6.8 %fusion.57 = f32[1024,2048]{1,0:T(8,128)} fusion(bf16[1024,1024]{1,0:T(8,128)(2,1)S(1)} %bitcast.239, bf16[1024,2048]{1,0:T(8,128)(2,1)S(1)} %copy-done.9), kind=kOutput, calls=%fused_computation.170 | convolution fusion | flops 4294967296 | bytes 14680064 | tf_op jit(solution)/shard_map/dot_general | solution.py:20
  185.1 12.0 %convert_reduce_fusion = (f32[2048]{0:T(1024)S(1)}, bf16[1024,2048]{1,0:T(8,128)(2,1)S(1)}) fusion(f32[1024,2048]{1,0:T(8,128)} %fusion.57, f32[2048]{0:T(1024)S(1)} %bitcast.264, bf16[1024,1024]{1,0:T(8,128)(2,1)S(1)} %bitcast.241, bf16[2048,1024]{1,0:T(8,128)(2,1)S(1)} %copy-done.31), kind=kOutput, calls=%fused_computation.10 | convolution fusion | flops 4343199744 | bytes 18890752 | tf_op jit(solution)/shard_map/dot_general | solution.py:28
  197.2 4.5 fusion.58
  202.6 2.5 copy-done.34
  205.1 5.4 %fusion.51 = f32[1024,1024]{1,0:T(8,128)S(1)} fusion(bf16[2048,1024]{1,0:T(8,128)(2,1)S(1)} %copy-done.31, f32[1024,2048]{1,0:T(8,128)S(1)} %copy-done.34, f32[2048]{0:T(1024)S(1)} %bitcast.265), kind=kOutput, calls=%fused_computation.166 | convolution fusion | flops 4315938816 | bytes 16785408 | tf_op jit(solution)/shard_map/dot_general | solution.py:20
  212.7 2.7 collective-permute-done.4
  215.3 3.6 convert_reduce_fusion.5
  222.0 1.7 broadcast_select_fusion.1
  227.3 33.0 %shard_map.282 = bf16[1280,1536]{1,0:T(8,128)(2,1)S(1)} custom-call(bf16[1280,1536]{1,0:T(8,128)(2,1)S(1)} %copy-done.3, s32[1024,1]{1,0:T(8,128)S(1)} %bitcast.216, bf16[1024,512]{1,0:T(8,128)(2,1)S(1)} %convolution_convert_fusion.4.upper_ref), custom_call_target="tpu_custom_call" | custom-call | flops 2684354560 | bytes 16777216 | tf_op jit(solution)/shard_map/pallas_call | solution.py:182
  261.7 7.6 %convolution_convert_fusion = bf16[2048,1024]{1,0:T(8,128)(2,1)} fusion(bf16[1024,1024]{1,0:T(8,128)(2,1)S(1)} %bitcast.242, f32[1024,2048]{1,0:T(8,128)S(1)} %bitcast.268, f32[2048]{0:T(1024)S(1)} %bitcast.266), kind=kOutput, calls=%fused_computation.13 | convolution fusion | flops 4318035968 | bytes 14688256 | tf_op jit(solution)/shard_map/dot_general | solution.py:24
  269.4 7.8 %collective-permute-done.8 = bf16[256,1024]{1,0:T(8,128)(2,1)S(1)} collective-permute-done((bf16[256,1024]{1,0:T(8,128)(2,1)S(1)}, bf16[256,1024]{1,0:T(8,128)(2,1)S(1)}, u32[]{:S(2)}, u32[]{:S(2)}) %collective-permute-start.8) | collective-permute-done | bytes 524320 | tf_op jit(solution)/shard_map/ppermute | solution.py:221
  277.4 3.4 fusion.8
  283.7 6.3 %convolution_convert_fusion.1 = bf16[1024,2048]{1,0:T(8,128)(2,1)} fusion(bf16[1024,1024]{1,0:T(8,128)(2,1)S(1)} %bitcast.240, bf16[1024,2048]{1,0:T(8,128)(2,1)S(1)} %copy-done.33), kind=kOutput, calls=%fused_computation.14 | convolution fusion | flops 4297064448 | bytes 10485760 | tf_op jit(solution)/shard_map/dot_general | solution.py:24
  291.5 2.3 convolution_convert_fusion.3
  293.8 6.0 %convolution_convert_fusion.2 = bf16[1024,1536]{1,0:T(8,128)(2,1)} fusion(bf16[1280,1536]{1,0:T(8,128)(2,1)S(1)} %copy-done.1, bf16[256,1024]{1,0:T(8,128)(2,1)S(1)} %collective-permute-done.1, bf16[1024,1024]{1,0:T(8,128)(2,1)S(1)} %bitcast.233), kind=kOutput, calls=%fused_computation.15 | convolution fusion | flops 4033347584 | bytes 9699328 | tf_op jit(solution)/shard_map/dot_general | solution.py:24
  301.9 147.6 %shard_map.283 = (bf16[2,64,3072]{2,1,0:T(8,128)(2,1)}, bf16[4,32,1024]{2,1,0:T(8,128)(2,1)}, bf16[2,64,4096]{2,1,0:T(8,128)(2,1)}, bf16[4,128,1024]{2,1,0:T(8,128)(2,1)}, f32[16,128]{1,0:T(8,128)}) custom-call(bf16[4,4,64,1536]{3,2,1,0:T(8,128)(2,1)} %bitcast.234, bf16[4,4,32,1024]{3,2,1,0:T(8,128)(2,1)} %bitcast.226, bf16[4,4,64,2048]{3,2,1,0:T(8,128)(2,1)} %bitcast.222, ...), custom_call_target="tpu_custom_call" | custom-call | tf_op jit(solution)/shard_map/pallas_call | solution.py:753
  449.4 1.5 slice_bitcast_fusion.7
  452.2 2.8 bitcast_convert_fusion
  455.0 1.6 bitcast_convert_fusion.1
  458.8 1.7 fusion.32
  (180 shorter events, 43.9 us)
Async XLA Ops:
  12.6 111.5 %copy-start.14 = (bf16[2,256,1024]{2,1,0:T(8,128)(2,1)S(1)}, bf16[2,256,1024]{2,1,0:T(8,128)(2,1)}, u32[]{:S(2)}) copy-start(bf16[2,256,1024]{2,1,0:T(8,128)(2,1)} %param.19) | copy-start | bytes 3145732
  124.0 2.4 copy-start.8
  124.1 2.6 copy-start.30
  126.4 3.0 collective-permute-start
  131.6 13.0 %collective-permute-start.1 = (bf16[256,1024]{1,0:T(8,128)(2,1)S(1)}, bf16[256,1024]{1,0:T(8,128)(2,1)S(1)}, u32[]{:S(2)}, u32[]{:S(2)}) collective-permute-start(bf16[256,1024]{1,0:T(8,128)(2,1)S(1)} %bitcast.246), channel_id=1, source_target_pairs={{0,8},{1,9},{2,10},{3,11},{4,12},{5,13},{6,14},{7,15},{8,16},{9,17... | collective-permute-start | bytes 1572872 | tf_op jit(solution)/shard_map/ppermute | solution.py:221
  151.4 9.3 %copy-start.2 = (bf16[1280,1536]{1,0:T(8,128)(2,1)}, bf16[1280,1536]{1,0:T(8,128)(2,1)S(1)}, u32[]{:S(2)}) copy-start(bf16[1280,1536]{1,0:T(8,128)(2,1)S(1)} %fusion.7.mixed_ref) | copy-start | bytes 11796484
  162.0 4.8 %copy-start.15 = (bf16[2,256,1024]{2,1,0:T(8,128)(2,1)S(1)}, bf16[2,256,1024]{2,1,0:T(8,128)(2,1)}, u32[]{:S(2)}) copy-start(bf16[2,256,1024]{2,1,0:T(8,128)(2,1)} %param.19) | copy-start | bytes 3145732
  162.6 4.2 collective-permute-start.2
  162.7 6.5 %collective-permute-start.5 = (bf16[512,1024]{1,0:T(8,128)(2,1)}, bf16[512,1024]{1,0:T(8,128)(2,1)}, u32[]{:S(2)}, u32[]{:S(2)}) collective-permute-start(bf16[512,1024]{1,0:T(8,128)(2,1)} %bitcast.33), channel_id=1, source_target_pairs={{0,4},{1,5},{2,6},{3,7},{4,0},{5,1},{6,2},{7,3},{8,12},{9,13},{10,... | collective-permute-start | bytes 3145736 | tf_op jit(solution)/shard_map/ppermute | solution.py:211
  169.0 3.0 collective-permute-start.3
  171.3 13.9 %copy-start.24 = (bf16[2,2,256,1024]{3,2,1,0:T(8,128)(2,1)}, bf16[2,2,256,1024]{3,2,1,0:T(8,128)(2,1)S(1)}, u32[]{:S(2)}) copy-start(bf16[2,2,256,1024]{3,2,1,0:T(8,128)(2,1)S(1)} %copy.44) | copy-start | bytes 6291460
  175.3 2.9 copy-start.9
  175.6 9.6 %copy-start.22 = (bf16[2,2,256,1024]{3,2,1,0:T(8,128)(2,1)}, bf16[2,2,256,1024]{3,2,1,0:T(8,128)(2,1)S(1)}, u32[]{:S(2)}) copy-start(bf16[2,2,256,1024]{3,2,1,0:T(8,128)(2,1)S(1)} %pad_maximum_fusion.2) | copy-start | bytes 6291460
  178.3 6.8 %copy-start.31 = (bf16[2048,1024]{1,0:T(8,128)(2,1)S(1)}, bf16[2048,1024]{1,0:T(8,128)(2,1)}, u32[]{:S(2)}) copy-start(bf16[2048,1024]{1,0:T(8,128)(2,1)} %get-tuple-element.41) | copy-start | bytes 12582916
  197.2 4.5 copy-start.32
  201.7 3.4 copy-start.34
  202.2 9.3 %collective-permute-start.6 = (f32[512,1024]{1,0:T(8,128)S(1)}, f32[512,1024]{1,0:T(8,128)S(1)}, u32[]{:S(2)}, u32[]{:S(2)}) collective-permute-start(f32[512,1024]{1,0:T(8,128)S(1)} %bitcast.237), channel_id=1, source_target_pairs={{0,4},{1,5},{2,6},{3,7},{4,0},{5,1},{6,2},{7,3},{8,12},{9,13},{10,... | collective-permute-start | bytes 6291464 | tf_op jit(solution)/shard_map/ppermute | solution.py:211
  211.1 4.2 collective-permute-start.4
  219.0 3.0 collective-permute-start.7
  225.2 36.5 %slice-start.1 = ((s8[8388608]{0:T(1024)(128)(4,1)}), s8[4194304]{0:T(1024)(128)(4,1)S(1)}, s32[]{:S(2)}) async-start(s8[8388608]{0:T(1024)(128)(4,1)} %bitcast.267), calls=%async_computation.1 | async-start | bytes 8388608
  227.3 34.4 %copy-start.25 = (bf16[2,2,256,1024]{3,2,1,0:T(8,128)(2,1)S(1)}, bf16[2,2,256,1024]{3,2,1,0:T(8,128)(2,1)}, u32[]{:S(2)}) copy-start(bf16[2,2,256,1024]{3,2,1,0:T(8,128)(2,1)} %copy-done.24) | copy-start | bytes 6291460
  227.3 34.4 %slice-start.2 = ((s8[8388608]{0:T(1024)(128)(4,1)}), s8[4194304]{0:T(1024)(128)(4,1)S(1)}, s32[]{:S(2)}) async-start(s8[8388608]{0:T(1024)(128)(4,1)} %bitcast.267), calls=%async_computation.2 | async-start | bytes 8388608
  260.3 9.0 %copy-start = (bf16[1280,1536]{1,0:T(8,128)(2,1)}, bf16[1280,1536]{1,0:T(8,128)(2,1)S(1)}, u32[]{:S(2)}) copy-start(bf16[1280,1536]{1,0:T(8,128)(2,1)S(1)} %shard_map.282) | copy-start | bytes 11796484
  260.4 16.8 %collective-permute-start.8 = (bf16[256,1024]{1,0:T(8,128)(2,1)S(1)}, bf16[256,1024]{1,0:T(8,128)(2,1)S(1)}, u32[]{:S(2)}, u32[]{:S(2)}) collective-permute-start(bf16[256,1024]{1,0:T(8,128)(2,1)S(1)} %slice.204), channel_id=1, source_target_pairs={{8,0},{9,1},{10,2},{11,3},{12,4},{13,5},{14,6},{15,7},{16,8},{17,9... | collective-permute-start | bytes 1572872 | tf_op jit(solution)/shard_map/ppermute | solution.py:221
  269.4 7.9 %slice-start = ((bf16[1280,1536]{1,0:T(8,128)(2,1)}), bf16[1024,1536]{1,0:T(8,128)(2,1)S(1)}, s32[]{:S(2)}) async-start(bf16[1280,1536]{1,0:T(8,128)(2,1)} %copy-done), calls=%async_computation | async-start | bytes 6291456 | tf_op jit(solution)/shard_map/slice | solution.py:899
  269.4 8.0 %copy-start.11 = (bf16[1024,1536]{1,0:T(8,128)(2,1)S(1)}, bf16[1024,1536]{1,0:T(8,128)(2,1)}, u32[]{:S(2)}) copy-start(bf16[1024,1536]{1,0:T(8,128)(2,1)} %copy-done.10) | copy-start | bytes 9437188
  280.9 2.8 copy-start.33
  281.5 8.5 %copy-start.1 = (bf16[1280,1536]{1,0:T(8,128)(2,1)S(1)}, bf16[1280,1536]{1,0:T(8,128)(2,1)}, u32[]{:S(2)}) copy-start(bf16[1280,1536]{1,0:T(8,128)(2,1)} %copy-done) | copy-start | bytes 11796484
  281.5 18.3 %collective-permute-start.9 = (f32[512,1024]{1,0:T(8,128)S(1)}, f32[512,1024]{1,0:T(8,128)S(1)}, u32[]{:S(2)}, u32[]{:S(2)}) collective-permute-start(f32[512,1024]{1,0:T(8,128)S(1)} %bitcast.236), channel_id=1, source_target_pairs={{0,4},{1,5},{2,6},{3,7},{4,0},{5,1},{6,2},{7,3},{8,12},{9,13},{10,... | collective-permute-start | bytes 6291464 | tf_op jit(solution)/shard_map/ppermute | solution.py:211
  293.8 6.0 %copy-start.16 = (bf16[2,256,1024]{2,1,0:T(8,128)(2,1)S(1)}, bf16[2,256,1024]{2,1,0:T(8,128)(2,1)}, u32[]{:S(2)}) copy-start(bf16[2,256,1024]{2,1,0:T(8,128)(2,1)} %param.19) | copy-start | bytes 3145732
  449.4 5.6 %copy-start.26 = (bf16[2,64,4096]{2,1,0:T(8,128)(2,1)S(1)}, bf16[2,64,4096]{2,1,0:T(8,128)(2,1)}, u32[]{:S(2)}) copy-start(bf16[2,64,4096]{2,1,0:T(8,128)(2,1)} %get-tuple-element.45) | copy-start | bytes 3145732
  455.0 3.0 copy-start.28
  (16 other events, 26.9 us)

commit v3 on v2

--- a/solution.py
+++ b/solution.py
@@ -361,14 +361,19 @@
     def start(self, name, source, target, device, when=None):
         copy = self.make(name, source, target, device)
         run_when(when, copy.start)
-        self.started.append((when, copy))
+        self.started.append((name, when, copy))
 
     def arrived(self, name, target, when=None):
         copy = self.make(name, target, target, self.links.other(x=1))
         run_when(when, copy.wait_recv)
 
+    def sent(self, name):
+        for item in [item for item in self.started if item[0] == name]:
+            run_when(item[1], item[2].wait_send)
+            self.started.remove(item)
+
     def finish(self):
-        for when, copy in self.started:
+        for _, when, copy in self.started:
             run_when(when, copy.wait_send)
 
 
@@ -581,187 +586,621 @@
     )(packed, *matrices)
 
 
-def reduce_kernel(chips, chunks, blocks_of, *refs):
-    grads, sums_in = refs[:4], refs[4]
-    outs, sums_out = refs[5:9], refs[9]
-    scratch = refs[10:]
-    count = len(chunks)
-    across, from_x, from_y, mine, from_z, totals = [
-        scratch[k * count : (k + 1) * count] for k in range(6)
-    ]
-    sums_came, rep_came, rep_sent, send, recv = scratch[6 * count :]
-    at = Place(chips)
-    copies = Copies(send, recv, at)
-    peers = [at.other(chip=lax.rem(at.chip + step, chips)) for step in range(1, chips)]
-    at.greet(at.neighbours())
-    x_side, y_side = at.other(x=1), at.other(y=1)
-    rep_x, rep_y, rep_xy = at.flipped(1), at.flipped(2), at.flipped(3)
-
-    def view(n):
-        index, first, width = chunks[n]
-        return grads[index], pl.ds(first, width), grads[index].shape[2] // 2
-
-    def send_across(n):
-        grad, columns, half = view(n)
+class Reduction:
+    def __init__(self, at, copies, blocks_of, outs):
+        self.at, self.copies, self.blocks_of, self.outs = at, copies, blocks_of, outs
+        self.x_side, self.y_side = at.other(x=1), at.other(y=1)
+        self.rep_x, self.rep_y, self.rep_xy = at.flipped(1), at.flipped(2), at.flipped(3)
+        self.chunks = []
+
+    def add(self, index, line, first, grad, across, from_x, from_y, from_z, totals):
+        self.chunks.append((index, line, first, grad, across, from_x, from_y, from_z, totals))
+
+    def send_across(self, n):
+        _, _, _, grad, across, from_x, from_y, _, _ = self.chunks[n]
+        half = grad.shape[2] // 2
         upper, lower = pl.ds(0, half), pl.ds(half, half)
-        copies.start(("ax", n), grad.at[:, rep_xy, upper, columns], across[n].at[0], x_side)
-        copies.start(("ay", n), grad.at[:, rep_xy, lower, columns], across[n].at[1], y_side)
-        copies.start(("bx", n), grad.at[:, rep_x, upper, columns], from_x[n].at[:, upper], x_side)
-        copies.start(("by", n), grad.at[:, rep_y, lower, columns], from_y[n].at[:, lower], y_side)
-
-    def add_across(n):
-        grad, columns, half = view(n)
+        start = self.copies.start
+        start(("ax", n), grad.at[:, self.rep_xy, upper], across.at[0], self.x_side)
+        start(("ay", n), grad.at[:, self.rep_xy, lower], across.at[1], self.y_side)
+        start(("bx", n), grad.at[:, self.rep_x, upper], from_x.at[:, upper], self.x_side)
+        start(("by", n), grad.at[:, self.rep_y, lower], from_y.at[:, lower], self.y_side)
+
+    def add_across(self, n):
+        _, _, _, grad, across, from_x, from_y, _, _ = self.chunks[n]
+        half = grad.shape[2] // 2
         upper, lower = pl.ds(0, half), pl.ds(half, half)
-        copies.arrived(("ay", n), across[n].at[1])
-        across[n][1] = (
-            across[n][1].astype(F32) + grad[:, rep_x, half : 2 * half, columns].astype(F32)
+        self.copies.arrived(("ay", n), across.at[1])
+        across[1] = (
+            across[1].astype(F32) + grad[:, self.rep_x, half : 2 * half].astype(F32)
         ).astype(LOW)
-        copies.start(("cx", n), across[n].at[1], from_x[n].at[:, lower], x_side)
-        copies.arrived(("ax", n), across[n].at[0])
-        across[n][0] = (
-            across[n][0].astype(F32) + grad[:, rep_y, 0:half, columns].astype(F32)
+        self.copies.start(("cx", n), across.at[1], from_x.at[:, lower], self.x_side)
+        self.copies.arrived(("ax", n), across.at[0])
+        across[0] = (across[0].astype(F32) + grad[:, self.rep_y, 0:half].astype(F32)).astype(LOW)
+        self.copies.start(("cy", n), across.at[0], from_y.at[:, upper], self.y_side)
+
+    def add_reps(self, n):
+        _, _, _, grad, _, from_x, from_y, from_z, _ = self.chunks[n]
+        at, half = self.at, grad.shape[2] // 2
+        upper, lower = pl.ds(0, half), pl.ds(half, half)
+        self.copies.arrived(("bx", n), from_x.at[:, upper])
+        self.copies.arrived(("by", n), from_y.at[:, lower])
+        self.copies.arrived(("cx", n), from_x.at[:, lower])
+        self.copies.arrived(("cy", n), from_y.at[:, upper])
+        from_x[...] = (
+            grad[:, at.rep].astype(F32) + from_x[...].astype(F32) + from_y[...].astype(F32)
         ).astype(LOW)
-        copies.start(("cy", n), across[n].at[0], from_y[n].at[:, upper], y_side)
-
-    def add_reps(n):
-        grad, columns, half = view(n)
-        upper, lower = pl.ds(0, half), pl.ds(half, half)
-        copies.arrived(("bx", n), from_x[n].at[:, upper])
-        copies.arrived(("by", n), from_y[n].at[:, lower])
-        copies.arrived(("cx", n), from_x[n].at[:, lower])
-        copies.arrived(("cy", n), from_y[n].at[:, upper])
-        mine[n][...] = (
-            grad[:, at.rep, :, columns].astype(F32)
-            + from_x[n][...].astype(F32)
-            + from_y[n][...].astype(F32)
-        ).astype(LOW)
-        for step in range(1, chips):
-            chip = lax.rem(at.chip + step, chips)
-            copies.start(("z", n, step), mine[n].at[chip], from_z[n].at[step - 1], peers[step - 1])
-
-    def add_chips(n):
-        grad, columns, half = view(n)
-        for step in range(1, chips):
-            copies.arrived(("z", n, step), from_z[n].at[step - 1])
-        total = (
-            grad[at.chip, at.rep, :, columns].astype(F32)
-            + from_x[n][at.chip].astype(F32)
-            + from_y[n][at.chip].astype(F32)
-        )
-        for step in range(chips - 1):
-            total = total + from_z[n][step].astype(F32)
-        totals[n][at.rep] = total.astype(LOW)
-        own = totals[n].at[at.rep]
-        copies.start(("ex", n), own, own, x_side)
-        copies.start(("ey", n), own, own, y_side)
-
-    def spread(n):
-        grad, columns, half = view(n)
-        copies.arrived(("ex", n), totals[n].at[rep_x])
-        part = totals[n].at[rep_x, pl.ds(0, half)]
-        copies.start(("exy", n), part, part, y_side)
-        copies.arrived(("ey", n), totals[n].at[rep_y])
-        part = totals[n].at[rep_y, pl.ds(half, half)]
-        copies.start(("eyx", n), part, part, x_side)
-
-    def sides(n):
-        index, first, width = chunks[n]
-        block = blocks_of[index]
+        for step in range(1, at.chips):
+            chip = lax.rem(at.chip + step, at.chips)
+            self.copies.start(
+                ("z", n, step), from_x.at[chip], from_z.at[step - 1], at.other(chip=chip)
+            )
+
+    def add_chips(self, n):
+        _, _, _, grad, _, from_x, _, from_z, totals = self.chunks[n]
+        at = self.at
+        total = from_x[at.chip].astype(F32)
+        for step in range(1, at.chips):
+            self.copies.arrived(("z", n, step), from_z.at[step - 1])
+            total = total + from_z[step - 1].astype(F32)
+        totals[at.rep] = total.astype(LOW)
+        own = totals.at[at.rep]
+        self.copies.start(("ex", n), own, own, self.x_side)
+        self.copies.start(("ey", n), own, own, self.y_side)
+
+    def spread(self, n):
+        totals = self.chunks[n][-1]
+        half = totals.shape[1] // 2
+        self.copies.arrived(("ex", n), totals.at[self.rep_x])
+        part = totals.at[self.rep_x, pl.ds(0, half)]
+        self.copies.start(("exy", n), part, part, self.y_side)
+        self.copies.arrived(("ey", n), totals.at[self.rep_y])
+        part = totals.at[self.rep_y, pl.ds(half, half)]
+        self.copies.start(("eyx", n), part, part, self.x_side)
+
+    def sides(self, n):
+        index, first, width = self.chunks[n][0], self.chunks[n][2], self.chunks[n][-1].shape[2]
+        block = self.blocks_of[index]
         for start in range(0, width, block):
             yield start, ((first + start) // block) * 2, block
 
-    def deliver(n):
-        index, first, width = chunks[n]
-        half = grads[index].shape[2] // 2
-        copies.arrived(("exy", n), totals[n].at[rep_xy, pl.ds(0, half)])
-        copies.arrived(("eyx", n), totals[n].at[rep_xy, pl.ds(half, half)])
-        if blocks_of[index] is None:
-            outs[index][:, :, first : first + width] = totals[n][...]
+    def deliver(self, n):
+        index, line, first, totals = *self.chunks[n][:3], self.chunks[n][-1]
+        quarter, width = totals.shape[1:]
+        half, at = quarter // 2, self.at
+        self.copies.arrived(("exy", n), totals.at[self.rep_xy, pl.ds(0, half)])
+        self.copies.arrived(("eyx", n), totals.at[self.rep_xy, pl.ds(half, half)])
+        out = self.outs[index]
+        if self.blocks_of[index] is None:
+            out[:, line : line + quarter, first : first + width] = totals[...]
             return
-        for start, place, block in sides(n):
+        for start, place, block in self.sides(n):
             columns = pl.ds(pl.multiple_of((place + at.core) * block, block), block)
-            copies.start(
+            self.copies.start(
                 ("pair", n, start),
-                totals[n].at[pl.ds(2 * (1 - at.core), 2), :, pl.ds(start, block)],
-                outs[index].at[:, :, columns],
+                totals.at[pl.ds(2 * (1 - at.core), 2), :, pl.ds(start, block)],
+                out.at[:, :, columns],
                 at.other(core=1),
             )
-            outs[index][:, :, columns] = totals[n][pl.ds(2 * at.core, 2), :, start : start + block]
-
-    def receive(n):
-        index = chunks[n][0]
-        if blocks_of[index] is None:
+            out[:, :, columns] = totals[pl.ds(2 * at.core, 2), :, start : start + block]
+
+    def receive(self, n):
+        index = self.chunks[n][0]
+        if self.blocks_of[index] is None:
             return
-        for start, place, block in sides(n):
-            columns = pl.ds(pl.multiple_of((place + 1 - at.core) * block, block), block)
-            copies.arrived(("pair", n, start), outs[index].at[:, :, columns])
-
-    for step in range(1, 2 * chips):
-        target = at.shard_at(step)
+        for start, place, block in self.sides(n):
+            columns = pl.ds(pl.multiple_of((place + 1 - self.at.core) * block, block), block)
+            self.copies.arrived(("pair", n, start), self.outs[index].at[:, :, columns])
+
+    def tick(self, time):
+        stages = (
+            self.send_across,
+            self.add_across,
+            self.add_reps,
+            self.add_chips,
+            self.spread,
+            self.deliver,
+            self.receive,
+        )
+        for stage, offset in zip(stages, OFFSETS):
+            if 0 <= time - offset < len(self.chunks):
+                stage(time - offset)
+
+
+OFFSETS = (0, 1, 2, 3, 5, 6, 7)
+PART = 512
+VECTOR_ROWS = 16
+
+
+def loop(count, body):
+    def step(index, carry):
+        body(index)
+        return carry
+
+    lax.fori_loop(0, count, step, 0)
+
+
+def backward_kernel(chips, micro, blocks, blocks_of, *refs):
+    (
+        activated_in,
+        down_low_in,
+        hidden_low_in,
+        normed_two_in,
+        up_in,
+        out_in,
+        in_in,
+        branch_in,
+        mixed_in,
+        all_normed_in,
+        middle_in,
+        tokens_in,
+        starts,
+        gains,
+    ) = refs[:14]
+    outs, vectors_out, input_grad_out = refs[14:18], refs[18], refs[19]
+    refs = refs[20:]
+    (
+        wide,
+        deep,
+        matrix,
+        out_matrix,
+        low,
+        normed,
+        branch,
+        attended,
+        give,
+        came,
+        middle,
+        tokens,
+        key_sums,
+        halo,
+        vectors,
+        vectors_came,
+    ) = refs[:16]
+    send, recv, local = refs[-3:]
+    pools = refs[16:-3]
+    at = Place(chips)
+    core = at.core
+    width = down_low_in.shape[1]
+    rows = down_low_in.shape[0]
+    body_rows, all_rows = rows, mixed_in.shape[0]
+    part_width = mixed_in.shape[1] // 3
+    hidden_width = hidden_low_in.shape[1]
+    own_rows, micro_rows = rows // 2, rows // micro
+    own_micro = micro_rows // 2
+    copies = Copies(send, recv, at)
+
+    loads = []
+
+    def load(source, target):
+        copy = pltpu.make_async_copy(source, target, local.at[len(loads)])
+        copy.start()
+        loads.append(copy)
+        return copy
+
+    activated = wide.at[pl.ds(0, rows)]
+    hidden_low = deep.at[pl.ds(0, rows)]
+    mixed = wide.at[:, pl.ds(0, 3 * part_width)]
+    mixed_grad = deep.at[:, pl.ds(0, 3 * part_width)]
+    in_matrix = matrix.at[:, pl.ds(0, 3 * part_width)]
+    normed_two = normed.at[pl.ds(0, rows)]
+    load_first = [load(activated_in, activated), load(down_low_in, low)]
+    load_up = [load(hidden_low_in, hidden_low), load(normed_two_in, normed_two)]
+    load_two = [load(up_in, matrix), load(middle_in, middle)]
+    load_three = [load(out_in, out_matrix), load(branch_in, branch), load(tokens_in, tokens)]
+    vectors[...] = jnp.zeros_like(vectors)
+    at.greet(at.neighbours())
+
+    reduction = Reduction(at, copies, blocks_of, outs)
+    (
+        grad_pool,
+        grad_pool_out,
+        across_pool,
+        across_out,
+        x_pool,
+        x_out,
+        y_pool,
+        y_out,
+        z_pool,
+        z_out,
+        t_pool,
+        t_out,
+    ) = pools
+    quarter = PART // 8
+
+    def pooled(n, grad_place, index, line, first):
+        reduction.add(
+            index,
+            line,
+            first,
+            grad_pool.at[grad_place],
+            across_pool.at[n],
+            x_pool.at[n],
+            y_pool.at[n],
+            z_pool.at[n],
+            t_pool.at[n],
+        )
+
+    down_parts, up_parts, in_parts = width // PART, hidden_width // PART, 3 * part_width // PART
+    for part in range(down_parts):
+        for line in range(2):
+            n = 2 * part + line
+            pooled(n, n, 3, line * quarter, part * PART)
+    for part in range(up_parts):
+        n = 2 * down_parts + part
+        pooled(n, n, 2, 0, part * PART)
+    reduction.add(1, 0, 0, grad_pool_out, across_out, x_out, y_out, z_out, t_out)
+    first_in = len(reduction.chunks)
+    for part in range(in_parts):
+        pooled(first_in - 1 + part, part, 0, 0, part * PART)
+
+    def own_place(row_side, step):
+        return pl.ds(pl.multiple_of(step * micro_rows + row_side * own_micro, own_micro), own_micro)
+
+    def dot_down(part):
+        block = activated_in.shape[1] // chips
+
+        def body(chip):
+            left = activated[:, pl.ds(pl.multiple_of(chip * block, block), block)]
+            result = rows_dot(left, low[:, part * PART : (part + 1) * PART]).astype(LOW)
+            result = result.reshape(4, 2, quarter, PART)
+            grad_pool[2 * part, chip] = result[:, 0]
+            grad_pool[2 * part + 1, chip] = result[:, 1]
+
+        loop(chips, body)
+
+    def dot_pair(place, left, right, part):
+        block = width // chips
+
+        def body(chip):
+            columns = left[:, pl.ds(pl.multiple_of(chip * block, block), block)]
+            result = rows_dot(columns, right[:, part * PART : (part + 1) * PART]).astype(LOW)
+            grad_pool[place, chip] = result.reshape(4, quarter, PART)
+
+        loop(chips, body)
+
+    def dot_up(part):
+        dot_pair(2 * down_parts + part, normed_two, hidden_low, part)
+
+    def dot_in(part):
+        for key in ("ax", "ay", "bx", "by"):
+            copies.sent((key, part))
+        dot_pair(part, normed, mixed_grad, part)
+
+    def dot_out():
+        block = part_width // chips
+
+        def body(chip):
+            left = branch[:, pl.ds(pl.multiple_of(chip * block, block), block)]
+            grad_pool_out[chip] = rows_dot(left, low[...]).astype(LOW).reshape(4, block // 4, width)
+
+        loop(chips, body)
+
+    def back_product(left, left_rows, right, target, target_rows, adding):
+        tile = 256
+
+        def body(step):
+            columns = pl.ds(pl.multiple_of(step * tile, tile), tile)
+            result = back_dot(left[left_rows, :], right[columns, :])
+            if adding:
+                result = result + target[target_rows, columns]
+            target[target_rows, columns] = result.astype(target.dtype)
+
+        loop(right.shape[0] // tile, body)
+
+    def give_partial(name, left, right):
+        for step in range(micro):
+            place = pl.ds(step * own_micro, own_micro)
+            back_product(left, own_place(1 - core, step), right, give, place, False)
+        copies.start(name, give, came, at.other(core=1))
+
+    def own_partial(name, left, right):
+        copies.arrived(name, came)
+        for step in range(micro):
+            place = pl.ds(step * own_micro, own_micro)
+            back_product(left, own_place(core, step), right, came, place, True)
+
+    def column_sum(row, values):
+        vectors[0, row : row + 1, :] += jnp.sum(values, axis=0, keepdims=True)
+
+    lines = 32
+
+    def second_norm_back():
+        gain = gains[1:2, :]
+
+        def body(step):
+            place = pl.ds(pl.multiple_of(step * lines, lines), lines)
+            chip_row = step // (own_micro // lines) * micro_rows + core * own_micro
+            chip_row = chip_row + lax.rem(step, own_micro // lines) * lines
+            chip_place = pl.ds(pl.multiple_of(chip_row, lines), lines)
+            unit, inverse = normalize(middle[place, :])
+            upper = came[place, :]
+            upstream = low[chip_place, :].astype(F32)
+            total = upstream + normalize_back(upper, gain, unit, inverse)
+            middle[place, :] = total
+            rounded = total.astype(LOW)
+            low[chip_place, :] = rounded
+            column_sum(2, rounded.astype(F32))
+            column_sum(3, upper * unit)
+            column_sum(4, upper)
+            column_sum(5, upstream)
+
+        loop(own_rows // lines, body)
+        for step in range(micro):
+            place = low.at[own_place(core, step)]
+            copies.start(("low", step), place, place, at.other(core=1))
+
+    def first_norm_back():
+        gain = gains[0:1, :]
+
+        def body(step):
+            place = pl.ds(pl.multiple_of(step * lines, lines), lines)
+            unit, inverse = normalize(tokens[place, :].astype(F32))
+            upper = came[place, :]
+            total = middle[place, :] + normalize_back(upper, gain, unit, inverse)
+            input_grad_out[place, :] = total.astype(LOW)
+            column_sum(0, upper * unit)
+            column_sum(1, upper)
+
+        loop(own_rows // lines, body)
+
+    def hidden_sums():
+        def body(step):
+            place = pl.ds(pl.multiple_of(step * lines, lines), lines)
+            for side in range(hidden_width // width):
+                column_sum(
+                    9 + side, hidden_low[place, side * width : (side + 1) * width].astype(F32)
+                )
+
+        loop(rows // lines, body)
+
+    def mixed_sums():
+        def body(step):
+            place = pl.ds(pl.multiple_of(step * lines, lines), lines)
+            joined = jnp.concatenate(
+                [
+                    mixed_grad[place, 0:part_width].astype(F32),
+                    mixed_grad[place, 2 * part_width : 3 * part_width].astype(F32),
+                ],
+                axis=1,
+            )
+            column_sum(8, joined)
+
+        loop(all_rows // lines, body)
+
+    left = lax.broadcasted_iota(jnp.int32, (BLOCK, BLOCK), 1) < HD
+    left_tall = lax.broadcasted_iota(jnp.int32, (2 * BLOCK, BLOCK), 1) < HD
+    scale = float(HD) ** (-0.5)
+
+    def attention_group(column):
+        key_sums[...] = jnp.zeros_like(key_sums)
+
+        def body(step):
+            row, previous = block_rows(step, blocks, body_rows)
+            allowed = allowed_keys(starts, row)
+            queries = mixed[pl.ds(row, BLOCK), column : column + BLOCK]
+            keys = window(mixed, row, previous, part_width + column)
+            values = window(mixed, row, previous, 2 * part_width + column)
+            upper = attended[pl.ds(row, BLOCK), column : column + BLOCK]
+            parts = []
+            for side in (left, ~left):
+                soft = soft_weights(jnp.where(side, queries, 0), keys, allowed)
+                soft_grad = back_dot(jnp.where(side, upper, 0), values)
+                total = jnp.sum(soft * soft_grad, axis=1, keepdims=True)
+                score_low = (soft * (soft_grad - total)).astype(LOW)
+                parts.append(
+                    (
+                        dot(score_low, keys) * scale,
+                        rows_dot(score_low, queries) * scale,
+                        rows_dot(soft.astype(LOW), upper),
+                    )
+                )
+            mixed_grad[pl.ds(row, BLOCK), column : column + BLOCK] = jnp.where(
+                left, parts[0][0], parts[1][0]
+            ).astype(LOW)
+            for slot in (1, 2):
+                joined = jnp.where(left_tall, parts[0][slot], parts[1][slot])
+                place = (slot - 1) * BLOCK
+                key_sums[pl.ds(previous, BLOCK), place : place + BLOCK] += joined[:BLOCK]
+                key_sums[pl.ds(row, BLOCK), place : place + BLOCK] += joined[BLOCK:]
+
+        loop(body_rows // BLOCK, body)
+        for slot in (1, 2):
+            place = (slot - 1) * BLOCK
+            mixed_grad[:, slot * part_width + column : slot * part_width + column + BLOCK] = (
+                key_sums[:, place : place + BLOCK].astype(LOW)
+            )
+        mixed_grad[body_rows:, column : column + BLOCK] = jnp.zeros(
+            (all_rows - body_rows, BLOCK), LOW
+        )
+
+    lower_chip = at.other(chip=jnp.maximum(at.chip - 1, 0))
+
+    def send_halo():
         copies.start(
-            ("sum", step), sums_in.at[target], sums_came.at[step - 1], {"shard": target, "rep": at.rep}
+            ("halo",),
+            mixed_grad.at[pl.ds(body_rows, all_rows - body_rows), pl.ds(part_width, 2 * part_width)],
+            halo,
+            lower_chip,
+            at.chip > 0,
         )
-    stages = (send_across, add_across, add_reps, add_chips, spread, deliver, receive)
-    for time in range(count + 2 * len(stages)):
-        for k, stage in enumerate(stages):
-            n = time - (k if k < 2 else 2 * k - 2)
-            if 0 <= n < count:
-                stage(n)
-        if time == 1:
-            total = sums_in[at.shard]
-            for step in range(1, 2 * chips):
-                copies.arrived(("sum", step), sums_came.at[step - 1])
-                total = total + sums_came[step - 1]
-            rep_sent[0] = total
-            copies.start(("sumx",), rep_sent.at[0], rep_came.at[0], x_side)
-        if time == 2:
-            copies.arrived(("sumx",), rep_came.at[0])
-            rep_sent[1] = rep_sent[0] + rep_came[0]
-            copies.start(("sumy",), rep_sent.at[1], rep_came.at[1], y_side)
-        if time == 3:
-            copies.arrived(("sumy",), rep_came.at[1])
-            sums_out[...] = rep_sent[1] + rep_came[1]
+
+    def add_halo():
+        copies.arrived(("halo",), halo, at.chip < chips - 1)
+
+        def body():
+            for step in range(micro):
+                place = pl.ds((step + 1) * micro_rows - BLOCK, BLOCK)
+                mixed_grad[place, part_width : 3 * part_width] = (
+                    mixed_grad[place, part_width : 3 * part_width].astype(F32)
+                    + halo[step * BLOCK : (step + 1) * BLOCK, :].astype(F32)
+                ).astype(LOW)
+
+        pl.when(at.chip < chips - 1)(body)
+
+    time = iter(range(100))
+
+    def tick():
+        reduction.tick(next(time))
+
+    def wait_for(members):
+        for member in members:
+            member.wait()
+
+    wait_for(load_first)
+    dot_down(0)
+    tick()
+    for part in range(1, down_parts):
+        dot_down(part)
+    tick()
+    load_mixed = [load(mixed_in, mixed)]
+    wait_for(load_up)
+    wait_for(load_two)
+    for part in range(up_parts // 2):
+        dot_up(part)
+    give_partial(("partial", 0), hidden_low, matrix)
+    tick()
+    for part in range(up_parts // 2, up_parts):
+        dot_up(part)
+    own_partial(("partial", 0), hidden_low, matrix)
+    load_last = [load(in_in, in_matrix), load(all_normed_in, normed)]
+    second_norm_back()
+    hidden_sums()
+    tick()
+    wait_for(load_three)
+    for step in range(micro):
+        back_product(
+            low, own_place(core, step), out_matrix, attended, own_place(core, step), False
+        )
+    for step in range(micro):
+        copies.arrived(("low", step), low.at[own_place(1 - core, step)])
+        back_product(
+            low, own_place(1 - core, step), out_matrix, attended, own_place(1 - core, step), False
+        )
+    dot_out()
+    tick()
+    wait_for(load_mixed)
+    for column in range(0, part_width, BLOCK):
+        attention_group(column)
+        tick()
+    send_halo()
+    wait_for(load_last)
+    dot_in(0)
+    tick()
+    for part in range(1, in_parts):
+        dot_in(part)
+        if part == in_parts - 1:
+            mixed_sums()
+            copies.sent(("halo",))
+            add_halo()
+            copies.sent(("partial", 0))
+            give_partial(("partial", 1), mixed_grad, in_matrix)
+        tick()
+    own_partial(("partial", 1), mixed_grad, in_matrix)
+    tick()
+    first_norm_back()
+    copies.start(("sum", "core"), vectors.at[0, pl.ds(0, 8)], vectors_came.at[0, pl.ds(0, 8)], at.other(core=1))
+    tick()
+    copies.arrived(("sum", "core"), vectors_came.at[0, pl.ds(0, 8)])
+    vectors[1, 0:8, :] = vectors[0, 0:8, :] + vectors_came[0, 0:8, :]
+    vectors[1, 8:16, :] = vectors[0, 8:16, :]
+    copies.start(("sum", "x"), vectors.at[1], vectors_came.at[1], at.other(x=1))
+    tick()
+    copies.arrived(("sum", "x"), vectors_came.at[1])
+    vectors[2] = vectors[1] + vectors_came[1]
+    copies.start(("sum", "y"), vectors.at[2], vectors_came.at[2], at.other(y=1))
+    tick()
+    copies.arrived(("sum", "y"), vectors_came.at[2])
+    vectors[3] = vectors[2] + vectors_came[2]
+    for step in range(1, chips):
+        copies.start(
+            ("sum", "z", step),
+            vectors.at[3],
+            vectors_came.at[2 + step],
+            at.other(chip=lax.rem(at.chip + step, chips)),
+        )
+    tick()
+    total = vectors[3]
+    for step in range(1, chips):
+        copies.arrived(("sum", "z", step), vectors_came.at[2 + step])
+        total = total + vectors_came[2 + step]
+    vectors_out[...] = total
+    for _ in range(OFFSETS[-1]):
+        tick()
     copies.finish()
 
 
-def reduce_grads(grads, sums, blocks_of, chips, chunk_width):
-    chunks = []
-    views = [grad.reshape(chips, 4, grad.shape[0] // (4 * chips), grad.shape[1]) for grad in grads]
-    for index in (3, 2, 1, 0):
-        for first in range(0, views[index].shape[3], chunk_width):
-            chunks.append((index, first, min(chunk_width, views[index].shape[3] - first)))
+def backward(chips, micro, blocks, blocks_of, members, starts, gains):
+    activated, down_low, hidden_low, normed_two, up, out_matrix, in_matrix, branch, mixed = members[:9]
+    rows, width = down_low.shape
+    all_rows, hidden_width, part_width = mixed.shape[0], hidden_low.shape[1], branch.shape[1]
+    own_rows = rows // 2
+    quarter = PART // 8
+    down_parts, up_parts, in_parts = width // PART, hidden_width // PART, 3 * part_width // PART
+    pooled = 2 * down_parts + up_parts + in_parts
+    any_space = pl.BlockSpec(memory_space=pl.ANY)
     vmem = pl.BlockSpec(memory_space=pltpu.VMEM)
-    out_shapes = []
-    for member, block in zip(views, blocks_of):
-        quarter, columns = member.shape[2:]
-        shape = (4, quarter, columns) if block is None else (2, quarter, 2 * columns)
-        out_shapes.append(jax.ShapeDtypeStruct(shape, LOW))
-    out_shapes.append(jax.ShapeDtypeStruct(sums.shape[1:], F32))
-    shapes = [(views[index].shape[2], width) for index, _, width in chunks]
-    scratch = [pltpu.VMEM((2, chips, q // 2, w), LOW) for q, w in shapes]
-    for _ in range(3):
-        scratch += [pltpu.VMEM((chips, q, w), LOW) for q, w in shapes]
-    scratch += [pltpu.VMEM((chips - 1, q, w), LOW) for q, w in shapes]
-    scratch += [pltpu.VMEM((4, q, w), LOW) for q, w in shapes]
-    scratch += [
-        pltpu.VMEM((2 * chips - 1,) + sums.shape[1:], F32),
-        pltpu.VMEM((2,) + sums.shape[1:], F32),
-        pltpu.VMEM((2,) + sums.shape[1:], F32),
+
+    def low(*shape):
+        return pltpu.VMEM(shape, LOW)
+
+    def full(*shape):
+        return pltpu.VMEM(shape, F32)
+
+    out_quarter = part_width // (4 * chips)
+    scratch = [
+        low(all_rows, hidden_width),
+        low(all_rows, hidden_width),
+        low(width, hidden_width),
+        low(part_width, width),
+        low(rows, width),
+        low(all_rows, width),
+        low(rows, part_width),
+        low(rows, part_width),
+        full(own_rows, width),
+        full(own_rows, width),
+        full(own_rows, width),
+        low(own_rows, width),
+        full(all_rows, 2 * BLOCK),
+        low(all_rows - rows, 2 * part_width),
+        full(4, VECTOR_ROWS, width),
+        full(chips + 2, VECTOR_ROWS, width),
+        low(2 * down_parts + up_parts, chips, 4, quarter, PART),
+        low(chips, 4, out_quarter, width),
+        low(pooled, 2, chips, quarter // 2, PART),
+        low(2, chips, out_quarter // 2, width),
+        low(pooled, chips, quarter, PART),
+        low(chips, out_quarter, width),
+        low(pooled, chips, quarter, PART),
+        low(chips, out_quarter, width),
+        low(pooled, chips - 1, quarter, PART),
+        low(chips - 1, out_quarter, width),
+        low(pooled, 4, quarter, PART),
+        low(4, out_quarter, width),
         pltpu.SemaphoreType.DMA((240,)),
         pltpu.SemaphoreType.DMA((240,)),
+        pltpu.SemaphoreType.DMA((16,)),
     ]
-    reduced = pl.pallas_call(
-        partial(reduce_kernel, chips, chunks, blocks_of),
+    out_shapes = [
+        jax.ShapeDtypeStruct((2, width // (4 * chips), 6 * part_width), LOW),
+        jax.ShapeDtypeStruct((4, out_quarter, width), LOW),
+        jax.ShapeDtypeStruct((2, width // (4 * chips), 2 * hidden_width), LOW),
+        jax.ShapeDtypeStruct((4, hidden_width // (4 * chips), width), LOW),
+        jax.ShapeDtypeStruct((VECTOR_ROWS, width), F32),
+        jax.ShapeDtypeStruct((own_rows, width), LOW),
+    ]
+    results = pl.pallas_call(
+        partial(backward_kernel, chips, micro, blocks, blocks_of),
         out_shape=tuple(out_shapes),
-        in_specs=[vmem] * 5,
-        out_specs=tuple([vmem] * 5),
+        in_specs=[any_space] * 12 + [vmem] * 2,
+        out_specs=tuple([vmem] * 6),
         scratch_shapes=scratch,
         compiler_params=pltpu.CompilerParams(
-            collective_id=1, has_side_effects=True, vmem_limit_bytes=60 << 20
+            collective_id=1, has_side_effects=True, vmem_limit_bytes=67_000_000
         ),
-    )(*views, sums)
-    flat = [member.reshape(-1, member.shape[2]).astype(F32) for member in reduced[:4]]
-    return flat, reduced[4]
+    )(*members, starts, gains)
+    flat = [member.reshape(-1, member.shape[2]).astype(F32) for member in results[:4]]
+    return flat, results[4], results[5]
 
 
 def shards(
@@ -880,75 +1319,102 @@
     hidden = dot(normed_two, up_part) + core_part(8)
     activated, gelu_back = jax.vjp(gelu_tanh, hidden)
     activated = activated.astype(LOW)
-    down_partial = rows_dot(activated, down_low).astype(LOW)
     result = middle + pair_sum(dot(activated, down_part)) + whole(7)
 
     upstream = cotangent.reshape(own_rows, width).astype(F32)
     (hidden_grad,) = gelu_back(back_dot(down_low, down_part))
     hidden_low = hidden_grad.astype(LOW)
-    up_partial = rows_dot(normed_two, hidden_low).astype(LOW)
-    upper_two = pair_sum(back_dot(hidden_low, up_part))
-    middle_grad = upstream + normalize_back(upper_two, whole(5), unit_two, inverse_two)
-    output_own = middle_grad.astype(LOW)
-    output_low = pair_rows(output_own)
-    output_partial = rows_dot(branch, output_low).astype(LOW)
-    attended = back_dot(output_low, output_part).astype(LOW)
-    mixed_grad = attention_back(mixed, starts, attended, blocks)
-    input_partial = rows_dot(all_normed, mixed_grad).astype(LOW)
-    back_halo = links.shift(mixed_grad[2 * own_rows :, half:], -1)
-    body = mixed_grad[: 2 * own_rows].reshape(micro, 2 * tok_rows, 3 * half)
-    tail_grad = body[:, 2 * tok_rows - BLOCK :, half:].astype(F32) + back_halo.reshape(
-        micro, BLOCK, width
-    ).astype(F32)
-    body = body.at[:, 2 * tok_rows - BLOCK :, half:].set(tail_grad.astype(LOW))
-    upper_one = pair_sum(back_dot(body.reshape(2 * own_rows, 3 * half), input_part))
-    input_grad = middle_grad + normalize_back(upper_one, whole(0), unit_one, inverse_one)
-
-    def by_shard(values):
-        return values.reshape(shard_count, -1)
-
-    def by_core_shard(values):
-        spread = values.reshape(chips, 1, -1)
-        mask = jnp.arange(2, dtype=jnp.int32)[None, :, None] == core
-        return jnp.where(mask, spread, 0.0).reshape(shard_count, -1)
-
-    def column_sum(values):
-        return jnp.sum(values.astype(F32), axis=0)
-
-    packed = jnp.concatenate(
-        [
-            by_shard(column_sum(upper_one * unit_one)),
-            by_shard(column_sum(upper_one)),
-            by_core_shard(column_sum(mixed_grad[:, :half])),
-            by_core_shard(column_sum(mixed_grad[:, width:])),
-            by_shard(column_sum(output_own)),
-            by_shard(column_sum(upper_two * unit_two)),
-            by_shard(column_sum(upper_two)),
-            by_shard(column_sum(upstream)),
-            by_core_shard(column_sum(hidden_low)),
-        ],
-        axis=1,
-    )
     if fast:
-        grads, sums = reduce_grads(
-            (input_partial, output_partial, up_partial, down_partial),
-            pad_lines(packed),
+        grads, sums, input_grad = backward(
+            chips,
+            micro,
+            blocks,
             (width // shard_count, None, up_part.shape[1] // chips, None),
-            chips,
-            512,
+            (
+                activated,
+                down_low,
+                hidden_low,
+                normed_two,
+                up_part,
+                output_part,
+                input_part,
+                branch,
+                mixed,
+                all_normed,
+                middle,
+                tokens.reshape(own_rows, width),
+            ),
+            starts,
+            jnp.concatenate([whole(0), whole(5)], axis=0),
         )
         input_weight_grad, output_grad, up_grad, down_grad = grads
-        sums = sums.reshape(-1)[:packed_length]
+        shared = pick(sums[:8].reshape(8, shard_count, -1), chip * 2 + core, 1)
+        sides = pick(sums[8].reshape(2, chips, -1), chip, 1)
+        vector_grads = [
+            shared[0],
+            shared[1],
+            sides[0],
+            sides[1],
+            shared[2],
+            shared[3],
+            shared[4],
+            shared[5],
+            pick(sums[9:].reshape(-1)[: up_part.shape[1]].reshape(chips, -1), chip),
+        ]
     else:
+        down_partial = rows_dot(activated, down_low).astype(LOW)
+        up_partial = rows_dot(normed_two, hidden_low).astype(LOW)
+        upper_two = pair_sum(back_dot(hidden_low, up_part))
+        middle_grad = upstream + normalize_back(upper_two, whole(5), unit_two, inverse_two)
+        output_own = middle_grad.astype(LOW)
+        output_low = pair_rows(output_own)
+        output_partial = rows_dot(branch, output_low).astype(LOW)
+        attended = back_dot(output_low, output_part).astype(LOW)
+        mixed_grad = attention_back(mixed, starts, attended, blocks)
+        input_partial = rows_dot(all_normed, mixed_grad).astype(LOW)
+        back_halo = links.shift(mixed_grad[2 * own_rows :, half:], -1)
+        body = mixed_grad[: 2 * own_rows].reshape(micro, 2 * tok_rows, 3 * half)
+        tail_grad = body[:, 2 * tok_rows - BLOCK :, half:].astype(F32) + back_halo.reshape(
+            micro, BLOCK, width
+        ).astype(F32)
+        body = body.at[:, 2 * tok_rows - BLOCK :, half:].set(tail_grad.astype(LOW))
+        upper_one = pair_sum(back_dot(body.reshape(2 * own_rows, 3 * half), input_part))
+        input_grad = middle_grad + normalize_back(upper_one, whole(0), unit_one, inverse_one)
+
+        def by_shard(values):
+            return values.reshape(shard_count, -1)
+
+        def by_core_shard(values):
+            spread = values.reshape(chips, 1, -1)
+            mask = jnp.arange(2, dtype=jnp.int32)[None, :, None] == core
+            return jnp.where(mask, spread, 0.0).reshape(shard_count, -1)
+
+        def column_sum(values):
+            return jnp.sum(values.astype(F32), axis=0)
+
+        packed = jnp.concatenate(
+            [
+                by_shard(column_sum(upper_one * unit_one)),
+                by_shard(column_sum(upper_one)),
+                by_core_shard(column_sum(mixed_grad[:, :half])),
+                by_core_shard(column_sum(mixed_grad[:, width:])),
+                by_shard(column_sum(output_own)),
+                by_shard(column_sum(upper_two * unit_two)),
+                by_shard(column_sum(upper_two)),
+                by_shard(column_sum(upstream)),
+                by_core_shard(column_sum(hidden_low)),
+            ],
+            axis=1,
+        )
         sums = links.reduce_vectors(packed)
         input_weight_grad = links.unhalves(links.reduce(input_partial), 3).astype(F32)
         output_grad = links.reduce(output_partial).astype(F32)
         up_grad = links.unhalves(links.reduce(up_partial), 1).astype(F32)
         down_grad = links.reduce(down_partial).astype(F32)
-    vector_grads, at = [], 0
-    for length in lengths:
-        vector_grads.append(sums[at : at + length])
-        at += length
+        vector_grads, at = [], 0
+        for length in lengths:
+            vector_grads.append(sums[at : at + length])
+            at += length
     return (
         result.astype(LOW).reshape(tokens.shape),
         input_grad.astype(LOW).reshape(tokens.shape),

time: 468 us -> 396 us (0.85)
  matrix products: 63.6 us -> 34.5 us
  Pallas kernels: 300 us -> 283 us
  waiting for transfers between devices: 29.5 us -> 17.6 us
  other arithmetic: 29.4 us -> 19.3 us
    dot_general x4 -> x0, matrix products: 22.1 us -> none  [rows_dot(): lax.dot_general(left, right, (((0,), (0,)), ((), ())), preferred_element_...]
    pallas_call x2 -> x1, Pallas kernels: 181 us -> 164 us  [backward(): pl.pallas_call(partial(backward_kernel, chips, micro, blocks, blocks_of),...]
    dot_general x4 -> x1, matrix products: 21.3 us -> 11.9 us  [back_dot(): lax.dot_general(left, right, (((1,), (1,)), ((), ())), preferred_element_...]
    reduce_sum x5 -> x0, other arithmetic: 7.71 us -> none  [column_sum(): return jnp.sum(values.astype(F32), axis=0)]
    ppermute x2 -> x1, waiting for transfers between devices: 19.1 us -> 11.5 us  [shift(): return lax.ppermute(values, AXES, pairs)]
    unnamed x95 -> x70, local copies, waits for them, and re-layouts: 26 us -> 19.1 us
    ppermute x8 -> x5, waiting for transfers between devices: 10.4 us -> 6.06 us  [swap(): return lax.ppermute(values, AXES, pairs)]
  transfers between devices with their start and end apart: 10 -> 6, of which waited for: 7 -> 3; matrix products, arithmetic and copies ran while one was open for 8% -> 4% of each run, Pallas kernels for 0% -> 0%
where the time goes in v3:
time: 396 us; the launch traced here: 389 us
  Pallas kernels  283 us (71%)
  matrix products  34.5 us (9%)
  local copies, waits for them, and re-layouts  29.8 us (8%)
  other arithmetic  19.3 us (5%)
  waiting for transfers between devices  17.6 us (4%)
    pallas_call x1, Pallas kernels, backward(): pl.pallas_call(partial(backward_kernel, chips, micro, blocks, blocks_of),...  164 us
    pallas_call x1, Pallas kernels, gather_weights(): pl.pallas_call(partial(gather_kernel, chips, splits), out_shape=tuple(sha...  110 us
    dot_general x4, matrix products, dot(): return jnp.dot(left, right, preferred_element_type=F32)  22.7 us
    unnamed x70, local copies, waits for them, and re-layouts  19.1 us
    dot_general x1, matrix products, back_dot(): lax.dot_general(left, right, (((1,), (1,)), ((), ())), preferred_element_...  11.9 us
    ppermute x1, waiting for transfers between devices, shift(): return lax.ppermute(values, AXES, pairs)  11.5 us
    pallas_call x1, Pallas kernels, attention(): pl.pallas_call(partial(attention_kernel, blocks, width), out_shape=jax.Sh...  8.99 us
  transfers between devices with their start and end apart: 6, of which 3 were waited for; matrix products, arithmetic and copies ran while one was open for 4% of the time, Pallas kernels for 0%

profile of v3, /device:TPU:0, one launch (start us, length us, event | category | flops | bytes accessed | tf_op | source)
XLA Modules:
  0.0 388.6 jit_solution(4135358445312343754)
XLA Ops:
  8.1 1.2 copy-done.7
  9.3 1.2 copy-done.8
  10.5 1.1 copy-done.9
  11.7 0.9 copy-done.10
  12.6 109.8 %shard_map.280 = (bf16[8,16,128]{2,1,0:T(8,128)(2,1)S(1)}, bf16[1024,1536]{1,0:T(8,128)(2,1)S(1)}, bf16[512,1024]{1,0:T(8,128)(2,1)S(1)}, bf16[1024,2048]{1,0:T(8,128)(2,1)S(1)}, bf16[2048,1024]{1,0:T(8,128)(2,1)}) custom-call(bf16[16,128]{1,0:T(8,128)(2,1)S(1)} %bitcast.155, bf16[128,3072]{1,0:T(8,128)(2,1)S(1)} %copy-done.9, ...), custom_call_target="tpu_custom_call" | custom-call | tf_op jit(solution)/shard_map/pallas_call | solution.py:573
  122.4 1.7 copy-done.5
  124.8 1.9 fusion.17
  127.5 2.1 collective-permute-done
  130.5 0.9 slice.118
  131.4 1.3 collective-permute-start.1
  133.2 11.5 %collective-permute-done.1 = bf16[256,1024]{1,0:T(8,128)(2,1)S(1)} collective-permute-done((bf16[256,1024]{1,0:T(8,128)(2,1)}, bf16[256,1024]{1,0:T(8,128)(2,1)S(1)}, u32[]{:S(2)}, u32[]{:S(2)}) %collective-permute-start.1) | collective-permute-done | bytes 524320 | tf_op jit(solution)/shard_map/ppermute | solution.py:221
  144.8 6.9 %fusion.7.mixed_ref.refs_8_ = bf16[1280,1536]{1,0:T(8,128)(2,1)S(1)} fusion(bf16[1024,1536]{1,0:T(8,128)(2,1)} %copy-done.5, f32[1536]{0:T(1024)S(1)} %fusion.23, bf16[256,1024]{1,0:T(8,128)(2,1)S(1)} %collective-permute-done.1, bf16[1024,1024]{1,0:T(8,128)(2,1)} %bitcast.158), kind=kOutput, calls=%fused_computation.11 | convolution fusion | flops 4035706880 | bytes 9705472 | tf_op jit(solution)/shard_map/dot_general | solution.py:20
  151.8 9.0 %shard_map.281.refs_7_ = bf16[1024,512]{1,0:T(8,128)(2,1)S(1)} custom-call(bf16[1280,1536]{1,0:T(8,128)(2,1)S(1)} %fusion.7.mixed_ref.refs_8_, s32[1024,1]{1,0:T(8,128)S(1)} %bitcast.152), custom_call_target="tpu_custom_call" | custom-call | flops 1073741824 | bytes 8388608 | tf_op jit(solution)/shard_map/pallas_call | solution.py:166
  160.8 1.3 fusion.41
  162.1 1.8 constant_dynamic-slice_fusion.8
  164.4 4.0 %collective-permute-done.2 = f32[512,1024]{1,0:T(8,128)} collective-permute-done((f32[512,1024]{1,0:T(8,128)}, f32[512,1024]{1,0:T(8,128)}, u32[]{:S(2)}, u32[]{:S(2)}) %collective-permute-start.2) | collective-permute-done | bytes 2097184 | tf_op jit(solution)/shard_map/ppermute | solution.py:211
  168.3 2.0 fusion.37
  172.0 1.7 select_bitcast_fusion.1
  174.1 1.4 copy-done.15
  175.5 2.0 pad_maximum_fusion.refs_9_
  178.6 2.7 copy-done.3
  181.4 4.5 %fusion.42 = f32[1024,2048]{1,0:T(8,128)S(1)} fusion(bf16[1024,1024]{1,0:T(8,128)(2,1)S(1)} %bitcast.162, bf16[1024,2048]{1,0:T(8,128)(2,1)S(1)} %copy-done.3), kind=kOutput, calls=%fused_computation.118 | convolution fusion | flops 4294967296 | bytes 14680064 | tf_op jit(solution)/shard_map/dot_general | solution.py:20
  185.9 11.9 %fusion.6 = (bf16[1024,2048]{1,0:T(8,128)(2,1)}, bf16[1024,2048]{1,0:T(8,128)(2,1)}) fusion(f32[1024,2048]{1,0:T(8,128)S(1)} %fusion.42, f32[2048]{0:T(1024)S(1)} %bitcast.180, bf16[1024,1024]{1,0:T(8,128)(2,1)S(1)} %bitcast.160, bf16[2048,1024]{1,0:T(8,128)(2,1)S(1)} %copy-done.27), kind=kOutput, calls=%fused_computation.9 | convolution fusion | flops 4343201792 | bytes 23076864 | tf_op jit(solution)/shard_map/dot_general | solution.py:28
  197.7 164.2 %shard_map.282 = (bf16[2,64,3072]{2,1,0:T(8,128)(2,1)}, bf16[4,32,1024]{2,1,0:T(8,128)(2,1)}, bf16[2,64,4096]{2,1,0:T(8,128)(2,1)}, bf16[4,128,1024]{2,1,0:T(8,1...) custom-call(bf16[1024,2048]{1,0:T(8,128)(2,1)} %get-tuple-element.42.refs_0_, bf16[1024,1024]{1,0:T(8,128)(2,1)} %bitcast.161, ...), custom_call_target="tpu_custom_call" | custom-call | tf_op jit(solution)/shard_map/pallas_call | solution.py:1192
  364.2 10.0 %fusion.43 = f32[1024,1024]{1,0:T(8,128)} fusion(bf16[1024,2048]{1,0:T(8,128)(2,1)} %get-tuple-element.42.refs_0_, bf16[2048,1024]{1,0:T(8,128)(2,1)} %get-tuple-element.30), kind=kOutput, calls=%fused_computation.119 | convolution fusion | flops 4294967296 | bytes 12582912 | tf_op jit(solution)/shard_map/dot_general | solution.py:20
  374.2 0.9 bitcast_convert_fusion.3
  375.6 2.6 constant_dynamic-slice_fusion.5
  380.1 1.6 bitcast_convert_fusion
  381.7 1.3 bitcast_convert_fusion.2
  383.1 1.6 bitcast_convert_fusion.1
  385.4 1.7 fusion.21
  387.1 1.0 copy.94
  (119 shorter events, 19.3 us)
Async XLA Ops:
  8.1 1.2 copy-start.7
  9.3 1.2 copy-start.8
  12.6 111.5 %copy-start.13 = (bf16[2,256,1024]{2,1,0:T(8,128)(2,1)S(1)}, bf16[2,256,1024]{2,1,0:T(8,128)(2,1)}, u32[]{:S(2)}) copy-start(bf16[2,256,1024]{2,1,0:T(8,128)(2,1)} %param.17) | copy-start | bytes 3145732
  122.4 1.7 copy-start.5
  124.1 2.7 copy-start.2
  124.1 36.7 %copy-start.6 = (bf16[512,1024]{1,0:T(8,128)(2,1)}, bf16[512,1024]{1,0:T(8,128)(2,1)S(1)}, u32[]{:S(2)}) copy-start(bf16[512,1024]{1,0:T(8,128)(2,1)S(1)} %get-tuple-element.28.refs_5_) | copy-start | bytes 3145732
  124.1 2.6 copy-start.25
  124.1 2.9 copy-start.26
  126.7 2.9 collective-permute-start
  130.5 2.4 copy-start.14
  131.4 13.3 %collective-permute-start.1 = (bf16[256,1024]{1,0:T(8,128)(2,1)}, bf16[256,1024]{1,0:T(8,128)(2,1)S(1)}, u32[]{:S(2)}, u32[]{:S(2)}) collective-permute-start(bf16[256,1024]{1,0:T(8,128)(2,1)} %bitcast.9), channel_id=1, source_target_pairs={{0,8},{1,9},{2,10},{3,11},{4,12},{5,13},{6,14},{7,15},{8,16},{9,17... | collective-permute-start | bytes 1572872 | tf_op jit(solution)/shard_map/ppermute | solution.py:221
  133.1 18.6 %copy-start.1 = (s32[1,1024]{0,1:T(8,128)}, s32[1,1024]{0,1:T(8,128)S(1)}, u32[]{:S(2)}) copy-start(s32[1,1024]{0,1:T(8,128)S(1)} %copy.81) | copy-start | bytes 12292
  144.8 7.0 %copy-start.22 = (bf16[256,1024]{1,0:T(8,128)(2,1)}, bf16[256,1024]{1,0:T(8,128)(2,1)S(1)}, u32[]{:S(2)}) copy-start(bf16[256,1024]{1,0:T(8,128)(2,1)S(1)} %collective-permute-done.1) | copy-start | bytes 1572868
  151.7 9.0 %copy-start = (bf16[1280,1536]{1,0:T(8,128)(2,1)}, bf16[1280,1536]{1,0:T(8,128)(2,1)S(1)}, u32[]{:S(2)}) copy-start(bf16[1280,1536]{1,0:T(8,128)(2,1)S(1)} %fusion.7.mixed_ref.refs_8_) | copy-start | bytes 11796484
  160.8 1.3 copy-start.4
  163.8 4.5 %collective-permute-start.2 = (f32[512,1024]{1,0:T(8,128)}, f32[512,1024]{1,0:T(8,128)}, u32[]{:S(2)}, u32[]{:S(2)}) collective-permute-start(f32[512,1024]{1,0:T(8,128)} %bitcast.20), channel_id=1, source_target_pairs={{0,4},{1,5},{2,6},{3,7},{4,0},{5,1},{6,2},{7,3},{8,12},{9,13},{10,... | collective-permute-start | bytes 6291464 | tf_op jit(solution)/shard_map/ppermute | solution.py:211
  163.8 8.1 %collective-permute-start.5 = (bf16[512,1024]{1,0:T(8,128)(2,1)}, bf16[512,1024]{1,0:T(8,128)(2,1)}, u32[]{:S(2)}, u32[]{:S(2)}) collective-permute-start(bf16[512,1024]{1,0:T(8,128)(2,1)} %bitcast.33), channel_id=1, source_target_pairs={{0,4},{1,5},{2,6},{3,7},{4,0},{5,1},{6,2},{7,3},{8,12},{9,13},{10,... | collective-permute-start | bytes 3145736 | tf_op jit(solution)/shard_map/ppermute | solution.py:211
  170.4 7.2 %copy-start.11 = (f32[512,1024]{1,0:T(8,128)}, f32[512,1024]{1,0:T(8,128)S(1)}, u32[]{:S(2)}) copy-start(f32[512,1024]{1,0:T(8,128)S(1)} %get-tuple-element.40.refs_10_) | copy-start | bytes 6291460
  171.1 6.4 %collective-permute-start.3 = (bf16[512,1024]{1,0:T(8,128)(2,1)S(1)}, bf16[512,1024]{1,0:T(8,128)(2,1)S(1)}, u32[]{:S(2)}, u32[]{:S(2)}) collective-permute-start(bf16[512,1024]{1,0:T(8,128)(2,1)S(1)} %add_convert_fusion), channel_id=1, source_target_pairs={{0,4},{1,5},{2,6},{3,7},{4,0},{5,1},{6,2},{7,3},{8,12},{9,13},{10,... | collective-permute-start | bytes 3145736 | tf_op jit(solution)/shard_map/ppermute | solution.py:211
  173.9 1.6 copy-start.15
  173.9 1.7 copy-start.23
  175.5 10.3 %copy-start.16 = (bf16[2,2,256,1024]{3,2,1,0:T(8,128)(2,1)}, bf16[2,2,256,1024]{3,2,1,0:T(8,128)(2,1)S(1)}, u32[]{:S(2)}) copy-start(bf16[2,2,256,1024]{3,2,1,0:T(8,128)(2,1)S(1)} %copy.63) | copy-start | bytes 6291460
  178.4 2.9 copy-start.3
  178.6 7.3 %copy-start.17 = (bf16[2,2,256,1024]{3,2,1,0:T(8,128)(2,1)}, bf16[2,2,256,1024]{3,2,1,0:T(8,128)(2,1)S(1)}, u32[]{:S(2)}) copy-start(bf16[2,2,256,1024]{3,2,1,0:T(8,128)(2,1)S(1)} %copy.60) | copy-start | bytes 6291460
  181.4 4.5 %copy-start.27 = (bf16[2048,1024]{1,0:T(8,128)(2,1)S(1)}, bf16[2048,1024]{1,0:T(8,128)(2,1)}, u32[]{:S(2)}) copy-start(bf16[2048,1024]{1,0:T(8,128)(2,1)} %get-tuple-element.30) | copy-start | bytes 12582916
  364.2 10.0 %copy-start.24 = (bf16[4,32,1024]{2,1,0:T(8,128)(2,1)S(1)}, bf16[4,32,1024]{2,1,0:T(8,128)(2,1)}, u32[]{:S(2)}) copy-start(bf16[4,32,1024]{2,1,0:T(8,128)(2,1)} %get-tuple-element.34) | copy-start | bytes 786436
  375.6 4.4 %copy-start.19 = (bf16[4,128,1024]{2,1,0:T(8,128)(2,1)S(1)}, bf16[4,128,1024]{2,1,0:T(8,128)(2,1)}, u32[]{:S(2)}) copy-start(bf16[4,128,1024]{2,1,0:T(8,128)(2,1)} %get-tuple-element.36) | copy-start | bytes 3145732
  378.3 3.4 copy-start.21
  378.3 6.4 %collective-permute-start.4 = (f32[512,1024]{1,0:T(8,128)S(1)}, f32[512,1024]{1,0:T(8,128)S(1)}, u32[]{:S(2)}, u32[]{:S(2)}) collective-permute-start(f32[512,1024]{1,0:T(8,128)S(1)} %bitcast.168), channel_id=1, source_target_pairs={{0,4},{1,5},{2,6},{3,7},{4,0},{5,1},{6,2},{7,3},{8,12},{9,13},{10,... | collective-permute-start | bytes 6291464 | tf_op jit(solution)/shard_map/ppermute | solution.py:211
  380.1 3.0 copy-start.18
  383.1 2.3 copy-start.12
  385.4 1.7 copy-start.20
  (2 other events, 2.1 us)

commit v4 on v3

--- a/solution.py
+++ b/solution.py
@@ -417,63 +417,117 @@
         return shards + [self.other(x=1), self.other(y=1)]
 
 
-def gather_kernel(
-    chips, splits, vec_in, in_in, out_in, up_in, down_in, *refs
-):
-    table, wholes, (send, recv, local) = refs[0], refs[1:5], refs[5:]
+def forward_kernel(chips, micro, blocks, splits, *refs):
+    vec_in, in_in, out_in, up_in, down_in, tokens_in, cotangent_in, starts = refs[:8]
+    (
+        in_out,
+        out_out,
+        up_out,
+        down_out,
+        mixed_out,
+        branch_out,
+        all_normed_out,
+        normed_two_out,
+        activated_out,
+        hidden_out,
+        middle_out,
+        low_out,
+        vectors,
+    ) = refs[8:21]
+    (
+        in_whole,
+        out_whole,
+        up_whole,
+        table,
+        mixed_bias,
+        up_bias,
+        tokens,
+        low,
+        all_normed,
+        mixed,
+        branch,
+        give,
+        came,
+        middle,
+        normed_two,
+        activated,
+        hidden,
+        send,
+        recv,
+        local,
+    ) = refs[21:]
     shards_in = (in_in, out_in, up_in, down_in)
+    wholes = (in_whole, out_whole, up_whole, down_out)
     at = Place(chips)
+    core = at.core
     copies = Copies(send, recv, at)
+    all_rows, width = all_normed.shape
+    rows = low.shape[0]
+    own_rows, micro_rows = rows // 2, rows // micro
+    own_micro = micro_rows // 2
+    part_width = branch.shape[1]
+    moved, staged = [], []
+
+    down_stage = activated.at[pl.ds(0, down_in.shape[0]), pl.ds(0, width)]
+
+    def keep(source, target):
+        copy = pltpu.make_async_copy(source, target, local.at[len(moved)])
+        copy.start()
+        moved.append(copy)
+        return copy
+
+    def own_place(row_side, step):
+        return pl.ds(pl.multiple_of(step * micro_rows + row_side * own_micro, own_micro), own_micro)
+
+    load_tokens = keep(tokens_in, tokens)
     at.greet(at.neighbours())
-    own_copies = []
-
-    def keep(source, target):
-        copy = pltpu.make_async_copy(source, target, local.at[len(own_copies)])
-        copy.start()
-        own_copies.append(copy)
-
-    keep(vec_in, table.at[at.shard])
+    partner = at.other(core=1)
+    load_table = keep(vec_in, table.at[at.shard])
     for step in range(1, 2 * chips):
         copies.start(
             ("vec", step), vec_in, table.at[at.shard], {"shard": at.shard_at(step), "rep": at.rep}
         )
     kept = []
-    for index, (source, whole, blocks) in enumerate(zip(shards_in, wholes, splits)):
-        rows = source.shape[0]
-        first = len(own_copies)
-        if blocks is None:
-            keep(source, whole.at[pl.ds(pl.multiple_of(at.chip * rows, rows), rows)])
+    for index, (source, whole, count) in enumerate(zip(shards_in, wholes, splits)):
+        shard_rows = source.shape[0]
+        first = len(moved)
+        if index == 3:
+            keep(source, down_stage)
+        elif count is None:
+            place = pl.ds(pl.multiple_of(at.chip * shard_rows, shard_rows), shard_rows)
+            keep(source, whole.at[place])
         else:
-            width = source.shape[1] // (2 * blocks)
-            place = pl.ds(pl.multiple_of(at.shard * rows, rows), rows)
-            for block in range(blocks):
-                columns = pl.ds(block * width, width)
-
-                def side(core):
-                    return pl.ds(pl.multiple_of((2 * block + core) * width, width), width)
+            piece_width = source.shape[1] // (2 * count)
+            place = pl.ds(pl.multiple_of(at.shard * shard_rows, shard_rows), shard_rows)
+            for block in range(count):
+                columns = pl.ds(block * piece_width, piece_width)
+
+                def side(which):
+                    start = pl.multiple_of((2 * block + which) * piece_width, piece_width)
+                    return pl.ds(start, piece_width)
 
                 copies.start(
                     ("pair", index, block),
-                    source.at[:, side(1 - at.core)],
+                    source.at[:, side(1 - core)],
                     whole.at[place, columns],
-                    at.other(core=1),
+                    partner,
                 )
-                keep(source.at[:, side(at.core)], whole.at[place, columns])
-        kept.append(own_copies[first:])
-
-    def piece(index, chip, part=None):
+                keep(source.at[:, side(core)], whole.at[place, columns])
+        kept.append(moved[first:])
+    load_low = []
+    for step in range(micro):
+        source = cotangent_in.at[pl.ds(step * own_micro, own_micro)]
+        load_low.append(keep(source, low.at[own_place(core, step)]))
+        copies.start(("low", step), source, low.at[own_place(core, step)], partner)
+
+    def piece(index, chip, bits=None, side=None):
         whole = wholes[index]
-        rows = whole.shape[0] // chips
-        quarter = rows // 4
-        if splits[index] is None and index == 1:
-            return whole.at[pl.ds(pl.multiple_of(chip * rows, rows), rows)]
-        start, size = chip * rows + at.rep * quarter, quarter
-        if part is not None:
-            bits, piece_half = part
-            start = chip * rows + at.flipped(bits) * quarter
-            if piece_half is not None:
-                size = quarter // 2
-                start = start + piece_half * size
+        chip_rows = whole.shape[0] // chips
+        size = chip_rows // 4
+        start = chip * chip_rows + (at.rep if bits is None else at.flipped(bits)) * size
+        if side is not None:
+            size = size // 2
+            start = start + side * size
         return whole.at[pl.ds(pl.multiple_of(start, size), size)]
 
     ways = (("up", 1), ("down", -1))
@@ -484,106 +538,322 @@
     def can_send(step):
         return at.chip < chips - 1 if step > 0 else at.chip > 0
 
-    def has(step, distance):
-        return at.chip >= distance if step > 0 else at.chip + distance < chips
+    def origins(index, distance):
+        for name, step in ways:
+            when = at.chip >= distance if step > 0 else at.chip + distance < chips
+            chip = jnp.clip(at.chip - step * distance, 0, chips - 1)
+            yield (name, index, distance), step, when, chip
 
     def open_z(index):
         for copy in kept[index]:
             copy.wait()
         if splits[index] is not None:
-            rows = shards_in[index].shape[0]
-            width = shards_in[index].shape[1] // (2 * splits[index])
-            place = pl.ds(pl.multiple_of((at.chip * 2 + 1 - at.core) * rows, rows), rows)
+            shard_rows = shards_in[index].shape[0]
+            piece_width = shards_in[index].shape[1] // (2 * splits[index])
+            place = (at.chip * 2 + 1 - core) * shard_rows
+            place = pl.ds(pl.multiple_of(place, shard_rows), shard_rows)
             for block in range(splits[index]):
-                copies.arrived(
-                    ("pair", index, block), wholes[index].at[place, pl.ds(block * width, width)]
+                columns = pl.ds(block * piece_width, piece_width)
+                copies.arrived(("pair", index, block), wholes[index].at[place, columns])
+        mine = target = piece(index, at.chip)
+        if index == 3:
+            place = pl.ds(pl.multiple_of(at.chip * down_in.shape[0], down_in.shape[0]), down_in.shape[0])
+            staged.append(keep(down_stage, down_out.at[place]))
+            quarter = down_in.shape[0] // 4
+            mine = down_in.at[pl.ds(pl.multiple_of(at.rep * quarter, quarter), quarter)]
+        for name, step in ways:
+            copies.start((name, index, 1), mine, target, neighbour(step), can_send(step))
+
+    def pass_on(index, distance):
+        for key, step, when, chip in origins(index, distance):
+            found = piece(index, chip)
+            copies.arrived(key, found, when)
+            if distance < chips - 1:
+                copies.start(
+                    (key[0], index, distance + 1),
+                    found,
+                    found,
+                    neighbour(step),
+                    when & can_send(step),
                 )
-        for name, step in ways:
-            mine = piece(index, at.chip)
-            copies.start((name, index, 1), mine, mine, neighbour(step), can_send(step))
-
-    def pass_on(index):
+            copies.start(("x",) + key, found, found, at.other(x=1), when)
+            copies.start(("y",) + key, found, found, at.other(y=1), when)
+
+    def across(index, distance):
+        for key, step, when, chip in origins(index, distance):
+            copies.arrived(("x",) + key, piece(index, chip, 1), when)
+            upper = piece(index, chip, 1, 0)
+            copies.start(("xy",) + key, upper, upper, at.other(y=1), when)
+            copies.arrived(("y",) + key, piece(index, chip, 2), when)
+            lower = piece(index, chip, 2, 1)
+            copies.start(("yx",) + key, lower, lower, at.other(x=1), when)
+
+    def close(index):
         for distance in range(1, chips):
-            for name, step in ways:
-                when = has(step, distance)
-                chip = jnp.clip(at.chip - step * distance, 0, chips - 1)
-                found = piece(index, chip)
-                copies.arrived((name, index, distance), found, when)
-                if distance < chips - 1:
-                    copies.start(
-                        (name, index, distance + 1),
-                        found,
-                        found,
-                        neighbour(step),
-                        when & can_send(step),
-                    )
-                if index != 1:
-                    copies.start(("x", name, index, distance), found, found, at.other(x=1), when)
-                    copies.start(("y", name, index, distance), found, found, at.other(y=1), when)
-
-    def across(index):
-        if index == 1:
-            return
-        for distance in range(1, chips):
-            for name, step in ways:
-                when = has(step, distance)
-                chip = jnp.clip(at.chip - step * distance, 0, chips - 1)
-                key = (name, index, distance)
-                copies.arrived(("x",) + key, piece(index, chip, (1, None)), when)
-                upper = piece(index, chip, (1, 0))
-                copies.start(("xy",) + key, upper, upper, at.other(y=1), when)
-                copies.arrived(("y",) + key, piece(index, chip, (2, None)), when)
-                lower = piece(index, chip, (2, 1))
-                copies.start(("yx",) + key, lower, lower, at.other(x=1), when)
-
-    def close(index):
-        if index == 1:
-            return
-        for distance in range(1, chips):
-            for name, step in ways:
-                when = has(step, distance)
-                chip = jnp.clip(at.chip - step * distance, 0, chips - 1)
-                key = (name, index, distance)
-                copies.arrived(("xy",) + key, piece(index, chip, (3, 0)), when)
-                copies.arrived(("yx",) + key, piece(index, chip, (3, 1)), when)
-
-    count = len(wholes)
+            for key, step, when, chip in origins(index, distance):
+                copies.arrived(("xy",) + key, piece(index, chip, 3, 0), when)
+                copies.arrived(("yx",) + key, piece(index, chip, 3, 1), when)
+
+    lines = 32
+
+    def own_lines(step):
+        place = pl.ds(pl.multiple_of(step * lines, lines), lines)
+        chip_row = step // (own_micro // lines) * micro_rows + core * own_micro
+        chip_row = chip_row + lax.rem(step, own_micro // lines) * lines
+        return place, pl.ds(pl.multiple_of(chip_row, lines), lines)
+
+    def spread_vectors():
+        load_table.wait()
+        for step in range(1, 2 * chips):
+            copies.arrived(("vec", step), table.at[at.shard_at(2 * chips - step)])
+        for shard in range(2 * chips):
+            vectors[:, shard * BLOCK : (shard + 1) * BLOCK] = table[shard].astype(F32)
+        mixed_bias[...] = jnp.zeros_like(mixed_bias)
+        each = up_bias.shape[1] // (chips * BLOCK)
+        for chip in range(chips):
+            member = table[2 * chip + core].astype(F32)
+            columns = pl.ds(chip * BLOCK, BLOCK)
+            mixed_bias[:, columns] = member[2:3, :]
+            mixed_bias[:, pl.ds(2 * part_width + chip * BLOCK, BLOCK)] = member[3:4, :]
+            for j in range(each):
+                up_bias[:, pl.ds((chip * each + j) * BLOCK, BLOCK)] = member[8 + j : 9 + j, :]
+
+    def halo_place(step):
+        return pl.ds(rows + step * BLOCK, BLOCK)
+
+    def first_norm():
+        def body(step):
+            place, chip_place = own_lines(step)
+            unit, _ = normalize(tokens[place, :].astype(F32))
+            all_normed[chip_place, :] = (unit * vectors[0:1, :] + vectors[1:2, :]).astype(LOW)
+
+        loop(own_rows // lines, body)
+        for step in range(micro):
+            mine = all_normed.at[own_place(core, step)]
+            copies.start(("normed", step), mine, mine, partner)
+            tail = all_normed.at[pl.ds((step + 1) * micro_rows - BLOCK, BLOCK)]
+            copies.start(
+                ("halo", step),
+                tail,
+                all_normed.at[halo_place(step)],
+                neighbour(1),
+                can_send(1) & (core == 1),
+            )
+
+        def clear():
+            all_normed[rows:, :] = jnp.zeros((all_rows - rows, width), LOW)
+
+        pl.when(at.chip == 0)(clear)
+
+    def halo_on():
+        for step in range(micro):
+            found = all_normed.at[halo_place(step)]
+            received = (at.chip > 0) & (core == 1)
+            copies.arrived(("halo", step), found, received)
+            copies.start(("halo on", step), found, found, partner, received)
+
+    def all_normed_ready():
+        for step in range(micro):
+            copies.arrived(("normed", step), all_normed.at[own_place(1 - core, step)])
+            copies.arrived(
+                ("halo on", step), all_normed.at[halo_place(step)], (at.chip > 0) & (core == 0)
+            )
+
+    tile = 256
+
+    def mix():
+        def body(step):
+            columns = pl.ds(pl.multiple_of(step * tile, tile), tile)
+            result = dot(all_normed[...], in_whole[:, columns]) + mixed_bias[:, columns]
+            mixed[:, columns] = result.astype(LOW)
+
+        loop(3 * part_width // tile, body)
+
+    left = lax.broadcasted_iota(jnp.int32, (BLOCK, BLOCK), 1) < HD
+
+    def attend(column):
+        def body(step):
+            row, previous = block_rows(step, blocks, rows)
+            allowed = allowed_keys(starts, row)
+            queries = mixed[pl.ds(row, BLOCK), column : column + BLOCK]
+            keys = window(mixed, row, previous, part_width + column)
+            values = window(mixed, row, previous, 2 * part_width + column)
+            parts = []
+            for side in (left, ~left):
+                soft = soft_weights(jnp.where(side, queries, 0), keys, allowed)
+                parts.append(dot(soft.astype(LOW), values))
+            branch[pl.ds(row, BLOCK), column : column + BLOCK] = jnp.where(
+                left, parts[0], parts[1]
+            ).astype(LOW)
+
+        loop(rows // BLOCK, body)
+
+    def project(side, target):
+        for step in range(micro):
+            place = pl.ds(step * own_micro, own_micro)
+            left_rows = branch[own_place(side, step), :]
+
+            def body(part):
+                columns = pl.ds(pl.multiple_of(part * tile, tile), tile)
+                target[place, columns] = dot(left_rows, out_whole[:, columns])
+
+            loop(width // tile, body)
+
+    def second_norm():
+        copies.arrived(("partial",), came)
+
+        def body(step):
+            place, chip_place = own_lines(step)
+            total = tokens[place, :].astype(F32) + (middle[place, :] + came[place, :])
+            total = total + vectors[4:5, :]
+            middle[place, :] = total
+            unit, _ = normalize(total)
+            normed_two[chip_place, :] = (unit * vectors[5:6, :] + vectors[6:7, :]).astype(LOW)
+
+        loop(own_rows // lines, body)
+        for step in range(micro):
+            mine = normed_two.at[own_place(core, step)]
+            copies.start(("normed two", step), mine, mine, partner)
+
+    def feed(first, last):
+        def body(step):
+            columns = pl.ds(pl.multiple_of((first + step) * tile, tile), tile)
+            result = dot(normed_two[...], up_whole[:, columns]) + up_bias[:, columns]
+            hidden[:, columns] = result
+            activated[:, columns] = gelu_tanh(result).astype(LOW)
+
+        loop(last - first, body)
+
     open_z(0)
-    for index in range(count):
-        if index + 1 < count:
-            open_z(index + 1)
-        pass_on(index)
-        across(index)
-    for index in range(count):
-        close(index)
-    own_copies[0].wait()
-    for step in range(1, 2 * chips):
-        copies.arrived(("vec", step), table.at[at.shard_at(2 * chips - step)])
+    load_tokens.wait()
+    spread_vectors()
+    first_norm()
+    open_z(1)
+    pass_on(0, 1)
+    pass_on(0, 2)
+    across(0, 1)
+    open_z(2)
+    pass_on(0, 3)
+    halo_on()
+    across(0, 2)
+    for distance in range(1, chips):
+        pass_on(1, distance)
+    across(0, 3)
+    for distance in range(1, chips):
+        across(1, distance)
+    all_normed_ready()
+    pass_on(2, 1)
+    open_z(3)
+    close(0)
+    pass_on(2, 2)
+    keep(in_whole, in_out)
+    keep(all_normed, all_normed_out)
+    mix()
+    keep(mixed, mixed_out)
+    across(2, 1)
+    attend(0)
+    attend(BLOCK)
+    pass_on(2, 3)
+    across(2, 2)
+    attend(2 * BLOCK)
+    pass_on(3, 1)
+    attend(3 * BLOCK)
+    keep(branch, branch_out)
+    across(2, 3)
+    close(1)
+    keep(out_whole, out_out)
+    project(1 - core, give)
+    copies.start(("partial",), give, came, partner)
+    project(core, middle)
+    pass_on(3, 2)
+    across(3, 1)
+    second_norm()
+    keep(middle, middle_out)
+    for copy in load_low:
+        copy.wait()
+    for step in range(micro):
+        copies.arrived(("low", step), low.at[own_place(1 - core, step)])
+    keep(low, low_out)
+    close(2)
+    keep(up_whole, up_out)
+    for step in range(micro):
+        copies.arrived(("normed two", step), normed_two.at[own_place(1 - core, step)])
+    keep(normed_two, normed_two_out)
+    tiles = activated.shape[1] // tile
+    staged[0].wait()
+    feed(0, tiles // 2)
+    pass_on(3, 3)
+    across(3, 2)
+    feed(tiles // 2, tiles)
+    keep(activated, activated_out)
+    keep(hidden, hidden_out)
+    across(3, 3)
+    close(3)
+    for copy in moved[sum(len(group) for group in kept) + 2 + len(load_low) :]:
+        if copy is not staged[0]:
+            copy.wait()
     copies.finish()
 
 
-def gather_weights(packed, matrices, splits, chips):
+def forward(chips, micro, blocks, splits, packed, matrices, tokens, cotangent, starts):
     any_space = pl.BlockSpec(memory_space=pl.ANY)
     vmem = pl.BlockSpec(memory_space=pltpu.VMEM)
-    shapes = [jax.ShapeDtypeStruct((2 * chips,) + packed.shape, LOW)]
-    for matrix, blocks in zip(matrices, splits):
-        rows, columns = matrix.shape
-        shape = (chips * rows, columns) if blocks is None else (2 * chips * rows, columns // 2)
-        shapes.append(jax.ShapeDtypeStruct(shape, LOW))
+    own_rows, width = tokens.shape
+    rows, half = 2 * own_rows, width // 2
+    all_rows = rows + micro * BLOCK
+    shapes = []
+    for matrix, count in zip(matrices, splits):
+        shard_rows, columns = matrix.shape
+        whole = (chips * shard_rows, columns)
+        shapes.append(whole if count is None else (2 * chips * shard_rows, columns // 2))
+    hidden_width = shapes[2][1]
+
+    def low(*shape):
+        return jax.ShapeDtypeStruct(shape, LOW)
+
+    def full(*shape):
+        return jax.ShapeDtypeStruct(shape, F32)
+
+    outs = [low(*shape) for shape in shapes] + [
+        low(all_rows, 3 * half),
+        low(rows, half),
+        low(all_rows, width),
+        low(rows, width),
+        low(rows, hidden_width),
+        full(rows, hidden_width),
+        full(own_rows, width),
+        low(rows, width),
+        full(packed.shape[0], width),
+    ]
+    scratch = [pltpu.VMEM(shape, LOW) for shape in shapes[:3]] + [
+        pltpu.VMEM((2 * chips,) + packed.shape, LOW),
+        pltpu.VMEM((1, 3 * half), F32),
+        pltpu.VMEM((1, hidden_width), F32),
+        pltpu.VMEM((own_rows, width), LOW),
+        pltpu.VMEM((rows, width), LOW),
+        pltpu.VMEM((all_rows, width), LOW),
+        pltpu.VMEM((all_rows, 3 * half), LOW),
+        pltpu.VMEM((rows, half), LOW),
+        pltpu.VMEM((own_rows, width), F32),
+        pltpu.VMEM((own_rows, width), F32),
+        pltpu.VMEM((own_rows, width), F32),
+        pltpu.VMEM((rows, width), LOW),
+        pltpu.VMEM((rows, hidden_width), LOW),
+        pltpu.VMEM((rows, hidden_width), F32),
+        pltpu.SemaphoreType.DMA((180,)),
+        pltpu.SemaphoreType.DMA((180,)),
+        pltpu.SemaphoreType.DMA((48,)),
+    ]
     return pl.pallas_call(
-        partial(gather_kernel, chips, splits),
-        out_shape=tuple(shapes),
-        in_specs=[any_space] * 5,
-        out_specs=tuple([vmem] * 5),
-        scratch_shapes=[
-            pltpu.SemaphoreType.DMA((160,)),
-            pltpu.SemaphoreType.DMA((160,)),
-            pltpu.SemaphoreType.DMA((32,)),
-        ],
+        partial(forward_kernel, chips, micro, blocks, splits),
+        out_shape=tuple(outs),
+        in_specs=[any_space] * 7 + [vmem],
+        out_specs=tuple([any_space] * 12 + [vmem]),
+        scratch_shapes=scratch,
         compiler_params=pltpu.CompilerParams(
-            collective_id=0, has_side_effects=True, vmem_limit_bytes=40 << 20
+            collective_id=0, has_side_effects=True, vmem_limit_bytes=63_000_000
         ),
-    )(packed, *matrices)
+    )(packed, *matrices, tokens, cotangent, starts)
 
 
 class Reduction:
@@ -712,6 +982,15 @@
 VECTOR_ROWS = 16
 
 
+def gelu_slope(values):
+    slope = float(2.0 / 3.141592653589793) ** 0.5
+    square = values * values
+    bend = jnp.tanh(slope * (values + 0.044715 * (values * square)))
+    return 0.5 * (1.0 + bend) + 0.5 * values * (1.0 - bend * bend) * slope * (
+        1.0 + 0.134145 * square
+    )
+
+
 def loop(count, body):
     def step(index, carry):
         body(index)
@@ -724,11 +1003,12 @@
     (
         activated_in,
         down_low_in,
-        hidden_low_in,
+        hidden_in,
         normed_two_in,
         up_in,
         out_in,
         in_in,
+        down_in,
         branch_in,
         mixed_in,
         all_normed_in,
@@ -736,9 +1016,9 @@
         tokens_in,
         starts,
         gains,
-    ) = refs[:14]
-    outs, vectors_out, input_grad_out = refs[14:18], refs[18], refs[19]
-    refs = refs[20:]
+    ) = refs[:15]
+    outs, vectors_out, input_grad_out, block_out = refs[15:19], refs[19], refs[20], refs[21]
+    refs = refs[22:]
     (
         wide,
         deep,
@@ -757,15 +1037,15 @@
         vectors,
         vectors_came,
     ) = refs[:16]
-    send, recv, local = refs[-3:]
-    pools = refs[16:-3]
+    credit, send, recv, local = refs[-4:]
+    pools = refs[16:-4]
     at = Place(chips)
     core = at.core
     width = down_low_in.shape[1]
     rows = down_low_in.shape[0]
     body_rows, all_rows = rows, mixed_in.shape[0]
     part_width = mixed_in.shape[1] // 3
-    hidden_width = hidden_low_in.shape[1]
+    hidden_width = hidden_in.shape[1]
     own_rows, micro_rows = rows // 2, rows // micro
     own_micro = micro_rows // 2
     copies = Copies(send, recv, at)
@@ -778,6 +1058,8 @@
         loads.append(copy)
         return copy
 
+    half_give = own_rows // 2
+    tile_sems = local.at[pl.ds(24, 2)]
     activated = wide.at[pl.ds(0, rows)]
     hidden_low = deep.at[pl.ds(0, rows)]
     mixed = wide.at[:, pl.ds(0, 3 * part_width)]
@@ -785,8 +1067,12 @@
     in_matrix = matrix.at[:, pl.ds(0, 3 * part_width)]
     normed_two = normed.at[pl.ds(0, rows)]
     load_first = [load(activated_in, activated), load(down_low_in, low)]
-    load_up = [load(hidden_low_in, hidden_low), load(normed_two_in, normed_two)]
-    load_two = [load(up_in, matrix), load(middle_in, middle)]
+    down_matrix_rows = matrix.shape[1]
+    load_down = [
+        load(down_in.at[pl.ds(side * width, width)], matrix.at[:, pl.ds(side * width, width)])
+        for side in range(down_matrix_rows // width)
+    ]
+    load_up = [load(normed_two_in, normed_two), load(middle_in, middle)]
     load_three = [load(out_in, out_matrix), load(branch_in, branch), load(tokens_in, tokens)]
     vectors[...] = jnp.zeros_like(vectors)
     at.greet(at.neighbours())
@@ -888,6 +1174,81 @@
 
         loop(right.shape[0] // tile, body)
 
+    def hidden_tile(row, side, slot):
+        return pltpu.make_async_copy(
+            hidden_in.at[
+                pl.ds(pl.multiple_of(row * half_give, half_give), half_give),
+                pl.ds(side * width, width),
+            ],
+            give.at[pl.ds(slot * half_give, half_give)],
+            tile_sems.at[slot],
+        )
+
+    def hidden_gradient():
+        count = rows // half_give
+        for side in range(2):
+            hidden_tile(0, side, side).start()
+
+        def body(row):
+            place = pl.ds(pl.multiple_of(row * half_give, half_give), half_give)
+            for side in range(2):
+                hidden_tile(row, side, side).wait()
+
+                def strip(part):
+                    start = side * width + part * 256
+                    columns = pl.ds(pl.multiple_of(start, 256), 256)
+                    from_place = pl.ds(pl.multiple_of(part * 256, 256), 256)
+                    values = give[side * half_give : (side + 1) * half_give, from_place]
+                    product = back_dot(low[place, :], matrix[from_place, side * width : (side + 1) * width])
+                    hidden_low[place, columns] = (product * gelu_slope(values)).astype(LOW)
+
+                loop(width // 256, strip)
+
+                def following():
+                    hidden_tile(row + 1, side, side).start()
+
+                pl.when(row + 1 < count)(following)
+
+        loop(count, body)
+
+    def down_product(left_rows, target_rows, finish):
+        def body(step):
+            columns = pl.ds(pl.multiple_of(step * 256, 256), 256)
+            result = None
+            for side in range(2):
+                start = pl.multiple_of(side * width + step * 256, 256)
+                term = dot(
+                    activated[left_rows, side * width : (side + 1) * width],
+                    matrix[:, pl.ds(start, 256)],
+                )
+                result = term if result is None else result + term
+            finish(target_rows, columns, result)
+
+        loop(width // 256, body)
+
+    def give_result():
+        def finish(place, columns, result):
+            give[place, columns] = result
+
+        for step in range(micro):
+            place = pl.ds(step * own_micro, own_micro)
+            down_product(own_place(1 - core, step), place, finish)
+        copies.start(("result",), give, came, at.other(core=1))
+
+    def own_result():
+        copies.arrived(("result",), came)
+
+        def finish(place, columns, result):
+            total = middle[place, columns] + (result + came[place, columns])
+            block_out[place, columns] = (total + gains[7:8, columns]).astype(LOW)
+
+        for step in range(micro):
+            place = pl.ds(step * own_micro, own_micro)
+            down_product(own_place(core, step), place, finish)
+        pl.semaphore_signal(
+            credit, 1, device_id=at.other(core=1), device_id_type=pl.DeviceIdType.MESH
+        )
+
     def give_partial(name, left, right):
         for step in range(micro):
             place = pl.ds(step * own_micro, own_micro)
@@ -906,7 +1267,7 @@
     lines = 32
 
     def second_norm_back():
-        gain = gains[1:2, :]
+        gain = gains[5:6, :]
 
         def body(step):
             place = pl.ds(pl.multiple_of(step * lines, lines), lines)
@@ -1053,19 +1414,27 @@
     for part in range(1, down_parts):
         dot_down(part)
     tick()
-    load_mixed = [load(mixed_in, mixed)]
+    wait_for(load_down)
+    hidden_gradient()
+    tick()
     wait_for(load_up)
-    wait_for(load_two)
+    give_result()
     for part in range(up_parts // 2):
         dot_up(part)
-    give_partial(("partial", 0), hidden_low, matrix)
+    own_result()
+    load_two = [load(up_in, matrix), load(mixed_in, mixed)]
     tick()
     for part in range(up_parts // 2, up_parts):
         dot_up(part)
+    hidden_sums()
+    wait_for(load_two)
+    copies.sent(("result",))
+    pl.semaphore_wait(credit, 1)
+    give_partial(("partial", 0), hidden_low, matrix)
+    load_normed = [load(all_normed_in, normed)]
     own_partial(("partial", 0), hidden_low, matrix)
-    load_last = [load(in_in, in_matrix), load(all_normed_in, normed)]
+    load_last = [load(in_in, in_matrix)] + load_normed
     second_norm_back()
-    hidden_sums()
     tick()
     wait_for(load_three)
     for step in range(micro):
@@ -1078,8 +1447,6 @@
             low, own_place(1 - core, step), out_matrix, attended, own_place(1 - core, step), False
         )
     dot_out()
-    tick()
-    wait_for(load_mixed)
     for column in range(0, part_width, BLOCK):
         attention_group(column)
         tick()
@@ -1131,7 +1498,7 @@
 
 
 def backward(chips, micro, blocks, blocks_of, members, starts, gains):
-    activated, down_low, hidden_low, normed_two, up, out_matrix, in_matrix, branch, mixed = members[:9]
+    down_low, hidden_low, branch, mixed = members[1], members[2], members[8], members[9]
     rows, width = down_low.shape
     all_rows, hidden_width, part_width = mixed.shape[0], hidden_low.shape[1], branch.shape[1]
     own_rows = rows // 2
@@ -1177,9 +1544,10 @@
         low(chips - 1, out_quarter, width),
         low(pooled, 4, quarter, PART),
         low(4, out_quarter, width),
+        pltpu.SemaphoreType.REGULAR,
         pltpu.SemaphoreType.DMA((240,)),
         pltpu.SemaphoreType.DMA((240,)),
-        pltpu.SemaphoreType.DMA((16,)),
+        pltpu.SemaphoreType.DMA((26,)),
     ]
     out_shapes = [
         jax.ShapeDtypeStruct((2, width // (4 * chips), 6 * part_width), LOW),
@@ -1188,22 +1556,23 @@
         jax.ShapeDtypeStruct((4, hidden_width // (4 * chips), width), LOW),
         jax.ShapeDtypeStruct((VECTOR_ROWS, width), F32),
         jax.ShapeDtypeStruct((own_rows, width), LOW),
+        jax.ShapeDtypeStruct((own_rows, width), LOW),
     ]
     results = pl.pallas_call(
         partial(backward_kernel, chips, micro, blocks, blocks_of),
         out_shape=tuple(out_shapes),
-        in_specs=[any_space] * 12 + [vmem] * 2,
-        out_specs=tuple([vmem] * 6),
+        in_specs=[any_space] * 13 + [vmem] * 2,
+        out_specs=tuple([vmem] * 7),
         scratch_shapes=scratch,
         compiler_params=pltpu.CompilerParams(
             collective_id=1, has_side_effects=True, vmem_limit_bytes=67_000_000
         ),
     )(*members, starts, gains)
     flat = [member.reshape(-1, member.shape[2]).astype(F32) for member in results[:4]]
-    return flat, results[4], results[5]
-
-
-def shards(
+    return flat, results[4], results[5], results[6]
+
+
+def shards_general(
     chips,
     reps,
     tokens,
@@ -1257,29 +1626,7 @@
         up_bias,
     )
     lengths = [member.shape[0] for member in vectors]
-    packed_length = sum(lengths)
-    fast = reps == 4
-    lines = -(-packed_length // (16 * BLOCK)) * 16
-
-    def pad_lines(values):
-        values = jnp.pad(values, ((0, 0), (0, lines * BLOCK - packed_length)))
-        return values.reshape(-1, lines, BLOCK)
-
-    packed_in = jnp.concatenate(vectors)
-    if fast:
-        table, input_part, output_part, up_part, down_part = gather_weights(
-            pad_lines(packed_in[None])[0],
-            (input_weight, output_weight, up_weight, down_weight),
-            (3 * chips, None, chips, None),
-            chips,
-        )
-        table = table.reshape(shard_count, -1)[:, :packed_length].astype(F32)
-    else:
-        table = links.gather_vectors(packed_in).astype(F32)
-        input_part = links.gather(links.halves(input_weight, 3))
-        output_part = links.gather(output_weight)
-        up_part = links.gather(links.halves(up_weight, 1))
-        down_part = links.gather(down_weight)
+    table = links.gather_vectors(jnp.concatenate(vectors)).astype(F32)
     wholes, at = [], 0
     for length in lengths:
         wholes.append(table[:, at : at + length])
@@ -1290,6 +1637,11 @@
 
     def core_part(index):
         return pick(wholes[index].reshape(chips, 2, -1), core, 1).reshape(1, -1)
+
+    input_part = links.gather(links.halves(input_weight, 3))
+    output_part = links.gather(output_weight)
+    up_part = links.gather(links.halves(up_weight, 1))
+    down_part = links.gather(down_weight)
 
     inputs = tokens.reshape(own_rows, width).astype(F32)
     unit_one, inverse_one = normalize(inputs)
@@ -1319,102 +1671,60 @@
     hidden = dot(normed_two, up_part) + core_part(8)
     activated, gelu_back = jax.vjp(gelu_tanh, hidden)
     activated = activated.astype(LOW)
+    down_grad = links.reduce(rows_dot(activated, down_low)).astype(F32)
     result = middle + pair_sum(dot(activated, down_part)) + whole(7)
 
     upstream = cotangent.reshape(own_rows, width).astype(F32)
     (hidden_grad,) = gelu_back(back_dot(down_low, down_part))
     hidden_low = hidden_grad.astype(LOW)
-    if fast:
-        grads, sums, input_grad = backward(
-            chips,
-            micro,
-            blocks,
-            (width // shard_count, None, up_part.shape[1] // chips, None),
-            (
-                activated,
-                down_low,
-                hidden_low,
-                normed_two,
-                up_part,
-                output_part,
-                input_part,
-                branch,
-                mixed,
-                all_normed,
-                middle,
-                tokens.reshape(own_rows, width),
-            ),
-            starts,
-            jnp.concatenate([whole(0), whole(5)], axis=0),
-        )
-        input_weight_grad, output_grad, up_grad, down_grad = grads
-        shared = pick(sums[:8].reshape(8, shard_count, -1), chip * 2 + core, 1)
-        sides = pick(sums[8].reshape(2, chips, -1), chip, 1)
-        vector_grads = [
-            shared[0],
-            shared[1],
-            sides[0],
-            sides[1],
-            shared[2],
-            shared[3],
-            shared[4],
-            shared[5],
-            pick(sums[9:].reshape(-1)[: up_part.shape[1]].reshape(chips, -1), chip),
-        ]
-    else:
-        down_partial = rows_dot(activated, down_low).astype(LOW)
-        up_partial = rows_dot(normed_two, hidden_low).astype(LOW)
-        upper_two = pair_sum(back_dot(hidden_low, up_part))
-        middle_grad = upstream + normalize_back(upper_two, whole(5), unit_two, inverse_two)
-        output_own = middle_grad.astype(LOW)
-        output_low = pair_rows(output_own)
-        output_partial = rows_dot(branch, output_low).astype(LOW)
-        attended = back_dot(output_low, output_part).astype(LOW)
-        mixed_grad = attention_back(mixed, starts, attended, blocks)
-        input_partial = rows_dot(all_normed, mixed_grad).astype(LOW)
-        back_halo = links.shift(mixed_grad[2 * own_rows :, half:], -1)
-        body = mixed_grad[: 2 * own_rows].reshape(micro, 2 * tok_rows, 3 * half)
-        tail_grad = body[:, 2 * tok_rows - BLOCK :, half:].astype(F32) + back_halo.reshape(
-            micro, BLOCK, width
-        ).astype(F32)
-        body = body.at[:, 2 * tok_rows - BLOCK :, half:].set(tail_grad.astype(LOW))
-        upper_one = pair_sum(back_dot(body.reshape(2 * own_rows, 3 * half), input_part))
-        input_grad = middle_grad + normalize_back(upper_one, whole(0), unit_one, inverse_one)
-
-        def by_shard(values):
-            return values.reshape(shard_count, -1)
-
-        def by_core_shard(values):
-            spread = values.reshape(chips, 1, -1)
-            mask = jnp.arange(2, dtype=jnp.int32)[None, :, None] == core
-            return jnp.where(mask, spread, 0.0).reshape(shard_count, -1)
-
-        def column_sum(values):
-            return jnp.sum(values.astype(F32), axis=0)
-
-        packed = jnp.concatenate(
-            [
-                by_shard(column_sum(upper_one * unit_one)),
-                by_shard(column_sum(upper_one)),
-                by_core_shard(column_sum(mixed_grad[:, :half])),
-                by_core_shard(column_sum(mixed_grad[:, width:])),
-                by_shard(column_sum(output_own)),
-                by_shard(column_sum(upper_two * unit_two)),
-                by_shard(column_sum(upper_two)),
-                by_shard(column_sum(upstream)),
-                by_core_shard(column_sum(hidden_low)),
-            ],
-            axis=1,
-        )
-        sums = links.reduce_vectors(packed)
-        input_weight_grad = links.unhalves(links.reduce(input_partial), 3).astype(F32)
-        output_grad = links.reduce(output_partial).astype(F32)
-        up_grad = links.unhalves(links.reduce(up_partial), 1).astype(F32)
-        down_grad = links.reduce(down_partial).astype(F32)
-        vector_grads, at = [], 0
-        for length in lengths:
-            vector_grads.append(sums[at : at + length])
-            at += length
+    up_grad = links.unhalves(links.reduce(rows_dot(normed_two, hidden_low)), 1).astype(F32)
+    upper_two = pair_sum(back_dot(hidden_low, up_part))
+    middle_grad = upstream + normalize_back(upper_two, whole(5), unit_two, inverse_two)
+    output_own = middle_grad.astype(LOW)
+    output_low = pair_rows(output_own)
+    output_grad = links.reduce(rows_dot(branch, output_low)).astype(F32)
+    attended = back_dot(output_low, output_part).astype(LOW)
+    mixed_grad = attention_back(mixed, starts, attended, blocks)
+    input_weight_grad = links.unhalves(links.reduce(rows_dot(all_normed, mixed_grad)), 3).astype(F32)
+    back_halo = links.shift(mixed_grad[2 * own_rows :, half:], -1)
+    body = mixed_grad[: 2 * own_rows].reshape(micro, 2 * tok_rows, 3 * half)
+    tail_grad = body[:, 2 * tok_rows - BLOCK :, half:].astype(F32) + back_halo.reshape(
+        micro, BLOCK, width
+    ).astype(F32)
+    body = body.at[:, 2 * tok_rows - BLOCK :, half:].set(tail_grad.astype(LOW))
+    upper_one = pair_sum(back_dot(body.reshape(2 * own_rows, 3 * half), input_part))
+    input_grad = middle_grad + normalize_back(upper_one, whole(0), unit_one, inverse_one)
+
+    def by_shard(values):
+        return values.reshape(shard_count, -1)
+
+    def by_core_shard(values):
+        spread = values.reshape(chips, 1, -1)
+        mask = jnp.arange(2, dtype=jnp.int32)[None, :, None] == core
+        return jnp.where(mask, spread, 0.0).reshape(shard_count, -1)
+
+    def column_sum(values):
+        return jnp.sum(values.astype(F32), axis=0)
+
+    packed = jnp.concatenate(
+        [
+            by_shard(column_sum(upper_one * unit_one)),
+            by_shard(column_sum(upper_one)),
+            by_core_shard(column_sum(mixed_grad[:, :half])),
+            by_core_shard(column_sum(mixed_grad[:, width:])),
+            by_shard(column_sum(output_own)),
+            by_shard(column_sum(upper_two * unit_two)),
+            by_shard(column_sum(upper_two)),
+            by_shard(column_sum(upstream)),
+            by_core_shard(column_sum(hidden_low)),
+        ],
+        axis=1,
+    )
+    sums = links.reduce_vectors(packed)
+    vector_grads, at = [], 0
+    for length in lengths:
+        vector_grads.append(sums[at : at + length])
+        at += length
     return (
         result.astype(LOW).reshape(tokens.shape),
         input_grad.astype(LOW).reshape(tokens.shape),
@@ -1431,6 +1741,135 @@
         vector_grads[8],
         down_grad,
         vector_grads[7],
+    )
+
+
+def shards(
+    chips,
+    reps,
+    tokens,
+    cotangent,
+    seq_lengths,
+    dealing,
+    *weights,
+):
+    if chips != 4 or reps != 4:
+        return shards_general(chips, reps, tokens, cotangent, seq_lengths, dealing, *weights)
+    (
+        attention_gain,
+        attention_shift,
+        input_weight,
+        query_bias,
+        value_bias,
+        output_weight,
+        output_bias,
+        feed_gain,
+        feed_shift,
+        up_weight,
+        up_bias,
+        down_weight,
+        down_bias,
+    ) = weights
+    shard = lax.axis_index("shard")
+    chip = shard // 2
+    micro, tok_rows, width = tokens.shape
+    shard_count, half = 2 * chips, width // 2
+    own_rows = micro * tok_rows
+    blocks = 2 * tok_rows // BLOCK
+    hidden_half = up_weight.shape[1] // 2
+
+    packed = jnp.concatenate(
+        [
+            attention_gain,
+            attention_shift,
+            query_bias,
+            value_bias,
+            output_bias,
+            feed_gain,
+            feed_shift,
+            down_bias,
+            up_bias,
+        ]
+    )
+    packed = jnp.pad(packed, (0, VECTOR_ROWS * BLOCK - packed.shape[0]))
+    first = chip * 2 * tok_rows
+    starts = jnp.stack(
+        [
+            sequence_starts(seq_lengths[m, 0], dealing[m, 0], first, 2 * tok_rows)
+            for m in range(micro)
+        ]
+    )
+    block_first = first + jnp.arange(2 * tok_rows, dtype=jnp.int32) // BLOCK * BLOCK - BLOCK
+    starts = (starts - block_first[None, :]).reshape(2 * own_rows, 1)
+    own_tokens = tokens.reshape(own_rows, width)
+    (
+        input_part,
+        output_part,
+        up_part,
+        down_part,
+        mixed,
+        branch,
+        all_normed,
+        normed_two,
+        activated,
+        hidden,
+        middle,
+        down_low,
+        vectors,
+    ) = forward(
+        chips,
+        micro,
+        blocks,
+        (3 * chips, None, chips, None),
+        packed.reshape(VECTOR_ROWS, BLOCK),
+        (input_weight, output_weight, up_weight, down_weight),
+        own_tokens,
+        cotangent.reshape(own_rows, width),
+        starts,
+    )
+    grads, sums, input_grad, block_out = backward(
+        chips,
+        micro,
+        blocks,
+        (width // shard_count, None, hidden_half // chips, None),
+        (
+            activated,
+            down_low,
+            hidden,
+            normed_two,
+            up_part,
+            output_part,
+            input_part,
+            down_part,
+            branch,
+            mixed,
+            all_normed,
+            middle,
+            own_tokens,
+        ),
+        starts,
+        vectors,
+    )
+    input_weight_grad, output_grad, up_grad, down_grad = grads
+    shared = pick(sums[:8].reshape(8, shard_count, -1), shard, 1)
+    sides = pick(sums[8].reshape(2, chips, -1), chip, 1)
+    up_sum = pick(sums[9:].reshape(-1)[:hidden_half].reshape(chips, -1), chip)
+    return (
+        block_out.reshape(tokens.shape),
+        input_grad.reshape(tokens.shape),
+        shared[0],
+        shared[1],
+        input_weight_grad,
+        sides[0],
+        sides[1],
+        output_grad,
+        shared[2],
+        shared[3],
+        shared[4],
+        up_grad,
+        up_sum,
+        down_grad,
+        shared[5],
     )
 
 

time: 396 us -> 318 us (0.80); the launches traced: 389 us -> 317 us
  matrix products: 34.5 us -> 0 us
  waiting for transfers between devices: 17.6 us -> 0 us
  local copies, waits for them, and re-layouts: 29.8 us -> 16.7 us
  other arithmetic: 19.3 us -> 7.99 us
  Pallas kernels: 283 us -> 292 us
    dot_general x5 -> x0, matrix products: 34.5 us -> none  [the longest x4 22.7 us: dot(): return jnp.dot(left, right, preferred_element_type=F32)]
    ppermute x6 -> x0, waiting for transfers between devices: 17.6 us -> none  [the longest x1 11.5 us: shift(): return lax.ppermute(values, AXES, pairs)]
    pallas_call x1, Pallas kernels: 164 us -> 180 us  [backward(): pl.pallas_call(partial(backward_kernel, chips, micro, blocks, blocks_of),...]
    unnamed x70 -> x20, local copies, waits for them, and re-layouts: 19.1 us -> 9.66 us
    pallas_call x2 -> x1, Pallas kernels: 119 us -> 112 us  [forward(): pl.pallas_call(partial(forward_kernel, chips, micro, blocks, splits), out...]
    dynamic_slice x5 -> x2, local copies, waits for them, and re-layouts: 5 us -> 0.59 us  [pick(): return lax.dynamic_index_in_dim(stacked, index, axis, keepdims=False)]
    convert_element_type x4 -> x0, other arithmetic: 4.07 us -> none  [the longest x1 1.91 us: shards(): normed = (unit_one * whole(0) + whole(1)).astype(LOW)]
  transfers between devices with their start and end apart: 6 -> 0, of which waited for: 3 -> 0; matrix products, arithmetic and copies ran while one was open for 4% -> 0% of each run, Pallas kernels for 0% -> 0%
where the time goes in v4:
time: 318 us; the launch traced here: 317 us
  Pallas kernels  292 us (92%)
  local copies, waits for them, and re-layouts  16.7 us (5%)
  other arithmetic  7.99 us (3%)
    pallas_call x1, Pallas kernels, backward(): pl.pallas_call(partial(backward_kernel, chips, micro, blocks, blocks_of),...  180 us
    pallas_call x1, Pallas kernels, forward(): pl.pallas_call(partial(forward_kernel, chips, micro, blocks, splits), out...  112 us
    unnamed x20, local copies, waits for them, and re-layouts  9.66 us
    convert_element_type x4, other arithmetic, backward(): member.reshape(-1, member.shape[2]).astype(F32)  7.46 us

profile of v4, /device:TPU:0, one launch (start us, length us, event | category | flops | bytes accessed | tf_op | source)
XLA Modules:
  0.0 317.2 jit_solution(1400186205534309498)
XLA Ops:
  0.7 0.7 slice_bitcast_fusion.7
  1.3 0.8 dynamic-update-slice
  2.2 0.8 dynamic-update-slice.1
  3.0 0.8 dynamic-update-slice.2
  3.9 0.8 dynamic-update-slice.3
  4.7 0.8 dynamic-update-slice.4
  5.5 0.8 dynamic-update-slice.5
  6.4 0.8 dynamic-update-slice.6
  7.2 0.8 dynamic-update-slice.7
  8.0 0.7 constant_dynamic-update-slice_fusion
  8.7 0.6 pad_bitcast_fusion.refs_0_
  9.3 0.7 fusion.9
  10.0 0.1 copy.41
  10.3 0.2 select_reduce_fusion.3
  10.5 0.1 select_reduce_fusion.2
  10.6 0.1 select_reduce_fusion.4
  10.8 0.1 select_reduce_fusion.1
  10.9 1.0 copy.53
  11.9 111.9 %shard_map.280 = (bf16[1024,1536]{1,0:T(8,128)(2,1)}, bf16[512,1024]{1,0:T(8,128)(2,1)}, bf16[1024,2048]{1,0:T(8,128)(2,1)}, bf16[2048,1024]{1,0:T(8,128)(2,1)},...) custom-call(bf16[16,128]{1,0:T(8,128)(2,1)} %pad_bitcast_fusion.refs, ...), custom_call_target="tpu_custom_call" | custom-call | tf_op jit(solution)/shard_map/pallas_call | solution.py:847
  123.8 179.9 %shard_map.281 = (bf16[2,64,3072]{2,1,0:T(8,128)(2,1)}, bf16[4,32,1024]{2,1,0:T(8,128)(2,1)}, bf16[2,64,4096]{2,1,0:T(8,128)(2,1)}, bf16[4,128,1024]{2,1,0:T(8,1...) custom-call(bf16[1024,2048]{1,0:T(8,128)(2,1)} %get-tuple-element.35.refs_0_, ...), custom_call_target="tpu_custom_call" | custom-call | tf_op jit(solution)/shard_map/pallas_call | solution.py:1561
  303.8 0.8 slice.63
  304.6 0.5 fusion.7
  305.1 0.8 slice.69
  305.9 0.8 slice_bitcast_fusion
  306.7 0.5 slice_bitcast_fusion.1
  307.2 0.6 constant_dynamic-slice_fusion.1
  307.8 1.8 bitcast_convert_fusion.3
  309.6 2.4 bitcast_convert_fusion.2
  312.0 1.6 bitcast_convert_fusion.1
  313.6 1.6 bitcast_convert_fusion
  315.3 1.0 copy.65
  316.2 1.0 copy.66
  (17 shorter events, 0.3 us)
Async XLA Ops:
  303.7 8.3 %copy-start.1 = (bf16[2,64,4096]{2,1,0:T(8,128)(2,1)S(1)}, bf16[2,64,4096]{2,1,0:T(8,128)(2,1)}, u32[]{:S(2)}) copy-start(bf16[2,64,4096]{2,1,0:T(8,128)(2,1)} %get-tuple-element.53) | copy-start | bytes 3145732
  312.0 1.6 copy-start
  313.6 1.6 copy-start.3
  313.6 2.6 copy-start.2

commit v5 on v4

--- a/solution.py
+++ b/solution.py
@@ -727,9 +727,9 @@
     open_z(0)
     load_tokens.wait()
     spread_vectors()
+    pass_on(0, 1)
+    open_z(1)
     first_norm()
-    open_z(1)
-    pass_on(0, 1)
     pass_on(0, 2)
     across(0, 1)
     open_z(2)
@@ -766,8 +766,9 @@
     copies.start(("partial",), give, came, partner)
     project(core, middle)
     pass_on(3, 2)
+    pass_on(3, 3)
+    second_norm()
     across(3, 1)
-    second_norm()
     keep(middle, middle_out)
     for copy in load_low:
         copy.wait()
@@ -782,7 +783,6 @@
     tiles = activated.shape[1] // tile
     staged[0].wait()
     feed(0, tiles // 2)
-    pass_on(3, 3)
     across(3, 2)
     feed(tiles // 2, tiles)
     keep(activated, activated_out)
@@ -964,8 +964,8 @@
 
     def tick(self, time):
         stages = (
+            self.add_across,
             self.send_across,
-            self.add_across,
             self.add_reps,
             self.add_chips,
             self.spread,
@@ -977,7 +977,7 @@
                 stage(time - offset)
 
 
-OFFSETS = (0, 1, 2, 3, 5, 6, 7)
+OFFSETS = (1, 0, 2, 3, 5, 6, 7)
 PART = 512
 VECTOR_ROWS = 16
 
@@ -1492,7 +1492,7 @@
         copies.arrived(("sum", "z", step), vectors_came.at[2 + step])
         total = total + vectors_came[2 + step]
     vectors_out[...] = total
-    for _ in range(OFFSETS[-1]):
+    for _ in range(7):
         tick()
     copies.finish()
 
@@ -1568,8 +1568,7 @@
             collective_id=1, has_side_effects=True, vmem_limit_bytes=67_000_000
         ),
     )(*members, starts, gains)
-    flat = [member.reshape(-1, member.shape[2]).astype(F32) for member in results[:4]]
-    return flat, results[4], results[5], results[6]
+    return results
 
 
 def shards_general(
@@ -1744,6 +1743,58 @@
     )
 
 
+def finish_kernel(chips, parts, *refs):
+    sums, vectors = refs[parts], refs[2 * parts + 1 :]
+    for source, target in zip(refs[:parts], refs[parts + 1 : 2 * parts + 1]):
+        target[...] = source[...].astype(target.dtype)
+
+    def own_vectors():
+        shard = lax.axis_index("shard")
+        chip = shard // 2
+        own = pl.ds(pl.multiple_of(shard * BLOCK, BLOCK), BLOCK)
+        for row in range(6):
+            vectors[row][...] = sums[row : row + 1, own]
+        half = sums.shape[1] // 2
+        for side in range(2):
+            place = pl.multiple_of(side * half + chip * BLOCK, BLOCK)
+            vectors[6 + side][...] = sums[8:9, pl.ds(place, BLOCK)]
+        length = vectors[8].shape[1]
+        each = sums.shape[1] // length
+        for at in range(chips):
+
+            def copy():
+                row, place = 9 + at // each, at % each * length
+                vectors[8][...] = sums[row : row + 1, place : place + length]
+
+            pl.when(chip == at)(copy)
+
+    pl.when(pl.program_id(0) == 0)(own_vectors)
+
+
+def finish(chips, grads, sums, rows):
+    steps = 4
+    members = list(grads) + list(rows)
+    specs = [
+        pl.BlockSpec((member.shape[0] // steps, member.shape[1]), lambda step: (step, 0))
+        for member in members
+    ]
+    lengths = [BLOCK] * 8 + [grads[2].shape[1] // (2 * chips)]
+    out_shapes = (
+        [jax.ShapeDtypeStruct(member.shape, F32) for member in grads]
+        + [jax.ShapeDtypeStruct(member.shape, LOW) for member in rows]
+        + [jax.ShapeDtypeStruct((1, length), F32) for length in lengths]
+    )
+    small = [pl.BlockSpec((1, length), lambda step: (0, 0)) for length in lengths]
+    return pl.pallas_call(
+        partial(finish_kernel, chips, len(members)),
+        grid=(steps,),
+        out_shape=tuple(out_shapes),
+        in_specs=specs + [pl.BlockSpec(sums.shape, lambda step: (0, 0))],
+        out_specs=tuple(specs + small),
+        compiler_params=pltpu.CompilerParams(vmem_limit_bytes=67_000_000),
+    )(*members, sums)
+
+
 def shards(
     chips,
     reps,
@@ -1778,20 +1829,20 @@
     blocks = 2 * tok_rows // BLOCK
     hidden_half = up_weight.shape[1] // 2
 
-    packed = jnp.concatenate(
-        [
-            attention_gain,
-            attention_shift,
-            query_bias,
-            value_bias,
-            output_bias,
-            feed_gain,
-            feed_shift,
-            down_bias,
-            up_bias,
-        ]
-    )
-    packed = jnp.pad(packed, (0, VECTOR_ROWS * BLOCK - packed.shape[0]))
+    members = [
+        attention_gain,
+        attention_shift,
+        query_bias,
+        value_bias,
+        output_bias,
+        feed_gain,
+        feed_shift,
+        down_bias,
+    ] + [up_bias[at : at + BLOCK] for at in range(0, up_bias.shape[0], BLOCK)]
+    line = lax.broadcasted_iota(jnp.int32, (VECTOR_ROWS, BLOCK), 0)
+    packed = jnp.zeros((VECTOR_ROWS, BLOCK), LOW)
+    for index, member in enumerate(members):
+        packed = jnp.where(line == index, member[None, :], packed)
     first = chip * 2 * tok_rows
     starts = jnp.stack(
         [
@@ -1821,13 +1872,13 @@
         micro,
         blocks,
         (3 * chips, None, chips, None),
-        packed.reshape(VECTOR_ROWS, BLOCK),
+        packed,
         (input_weight, output_weight, up_weight, down_weight),
         own_tokens,
         cotangent.reshape(own_rows, width),
         starts,
     )
-    grads, sums, input_grad, block_out = backward(
+    results = backward(
         chips,
         micro,
         blocks,
@@ -1850,26 +1901,25 @@
         starts,
         vectors,
     )
-    input_weight_grad, output_grad, up_grad, down_grad = grads
-    shared = pick(sums[:8].reshape(8, shard_count, -1), shard, 1)
-    sides = pick(sums[8].reshape(2, chips, -1), chip, 1)
-    up_sum = pick(sums[9:].reshape(-1)[:hidden_half].reshape(chips, -1), chip)
+    flat = [member.reshape(-1, member.shape[2]) for member in results[:4]]
+    finished = finish(chips, flat, results[4], results[5:])
+    vector_grads = [member.reshape(-1) for member in finished[6:]]
     return (
-        block_out.reshape(tokens.shape),
-        input_grad.reshape(tokens.shape),
-        shared[0],
-        shared[1],
-        input_weight_grad,
-        sides[0],
-        sides[1],
-        output_grad,
-        shared[2],
-        shared[3],
-        shared[4],
-        up_grad,
-        up_sum,
-        down_grad,
-        shared[5],
+        finished[5].reshape(tokens.shape),
+        finished[4].reshape(tokens.shape),
+        vector_grads[0],
+        vector_grads[1],
+        finished[0],
+        vector_grads[6],
+        vector_grads[7],
+        finished[1],
+        vector_grads[2],
+        vector_grads[3],
+        vector_grads[4],
+        finished[2],
+        vector_grads[8],
+        finished[3],
+        vector_grads[5],
     )
 
 

time: 318 us -> 304 us (0.956)
  local copies, waits for them, and re-layouts: 16.7 us -> 3.57 us
  other arithmetic: 7.99 us -> 2.03 us
  Pallas kernels: 292 us -> 297 us
    unnamed x20 -> x2, local copies, waits for them, and re-layouts: 9.66 us -> 1.03 us
    convert_element_type x4 -> x0, other arithmetic: 7.46 us -> none  [backward(): member.reshape(-1, member.shape[2]).astype(F32)]
    pallas_call x0 -> x1, Pallas kernels: none -> 6.29 us  [finish(): pl.pallas_call(partial(finish_kernel, chips, len(members)), grid=(steps,)...]
where the time goes in v5:
time: 304 us; the launch traced here: 303 us
  Pallas kernels  297 us (98%)
  local copies, waits for them, and re-layouts  3.57 us (1%)
    pallas_call x1, Pallas kernels, backward(): pl.pallas_call(partial(backward_kernel, chips, micro, blocks, blocks_of),...  180 us
    pallas_call x1, Pallas kernels, forward(): pl.pallas_call(partial(forward_kernel, chips, micro, blocks, splits), out...  110 us
    pallas_call x1, Pallas kernels, finish(): pl.pallas_call(partial(finish_kernel, chips, len(members)), grid=(steps,)...  6.29 us

profile of v5, /device:TPU:0, one launch (start us, length us, event | category | flops | bytes accessed | tf_op | source)
XLA Modules:
  0.0 303.0 jit_solution(13563658516871674800)
XLA Ops:
  0.7 0.7 slice_bitcast_fusion
  1.4 0.8 fusion.8
  2.2 1.5 select_select_fusion.refs_0_
  3.7 0.7 fusion.7
  4.4 0.1 copy.39
  4.5 0.1 mul.53
  4.6 0.1 copy.38
  4.6 0.1 mul.47
  4.7 0.2 select_reduce_fusion.3
  4.9 0.1 select_reduce_fusion.2
  5.0 0.1 select_reduce_fusion.4
  5.1 0.1 select_reduce_fusion.1
  5.3 1.0 copy.43
  6.3 110.2 %shard_map.280 = (bf16[1024,1536]{1,0:T(8,128)(2,1)}, bf16[512,1024]{1,0:T(8,128)(2,1)}, bf16[1024,2048]{1,0:T(8,128)(2,1)}, bf16[2048,1024]{1,0:T(8,128)(2,1)},...) custom-call(bf16[16,128]{1,0:T(8,128)(2,1)} %select_select_fusion.re, ...), custom_call_target="tpu_custom_call" | custom-call | tf_op jit(solution)/shard_map/pallas_call | solution.py:847
  116.5 180.0 %shard_map.281 = (bf16[2,64,3072]{2,1,0:T(8,128)(2,1)}, bf16[4,32,1024]{2,1,0:T(8,128)(2,1)}, bf16[2,64,4096]{2,1,0:T(8,128)(2,1)}, bf16[4,128,1024]{2,1,0:T(8,1...) custom-call(bf16[1024,2048]{1,0:T(8,128)(2,1)} %get-tuple-element.50.refs_0_, ...), custom_call_target="tpu_custom_call" | custom-call | tf_op jit(solution)/shard_map/pallas_call | solution.py:1561
  296.6 6.3 %shard_map.282 = (f32[128,3072]{1,0:T(8,128)}, f32[128,1024]{1,0:T(8,128)}, f32[128,4096]{1,0:T(8,128)}, f32[512,1024]{1,0:T(8,128)}, bf16[512,1024]{1,0:T(8,128...) custom-call(bf16[128,3072]{1,0:T(8,128)(2,1)} %bitcast.39, ...), custom_call_target="tpu_custom_call" | custom-call | tf_op jit(solution)/shard_map/pallas_call | solution.py:1788
  (9 shorter events, 0.1 us)

commit v6 on v5

--- a/solution.py
+++ b/solution.py
@@ -750,23 +750,23 @@
     keep(all_normed, all_normed_out)
     mix()
     keep(mixed, mixed_out)
+    pass_on(2, 3)
     across(2, 1)
     attend(0)
+    across(2, 2)
+    pass_on(3, 1)
     attend(BLOCK)
-    pass_on(2, 3)
-    across(2, 2)
+    pass_on(3, 2)
     attend(2 * BLOCK)
-    pass_on(3, 1)
+    across(2, 3)
     attend(3 * BLOCK)
+    pass_on(3, 3)
     keep(branch, branch_out)
-    across(2, 3)
     close(1)
     keep(out_whole, out_out)
     project(1 - core, give)
     copies.start(("partial",), give, came, partner)
     project(core, middle)
-    pass_on(3, 2)
-    pass_on(3, 3)
     second_norm()
     across(3, 1)
     keep(middle, middle_out)
@@ -1184,12 +1184,14 @@
             tile_sems.at[slot],
         )
 
-    def hidden_gradient():
+    def hidden_gradient(part):
         count = rows // half_give
         for side in range(2):
-            hidden_tile(0, side, side).start()
-
-        def body(row):
+            if part == 0:
+                hidden_tile(0, side, side).start()
+
+        def body(part_row):
+            row = part_row + part * (count // 2)
             place = pl.ds(pl.multiple_of(row * half_give, half_give), half_give)
             for side in range(2):
                 hidden_tile(row, side, side).wait()
@@ -1209,7 +1211,7 @@
 
                 pl.when(row + 1 < count)(following)
 
-        loop(count, body)
+        loop(count // 2, body)
 
     def down_product(left_rows, target_rows, finish):
         def body(step):
@@ -1413,9 +1415,10 @@
     tick()
     for part in range(1, down_parts):
         dot_down(part)
+    wait_for(load_down)
+    hidden_gradient(0)
     tick()
-    wait_for(load_down)
-    hidden_gradient()
+    hidden_gradient(1)
     tick()
     wait_for(load_up)
     give_result()
@@ -1426,16 +1429,16 @@
     tick()
     for part in range(up_parts // 2, up_parts):
         dot_up(part)
-    hidden_sums()
     wait_for(load_two)
     copies.sent(("result",))
     pl.semaphore_wait(credit, 1)
     give_partial(("partial", 0), hidden_low, matrix)
+    hidden_sums()
     load_normed = [load(all_normed_in, normed)]
     own_partial(("partial", 0), hidden_low, matrix)
     load_last = [load(in_in, in_matrix)] + load_normed
+    tick()
     second_norm_back()
-    tick()
     wait_for(load_three)
     for step in range(micro):
         back_product(
@@ -1447,17 +1450,20 @@
             low, own_place(1 - core, step), out_matrix, attended, own_place(1 - core, step), False
         )
     dot_out()
+    tick()
     for column in range(0, part_width, BLOCK):
         attention_group(column)
-        tick()
+        if column < part_width - BLOCK:
+            tick()
     send_halo()
     wait_for(load_last)
     dot_in(0)
     tick()
     for part in range(1, in_parts):
         dot_in(part)
+        if part == 1:
+            mixed_sums()
         if part == in_parts - 1:
-            mixed_sums()
             copies.sent(("halo",))
             add_halo()
             copies.sent(("partial", 0))

time: 304 us -> 296 us (0.974)
  Pallas kernels: 297 us -> 289 us
    pallas_call x1, Pallas kernels: 180 us -> 171 us  [backward(): pl.pallas_call(partial(backward_kernel, chips, micro, blocks, blocks_of),...]
where the time goes in v6:
time: 296 us; the launch traced here: 295 us
  Pallas kernels  289 us (98%)
  local copies, waits for them, and re-layouts  3.57 us (1%)
    pallas_call x1, Pallas kernels, backward(): pl.pallas_call(partial(backward_kernel, chips, micro, blocks, blocks_of),...  171 us
    pallas_call x1, Pallas kernels, forward(): pl.pallas_call(partial(forward_kernel, chips, micro, blocks, splits), out...  111 us
    pallas_call x1, Pallas kernels, finish(): pl.pallas_call(partial(finish_kernel, chips, len(members)), grid=(steps,)...  6.29 us

profile of v6, /device:TPU:0, one launch (start us, length us, event | category | flops | bytes accessed | tf_op | source)
XLA Modules:
  0.0 295.5 jit_solution(2135342170924318979)
XLA Ops:
  0.7 0.7 slice_bitcast_fusion
  1.4 0.8 fusion.8
  2.2 1.5 select_select_fusion.refs_0_
  3.7 0.7 fusion.7
  4.4 0.1 copy.39
  4.5 0.1 mul.53
  4.6 0.1 copy.38
  4.6 0.1 mul.47
  4.7 0.2 select_reduce_fusion.3
  4.9 0.1 select_reduce_fusion.2
  5.0 0.1 select_reduce_fusion.4
  5.1 0.1 select_reduce_fusion.1
  5.3 1.0 copy.43
  6.3 111.4 %shard_map.280 = (bf16[1024,1536]{1,0:T(8,128)(2,1)}, bf16[512,1024]{1,0:T(8,128)(2,1)}, bf16[1024,2048]{1,0:T(8,128)(2,1)}, bf16[2048,1024]{1,0:T(8,128)(2,1)},...) custom-call(bf16[16,128]{1,0:T(8,128)(2,1)} %select_select_fusion.re, ...), custom_call_target="tpu_custom_call" | custom-call | tf_op jit(solution)/shard_map/pallas_call | solution.py:847
  117.7 171.3 %shard_map.281 = (bf16[2,64,3072]{2,1,0:T(8,128)(2,1)}, bf16[4,32,1024]{2,1,0:T(8,128)(2,1)}, bf16[2,64,4096]{2,1,0:T(8,128)(2,1)}, bf16[4,128,1024]{2,1,0:T(8,1...) custom-call(bf16[1024,2048]{1,0:T(8,128)(2,1)} %get-tuple-element.50.refs_0_, ...), custom_call_target="tpu_custom_call" | custom-call | tf_op jit(solution)/shard_map/pallas_call | solution.py:1567
  289.0 6.3 %shard_map.282 = (f32[128,3072]{1,0:T(8,128)}, f32[128,1024]{1,0:T(8,128)}, f32[128,4096]{1,0:T(8,128)}, f32[512,1024]{1,0:T(8,128)}, bf16[512,1024]{1,0:T(8,128...) custom-call(bf16[128,3072]{1,0:T(8,128)(2,1)} %bitcast.39, ...), custom_call_target="tpu_custom_call" | custom-call | tf_op jit(solution)/shard_map/pallas_call | solution.py:1794
  (9 shorter events, 0.1 us)
